TPU v7x, 256 devices: a whole 4x4x8 slice. The times are simulated.
256 devices in a mesh: dp: 16 (over y_hi, z), mx: 8 (over x, core), my: 2 (over y_lo).
Axes of the slice: x: 4, y: 4 (y_hi: 2, y_lo: 2; y = y_hi * 2 + y_lo), z: 8, core: 2. Of those that a mesh axis runs over, the one named last changes fastest.
Arguments:
- inputs: bfloat16 [4096, 6144], P('dp', 'mx'), may hold values from -300 to 300
- ln_gain: float32 [6144], P('mx'), may hold values from 0.5 to 1.5
- w_qkv: bfloat16 [3, 6144, 4096], P(None, 'mx', 'my'), may hold values from -1 to 1
- qk_gain: float32 [2, 32, 128], P(None, ('my', 'mx')), may hold values from 0 to 8, as said below
- d_out: bfloat16 [4096, 4096], P('dp', ('my', 'mx')), may hold values from -110 to 110
Outputs:
- input_grad: bfloat16 [4096, 6144], P('dp', 'mx')
- w_grad: bfloat16 [3, 6144, 4096], P(None, ('mx', 'dp'), 'my')
- ln_gain_grad: float32 [6144], P('mx')
- qk_gain_grad: float32 [2, 32, 128], P(None, ('my', 'mx'))
Inputs may be any that keep to these rules, and one draw needn't show every extreme that they name: `qk_gain`: positive.
All inputs are finite; a program needn't handle non-finite values.
Results may differ from a plain program's by a relative error of at most 0.015.
The roundings to bfloat16 on the way count: a program that leaves them out, or rounds other values in their place, can miss the bound.
Values may be sent and summed in bfloat16 or wider, within the bound.
A program may use at most 128 MiB of HBM per device.

v0:
```python
import math

import jax
import jax.numpy as jnp
from jax import lax
from jax.sharding import PartitionSpec as P

PATCH = 256


epsilon = 1e-06


def head_norm(values):
    average = jnp.mean(values, axis=-1, keepdims=True)
    spread = jnp.mean(values * values, axis=-1, keepdims=True) - average * average
    inv_scale = lax.rsqrt(spread + epsilon)
    return ((values - average) * inv_scale, inv_scale)


def norm_back(d_normed, normed, inv_scale, gain_row):
    d_hat = d_normed * gain_row
    return inv_scale * (
        d_hat
        - jnp.mean(d_hat, axis=-1, keepdims=True)
        - normed * jnp.mean(d_hat * normed, axis=-1, keepdims=True)
    )


def body(inputs, ln_gain, w_qkv, qk_gain, d_out):
    token_rows = inputs.shape[0]
    width_local = inputs.shape[1]
    width = width_local * lax.axis_size("mx")
    widened = inputs.astype(jnp.float32)
    totals = lax.psum((jnp.sum(widened, axis=1), jnp.sum(widened * widened, axis=1)), "mx")
    average = totals[0][:, None] / width
    spread = totals[1][:, None] / width - average * average
    inv_scale = lax.rsqrt(spread + epsilon)
    normed = (widened - average) * inv_scale
    scaled = (normed * ln_gain[None, :]).astype(jnp.bfloat16)
    local_heads = qk_gain.shape[1]
    head_size = qk_gain.shape[2]
    group_heads = w_qkv.shape[2] // head_size
    weights = w_qkv.reshape(3, width_local, group_heads, head_size)
    projected = lax.psum_scatter(
        jnp.einsum("td,sdhe->hste", scaled, weights, preferred_element_type=jnp.float32),
        "mx",
        scatter_dimension=0,
        tiled=True,
    ).astype(jnp.bfloat16)
    images = token_rows // PATCH
    shaped = projected.reshape(local_heads, 3, images, PATCH, head_size)
    q_hat, q_inv = head_norm(shaped[:, 0].astype(jnp.float32))
    k_hat, k_inv = head_norm(shaped[:, 1].astype(jnp.float32))
    values = shaped[:, 2]
    q_gain = qk_gain[0][:, None, None, :]
    k_gain = qk_gain[1][:, None, None, :]
    q_normed = (q_hat * q_gain).astype(jnp.bfloat16)
    k_normed = (k_hat * k_gain).astype(jnp.bfloat16)
    factor = 1.0 / math.sqrt(head_size)
    scores = (
        jnp.einsum("hipe,hiqe->hipq", q_normed, k_normed, preferred_element_type=jnp.float32)
        * factor
    )
    row_max = jnp.max(scores, axis=-1, keepdims=True)
    exponent = jnp.exp(scores - row_max)
    probabilities = exponent / jnp.sum(exponent, axis=-1, keepdims=True)
    probs_low = probabilities.astype(jnp.bfloat16)
    grad_heads = (
        d_out.reshape(token_rows, local_heads, head_size)
        .transpose(1, 0, 2)
        .reshape(local_heads, images, PATCH, head_size)
    )
    d_values = jnp.einsum(
        "hipq,hipe->hiqe", probs_low, grad_heads, preferred_element_type=jnp.float32
    ).astype(jnp.bfloat16)
    d_probs = jnp.einsum("hipe,hiqe->hipq", grad_heads, values, preferred_element_type=jnp.float32)
    row_delta = jnp.sum(probabilities * d_probs, axis=-1, keepdims=True)
    d_scores = (probabilities * (d_probs - row_delta) * factor).astype(jnp.bfloat16)
    d_qn = jnp.einsum("hipq,hiqe->hipe", d_scores, k_normed, preferred_element_type=jnp.float32)
    d_kn = jnp.einsum("hipq,hipe->hiqe", d_scores, q_normed, preferred_element_type=jnp.float32)
    head_gain_part = jnp.stack(
        [jnp.sum(d_qn * q_hat, axis=(1, 2)), jnp.sum(d_kn * k_hat, axis=(1, 2))]
    )
    d_query = norm_back(d_qn, q_hat, q_inv, q_gain).astype(jnp.bfloat16)
    d_key = norm_back(d_kn, k_hat, k_inv, k_gain).astype(jnp.bfloat16)

    def head_rows(grads):
        return grads.reshape(local_heads, token_rows, head_size)

    block_rows = width_local // lax.axis_size("dp")
    stacked = jnp.stack([head_rows(d_query), head_rows(d_key), head_rows(d_values)], axis=1)
    gathered = lax.all_gather(stacked, "mx", axis=0, tiled=True)
    d_scaled = jnp.einsum("hste,sdhe->td", gathered, weights, preferred_element_type=jnp.float32)
    feature_part = scaled
    w_rows = lax.psum_scatter(
        jnp.einsum(
            "td,hste->dshe", feature_part, gathered, preferred_element_type=jnp.float32
        ).astype(jnp.bfloat16),
        "dp",
        scatter_dimension=0,
        tiled=True,
    ).astype(jnp.float32)
    w_grad = (
        w_rows.reshape(block_rows, 3, group_heads * head_size)
        .transpose(1, 0, 2)
        .astype(jnp.bfloat16)
    )
    gain_row = ln_gain[None, :]
    d_rows = lax.psum(d_scaled.astype(jnp.bfloat16), "my").astype(jnp.float32)
    d_hat = d_rows * gain_row
    stat_sums = lax.psum((jnp.sum(d_hat, axis=1), jnp.sum(d_hat * normed, axis=1)), "mx")
    sum_first = stat_sums[0]
    sum_second = stat_sums[1]
    result_rows = (
        inv_scale * (d_hat - sum_first[:, None] / width - normed * sum_second[:, None] / width)
    ).astype(jnp.bfloat16)
    feature_part = jnp.sum(d_rows * normed, axis=0)
    head_total, feature_total = lax.psum((head_gain_part, feature_part), "dp")
    return (result_rows, w_grad, feature_total, head_total)


def solution(mesh):
    in_specs = (
        P("dp", "mx"),
        P("mx"),
        P(None, "mx", "my"),
        P(None, ("my", "mx"), None),
        P("dp", ("my", "mx")),
    )
    out_specs = (P("dp", "mx"), P(None, ("mx", "dp"), "my"), P("mx"), P(None, ("my", "mx"), None))
    return jax.shard_map(body, mesh=mesh, in_specs=in_specs, out_specs=out_specs, check_vma=False)
```

profile of v0, /device:TPU:2, one launch (start us, length us, event | category | flops | bytes accessed | tf_op | source)
XLA Modules:
  0.0 439.1 jit_solution(7487721284132833700)
XLA Ops:
  7.2 0.0 copy-start
  7.2 0.0 all-gather.2.cloned.1.call-start
  7.2 0.7 slice_bitcast_fusion.3
  7.9 1.2 fusion.44
  9.1 11.7 %all-reduce.3 = (f32[256]{0:T(256)S(1)}, f32[256]{0:T(256)S(1)}) all-reduce(f32[256]{0:T(256)S(1)} %get-tuple-element.18, f32[256]{0:T(256)S(1)} %get-tuple-element.17), channel_id=1, replica_groups=mesh['dp'=16,'mx'=8,'my'=2] {'mx'}, use_global_device_ids=true, to_apply=%region_3.0 | all-reduce | flops 512 | bytes 4096 | tf_op jit(solution)/shard_map/psum | solution.py:35
  20.8 9.2 %fusion.10 = f32[16,3,256,128]{3,2,0,1:T(8,128)} fusion(bf16[256,768]{1,0:T(8,128)(2,1)} %param.5, f32[768]{0:T(1024)} %param.6, f32[256]{0:T(256)S(1)} %get-tuple-element.36, f32[256]{0:T(256)S(1)} %get-tuple-element.35, bf16[3,768,2048]{2,1,0:T(8,128)(2,1)} %param.7), kind=kOutput, calls=%fused_computation.11 | convolution fusion | flops 2416902144 | bytes 16126976 | tf_op jit(solution)/shard_map/td,sdhe->hste/dot_general | solution.py:46
  30.0 0.0 copy-start.5
  30.0 71.0 %all-reduce.8 = bf16[16,3,256,128]{3,2,0,1:T(8,128)(2,1)S(1)} all-reduce(f32[16,3,256,128]{3,2,0,1:T(8,128)} %fusion.10), channel_id=2, replica_groups=mesh['dp'=16,'mx'=8,'my'=2] {'mx'}, use_global_device_ids=true, to_apply=%region_4.0.clone | all-reduce | flops 1572864 | bytes 9437184
  101.0 0.0 copy-done.5
  101.0 0.6 dynamic-slice
  102.3 0.0 copy-start.2
  102.3 0.3 fusion.52
  102.6 0.4 copy-done.2
  103.1 0.0 copy-done
  103.1 0.2 convolution_bitcast_fusion
  103.3 0.0 copy-start.3
  103.3 1.6 fusion.109
  104.9 0.2 fusion.29
  105.2 1.3 fusion.30
  106.5 2.1 fusion.64
  108.6 0.0 copy-done.3
  108.6 0.6 fusion.84
  109.3 0.8 pad_maximum_fusion
  110.1 0.0 all-gather.2.cloned.1.call-update
  110.1 0.0 copy-start.1
  110.1 0.0 copy-start.4
  110.1 0.0 all-reduce.7.cloned.1.call-start
  110.2 33.7 %all-gather.2.cloned.1.call-done = bf16[16,3,256,128]{3,2,0,1:T(8,128)(2,1)} async-done(((bf16[2,3,256,128]{3,2,0,1:T(8,128)(2,1)}), bf16[16,3,256,128]{3,2,0,1:T(8,128)(2,1)}) %all-gather.2.cloned.1.call-update) | async-done | bytes 3145744 | tf_op jit(solution)/shard_map/all_gather | solution.py:93
  143.8 8.0 %fusion.19 = bf16[256,768]{1,0:T(8,128)(2,1)} fusion(bf16[16,3,256,128]{3,2,0,1:T(8,128)(2,1)} %all-gather.2.cloned.1.call-done, bf16[3,768,2048]{2,1,0:T(8,128)(2,1)} %param.7), kind=kOutput, calls=%fused_computation.14 | convolution fusion | flops 2416115712 | bytes 12976128 | tf_op jit(solution)/shard_map/hste,sdhe->td/dot_general | solution.py:94
  151.8 0.0 all-reduce.7.cloned.1.call-update
  151.8 0.2 reduce-scatter.5.cloned.1.call-start
  152.1 0.0 copy-done.1
  152.1 0.0 copy-done.4
  152.1 8.3 %convert_bitcast_fusion = bf16[768,3,16,128]{0,3,1,2:T(8,128)(2,1)} fusion(bf16[16,3,256,128]{3,2,0,1:T(8,128)(2,1)} %all-gather.2.cloned.1.call-done, bf16[256,768]{1,0:T(8,128)(2,1)S(1)} %copy-done.1, f32[768]{0:T(1024)S(1)} %copy-done.4, f32[256]{0:T(256)S(1)} %get-tuple-element.36, f32[256]{0:T(256)S(1)} %get-tuple-element.35), kind=kOutput, calls=%fused_computation.8 | convolution fusion | flops 2421620736 | bytes 12981248 | tf_op jit(solution)/shard_map/td,hste->dshe/dot_general | solution.py:97
  160.4 13.2 %copy.49 = bf16[768,3,16,128]{3,2,1,0:T(8,128)(2,1)} copy(bf16[768,3,16,128]{0,3,1,2:T(8,128)(2,1)} %convert_bitcast_fusion) | data formatting | bytes 18874368 | tf_op jit(solution)/shard_map/convert_element_type | solution.py:99
  173.6 0.0 reduce-scatter.5.cloned.1.call-update
  173.7 16.8 %all-reduce.7.cloned.1.call-done = bf16[256,768]{1,0:T(8,128)(2,1)} async-done(((bf16[256,768]{1,0:T(8,128)(2,1)}), bf16[256,768]{1,0:T(8,128)(2,1)}) %all-reduce.7.cloned.1.call-update) | async-done | bytes 393232 | tf_op jit(solution)/shard_map/psum | solution.py:110
  190.5 1.4 fusion.43
  191.9 11.5 %all-reduce.2 = (f32[256]{0:T(256)S(1)}, f32[256]{0:T(256)S(1)}) all-reduce(f32[256]{0:T(256)S(1)} %get-tuple-element.5, f32[256]{0:T(256)S(1)} %get-tuple-element.10), channel_id=1, replica_groups=mesh['dp'=16,'mx'=8,'my'=2] {'mx'}, use_global_device_ids=true, to_apply=%region_20.0 | all-reduce | flops 512 | bytes 4096 | tf_op jit(solution)/shard_map/psum | solution.py:112
  203.4 43.4 %all-reduce.1 = (f32[768]{0:T(1024)}, f32[2,2,128]{2,1,0:T(2,128)}) all-reduce(f32[768]{0:T(1024)S(1)} %get-tuple-element.4, f32[2,2,128]{2,1,0:T(2,128)S(1)} %pad_maximum_fusion.1), channel_id=1, replica_groups=mesh['dp'=16,'mx'=8,'my'=2] {'dp'}, use_global_device_ids=true, to_apply=%region_23.0 | all-reduce | flops 1280 | bytes 10240 | tf_op jit(solution)/shard_map/psum | solution.py:119
  246.8 2.1 fusion.41
  248.9 181.5 %reduce-scatter.5.cloned.1.call-done = bf16[48,3,16,128]{3,2,1,0:T(8,128)(2,1)} async-done(((bf16[768,3,16,128]{3,2,1,0:T(8,128)(2,1)}), bf16[48,3,16,128]{3,2,1,0:T(8,128)(2,1)}) %reduce-scatter.5.cloned.1.call-update) | async-done | bytes 589840 | tf_op jit(solution)/shard_map/reduce_scatter | solution.py:96
  430.4 1.2 copy.50
  431.6 1.1 convert_element_type.144
  (9 shorter events, 0.1 us)
Async XLA Ops:
  7.2 95.9 %copy-start = (bf16[256,256]{1,0:T(8,128)(2,1)S(1)}, bf16[256,256]{1,0:T(8,128)(2,1)}, u32[]{:S(2)}) copy-start(bf16[256,256]{1,0:T(8,128)(2,1)} %param.9) | copy-start | bytes 393220
  7.2 136.6 %all-gather.2.cloned.1.call-start = ((), (), s32[]{:S(2)}) async-start(), calls=%async_computation.1 | async-start | bytes 3538944 | tf_op jit(solution)/shard_map/all_gather | solution.py:93
  30.0 71.0 %copy-start.5 = (u32[256]{0:T(256)S(1)}, u32[256]{0:T(256)}, u32[]{:S(2)}) copy-start(u32[256]{0:T(256)} %constant.29) | copy-start | bytes 3076
  102.3 0.7 copy-start.2
  103.3 5.3 %copy-start.3 = (bf16[2,3,1,256,128]{4,3,0,2,1:T(8,128)(2,1)S(1)}, bf16[2,3,1,256,128]{4,3,0,2,1:T(8,128)(2,1)}, u32[]{:S(2)}) copy-start(bf16[2,3,1,256,128]{4,3,0,2,1:T(8,128)(2,1)} %copy-done.2) | copy-start | bytes 1179652
  110.1 42.0 %copy-start.1 = (bf16[256,768]{1,0:T(8,128)(2,1)S(1)}, bf16[256,768]{1,0:T(8,128)(2,1)}, u32[]{:S(2)}) copy-start(bf16[256,768]{1,0:T(8,128)(2,1)} %param.5) | copy-start | bytes 1179652
  110.1 42.0 %copy-start.4 = (f32[768]{0:T(1024)S(1)}, f32[768]{0:T(1024)}, u32[]{:S(2)}) copy-start(f32[768]{0:T(1024)} %param.6) | copy-start | bytes 9220
  110.1 80.4 %all-reduce.7.cloned.1.call-start = ((), (), s32[]{:S(2)}) async-start(), calls=%async_computation.2 | async-start | bytes 786432 | tf_op jit(solution)/shard_map/psum | solution.py:110
  151.8 278.5 %reduce-scatter.5.cloned.1.call-start = ((), (), s32[]{:S(2)}) async-start(), calls=%async_computation.3 | async-start | bytes 10027008 | tf_op jit(solution)/shard_map/reduce_scatter | solution.py:96
Sparse Core Ops, SparseCore 0:
  110.2 33.5 all-gather.1
  152.0 38.4 all-reduce.6
  194.7 235.6 reduce-scatter.4
where the time goes:
time: 440 us; the launch traced here: 439 us
  waiting for transfers between devices  232 us (53%)
  blocking collectives  138 us (31%)
  matrix products  31 us (7%)
  local copies, waits for them, and re-layouts  17.3 us (4%)
  between operations  14.6 us (3%)
  other arithmetic  6.45 us (1%)
    reduce_scatter x1, waiting for transfers between devices, body(): lax.psum_scatter(jnp.einsum('td,hste->dshe', feature_part, gathered, pref...  181 us
    unnamed x1, blocking collectives  71 us
    psum x1, blocking collectives, body(): head_total, feature_total = lax.psum((head_gain_part, feature_part), 'dp')  43.4 us
    all_gather x1, waiting for transfers between devices, body(): gathered = lax.all_gather(stacked, 'mx', axis=0, tiled=True)  33.7 us
    psum x1, waiting for transfers between devices, body(): d_rows = lax.psum(d_scaled.astype(jnp.bfloat16), 'my').astype(jnp.float32)  16.8 us
    convert_element_type x1, local copies, waits for them, and re-layouts, body(): w_rows = lax.psum_scatter(jnp.einsum('td,hste->dshe', feature_part, gathe...  13.2 us
    psum x1, blocking collectives, body(): lax.psum((jnp.sum(widened, axis=1), jnp.sum(widened * widened, axis=1)),...  11.7 us
    psum x1, blocking collectives, body(): lax.psum((jnp.sum(d_hat, axis=1), jnp.sum(d_hat * normed, axis=1)), 'mx')  11.5 us
  transfers between devices with their start and end apart: 3, of which 3 were waited for; matrix products, arithmetic and copies ran while one was open for 6% of the time, Pallas kernels for 0%

commit v1 on v0

--- a/solution.py
+++ b/solution.py
@@ -88,26 +88,25 @@
     def head_rows(grads):
         return grads.reshape(local_heads, token_rows, head_size)
 
-    block_rows = width_local // lax.axis_size("dp")
+    block_rows = width_local // (lax.axis_size("dph") * lax.axis_size("dpz"))
     stacked = jnp.stack([head_rows(d_query), head_rows(d_key), head_rows(d_values)], axis=1)
     gathered = lax.all_gather(stacked, "mx", axis=0, tiled=True)
     d_scaled = jnp.einsum("hste,sdhe->td", gathered, weights, preferred_element_type=jnp.float32)
     feature_part = scaled
-    w_rows = lax.psum_scatter(
-        jnp.einsum(
-            "td,hste->dshe", feature_part, gathered, preferred_element_type=jnp.float32
-        ).astype(jnp.bfloat16),
-        "dp",
-        scatter_dimension=0,
-        tiled=True,
-    ).astype(jnp.float32)
+    w_part = jnp.einsum(
+        "td,hste->dshe", feature_part, gathered, preferred_element_type=jnp.float32
+    ).astype(jnp.bfloat16)
+    w_half = lax.psum_scatter(w_part, "dph", scatter_dimension=0, tiled=True)
+    w_rows = lax.psum_scatter(w_half, "dpz", scatter_dimension=0, tiled=True).astype(jnp.float32)
     w_grad = (
         w_rows.reshape(block_rows, 3, group_heads * head_size)
         .transpose(1, 0, 2)
         .astype(jnp.bfloat16)
     )
     gain_row = ln_gain[None, :]
-    d_rows = lax.psum(d_scaled.astype(jnp.bfloat16), "my").astype(jnp.float32)
+    d_low = d_scaled.astype(jnp.bfloat16)
+    d_other = lax.ppermute(d_low, "my", [(0, 1), (1, 0)])
+    d_rows = d_low.astype(jnp.float32) + d_other.astype(jnp.float32)
     d_hat = d_rows * gain_row
     stat_sums = lax.psum((jnp.sum(d_hat, axis=1), jnp.sum(d_hat * normed, axis=1)), "mx")
     sum_first = stat_sums[0]
@@ -116,17 +115,20 @@
         inv_scale * (d_hat - sum_first[:, None] / width - normed * sum_second[:, None] / width)
     ).astype(jnp.bfloat16)
     feature_part = jnp.sum(d_rows * normed, axis=0)
-    head_total, feature_total = lax.psum((head_gain_part, feature_part), "dp")
+    head_total, feature_total = lax.psum((head_gain_part, feature_part), ("dph", "dpz"))
     return (result_rows, w_grad, feature_total, head_total)
 
 
 def solution(mesh):
+    dp = ("dph", "dpz")
+    devices = mesh.devices.reshape(2, mesh.shape["dp"] // 2, mesh.shape["mx"], mesh.shape["my"])
+    split_mesh = jax.sharding.Mesh(devices, ("dph", "dpz", "mx", "my"))
     in_specs = (
-        P("dp", "mx"),
+        P(dp, "mx"),
         P("mx"),
         P(None, "mx", "my"),
         P(None, ("my", "mx"), None),
-        P("dp", ("my", "mx")),
+        P(dp, ("my", "mx")),
     )
-    out_specs = (P("dp", "mx"), P(None, ("mx", "dp"), "my"), P("mx"), P(None, ("my", "mx"), None))
-    return jax.shard_map(body, mesh=mesh, in_specs=in_specs, out_specs=out_specs, check_vma=False)
+    out_specs = (P(dp, "mx"), P(None, ("mx",) + dp, "my"), P("mx"), P(None, ("my", "mx"), None))
+    return jax.shard_map(body, mesh=split_mesh, in_specs=in_specs, out_specs=out_specs, check_vma=False)

time: 440 us -> 419 us (0.952)
  waiting for transfers between devices: 232 us -> 162 us
  local copies, waits for them, and re-layouts: 17.3 us -> 68.7 us
    reduce_scatter x1, waiting for transfers between devices: 181 us -> 0.01 us  [body(): lax.psum_scatter(w_half, 'dpz', scatter_dimension=0, tiled=True)]
    unnamed x3 -> x4, waiting for transfers between devices: 0.05 us -> 118 us
    unnamed x13 -> x14, local copies, waits for them, and re-layouts: 1.07 us -> 58.5 us
    psum x1 -> x0, waiting for transfers between devices: 16.8 us -> none  [body(): d_rows = lax.psum(d_scaled.astype(jnp.bfloat16), 'my').astype(jnp.float32)]
    convert_element_type x1 -> x0, local copies, waits for them, and re-layouts: 13.2 us -> none  [body(): w_rows = lax.psum_scatter(jnp.einsum('td,hste->dshe', feature_part, gathe...]
    ppermute x0 -> x1, waiting for transfers between devices: none -> 10.1 us  [body(): d_other = lax.ppermute(d_low, 'my', [(0, 1), (1, 0)])]
    reduce_scatter x1 -> x2, local copies, waits for them, and re-layouts: 1.17 us -> 7.34 us  [the longest x1 6.17 us: body(): w_half = lax.psum_scatter(w_part, 'dph', scatter_dimension=0, tiled=True)]
  transfers between devices with their start and end apart: 3 -> 4, of which waited for: 3 -> 3; matrix products, arithmetic and copies ran while one was open for 6% -> 2% of each run, Pallas kernels for 0% -> 0%
where the time goes in v1:
time: 419 us; the launch traced here: 415 us
  waiting for transfers between devices  162 us (39%)
  blocking collectives  137 us (33%)
  local copies, waits for them, and re-layouts  68.7 us (16%)
  matrix products  27.5 us (7%)
  between operations  14.5 us (3%)
  other arithmetic  4.47 us (1%)
    unnamed x4, waiting for transfers between devices  118 us
    unnamed x1, blocking collectives  71.4 us
    unnamed x14, local copies, waits for them, and re-layouts  58.5 us
    psum x1, blocking collectives, body(): lax.psum((head_gain_part, feature_part), ('dph', 'dpz'))  42.7 us
    all_gather x1, waiting for transfers between devices, body(): gathered = lax.all_gather(stacked, 'mx', axis=0, tiled=True)  33.7 us
    psum x1, blocking collectives, body(): lax.psum((jnp.sum(widened, axis=1), jnp.sum(widened * widened, axis=1)),...  11.7 us
    psum x1, blocking collectives, body(): lax.psum((jnp.sum(d_hat, axis=1), jnp.sum(d_hat * normed, axis=1)), 'mx')  11.1 us
    ppermute x1, waiting for transfers between devices, body(): d_other = lax.ppermute(d_low, 'my', [(0, 1), (1, 0)])  10.1 us
  transfers between devices with their start and end apart: 4, of which 3 were waited for; matrix products, arithmetic and copies ran while one was open for 2% of the time, Pallas kernels for 0%

profile of v1, /device:TPU:2, one launch (start us, length us, event | category | flops | bytes accessed | tf_op | source)
XLA Modules:
  0.0 414.9 jit_solution(134687811085896903)
XLA Ops:
  7.2 0.0 copy-start
  7.2 0.0 all-gather.2.cloned.1.call-start
  7.2 0.7 slice_bitcast_fusion.3
  7.9 1.2 fusion.36
  9.1 11.7 %all-reduce.3 = (f32[256]{0:T(256)S(1)}, f32[256]{0:T(256)S(1)}) all-reduce(f32[256]{0:T(256)S(1)} %get-tuple-element.18, f32[256]{0:T(256)S(1)} %get-tuple-element.17), channel_id=1, replica_groups=mesh['dph'=2,'dpz'=8,'mx'=8,'my'=2] {'mx'}, use_global_device_ids=true, to_apply=%region_3.0 | all-reduce | flops 512 | bytes 4096 | tf_op jit(solution)/shard_map/psum | solution.py:35
  20.8 9.2 %fusion.10 = f32[16,3,256,128]{3,2,0,1:T(8,128)} fusion(bf16[256,768]{1,0:T(8,128)(2,1)} %param.5, f32[768]{0:T(1024)} %param.6, f32[256]{0:T(256)S(1)} %get-tuple-element.36, f32[256]{0:T(256)S(1)} %get-tuple-element.35, bf16[3,768,2048]{2,1,0:T(8,128)(2,1)} %param.7), kind=kOutput, calls=%fused_computation.11 | convolution fusion | flops 2416902144 | bytes 16126976 | tf_op jit(solution)/shard_map/td,sdhe->hste/dot_general | solution.py:46
  30.0 0.0 copy-start.4
  30.0 71.4 %all-reduce.5 = bf16[16,3,256,128]{3,2,0,1:T(8,128)(2,1)} all-reduce(f32[16,3,256,128]{3,2,0,1:T(8,128)} %fusion.10), channel_id=2, replica_groups=mesh['dph'=2,'dpz'=8,'mx'=8,'my'=2] {'mx'}, use_global_device_ids=true, to_apply=%region_4.0.clone | all-reduce | flops 1572864 | bytes 9437184
  101.4 0.0 copy-start.2
  101.4 0.0 copy-start.3
  101.4 0.0 copy-done.4
  101.4 0.6 dynamic-slice
  102.6 1.0 fusion.51
  103.6 0.3 fusion.53
  103.9 0.0 copy-done
  103.9 0.2 convolution_bitcast_fusion
  104.2 0.8 fusion.110
  105.0 0.2 fusion.29
  105.2 0.4 fusion.30
  105.7 1.1 fusion.65
  106.8 0.6 fusion.85
  107.4 0.8 pad_maximum_fusion
  108.2 0.0 all-gather.2.cloned.1.call-update
  108.2 0.0 reduce-scatter.10.cloned.1.call-start
  108.3 33.7 %all-gather.2.cloned.1.call-done = bf16[16,3,256,128]{3,2,0,1:T(8,128)(2,1)} async-done(((bf16[2,3,256,128]{3,2,0,1:T(8,128)(2,1)}), bf16[16,3,256,128]{3,2,0,1:T(8,128)(2,1)}) %all-gather.2.cloned.1.call-update) | async-done | bytes 3145744 | tf_op jit(solution)/shard_map/all_gather | solution.py:93
  141.9 0.0 copy-done.2
  141.9 0.0 copy-done.3
  141.9 8.2 %convert_bitcast_fusion = bf16[768,3,16,128]{0,3,1,2:T(8,128)(2,1)} fusion(bf16[16,3,256,128]{3,2,0,1:T(8,128)(2,1)} %all-gather.2.cloned.1.call-done, bf16[256,768]{1,0:T(8,128)(2,1)S(1)} %copy-done.2, f32[768]{0:T(1024)S(1)} %copy-done.3, f32[256]{0:T(256)S(1)} %get-tuple-element.36, f32[256]{0:T(256)S(1)} %get-tuple-element.35), kind=kOutput, calls=%fused_computation.8 | convolution fusion | flops 2421620736 | bytes 12981248 | tf_op jit(solution)/shard_map/td,hste->dshe/dot_general | solution.py:96
  150.2 20.7 %copy.65 = bf16[768,3,16,128]{3,1,2,0:T(4,128)(2,1)} copy(bf16[768,3,16,128]{0,3,1,2:T(8,128)(2,1)} %convert_bitcast_fusion) | data formatting | bytes 18874368
  170.8 23.6 %reshape.271 = bf16[768,6144]{1,0:T(8,128)(2,1)} reshape(bf16[768,16,3,128]{3,2,1,0:T(4,128)(2,1)} %bitcast.159) | data formatting | bytes 18874368
  194.4 0.0 reduce-scatter.10.cloned.1.call-update
  194.5 0.2 reduce-scatter.8.cloned.1.call-start
  194.7 118.1 %reduce-scatter.10.cloned.1.call-done = bf16[384,6144]{1,0:T(8,128)(2,1)} async-done(((bf16[768,6144]{1,0:T(8,128)(2,1)}), bf16[384,6144]{1,0:T(8,128)(2,1)}) %reduce-scatter.10.cloned.1.call-update) | async-done | bytes 4718608
  312.8 13.6 %reshape.272 = bf16[384,16,3,128]{3,2,1,0:T(4,128)(2,1)} reshape(bf16[384,6144]{1,0:T(8,128)(2,1)} %reduce-scatter.10.cloned.1.call-done) | data formatting | bytes 9437184
  326.5 6.2 %copy.49 = bf16[384,3,16,128]{3,2,1,0:T(8,128)(2,1)} copy(bf16[384,3,16,128]{3,1,2,0:T(4,128)(2,1)} %bitcast.160) | data formatting | bytes 9437184 | tf_op jit(solution)/shard_map/reduce_scatter | solution.py:99
  332.6 0.0 reduce-scatter.8.cloned.1.call-update
  332.7 0.0 copy-start.1
  332.7 7.3 %fusion.19 = bf16[256,768]{1,0:T(8,128)(2,1)S(1)} fusion(bf16[16,3,256,128]{3,2,0,1:T(8,128)(2,1)} %all-gather.2.cloned.1.call-done, bf16[3,768,2048]{2,1,0:T(8,128)(2,1)} %param.7), kind=kOutput, calls=%fused_computation.14 | convolution fusion | flops 2416115712 | bytes 12976128 | tf_op jit(solution)/shard_map/hste,sdhe->td/dot_general | solution.py:94
  340.0 0.7 collective-permute-start
  340.7 10.1 %collective-permute-done = bf16[256,768]{1,0:T(8,128)(2,1)S(1)} collective-permute-done((bf16[256,768]{1,0:T(8,128)(2,1)S(1)}, bf16[256,768]{1,0:T(8,128)(2,1)S(1)}, u32[]{:S(2)}, u32[]{:S(2)}) %collective-permute-start) | collective-permute-done | bytes 393248 | tf_op jit(solution)/shard_map/ppermute | solution.py:108
  350.8 0.4 fusion.48
  351.2 11.1 %all-reduce.2 = (f32[256]{0:T(256)S(1)}, f32[256]{0:T(256)S(1)}) all-reduce(f32[256]{0:T(256)S(1)} %get-tuple-element.5, f32[256]{0:T(256)S(1)} %get-tuple-element.6), channel_id=1, replica_groups=mesh['dph'=2,'dpz'=8,'mx'=8,'my'=2] {'mx'}, use_global_device_ids=true, to_apply=%region_19.0 | all-reduce | flops 512 | bytes 4096 | tf_op jit(solution)/shard_map/psum | solution.py:111
  362.3 42.7 %all-reduce.1 = (f32[768]{0:T(1024)}, f32[2,2,128]{2,1,0:T(2,128)}) all-reduce(f32[768]{0:T(1024)S(1)} %get-tuple-element.4, f32[2,2,128]{2,1,0:T(2,128)S(1)} %pad_maximum_fusion.1), channel_id=1, replica_groups=mesh['dph'=2,'dpz'=8,'mx'=8,'my'=2] {'dph','dpz'}, use_global_device_ids=true, to_apply=%region_23.0 | all-reduce | flops 1280 | bytes 10240 | tf_op jit(solution)/shard_map/psum | solution.py:118
  405.0 1.1 fusion.47
  406.1 0.0 reduce-scatter.8.cloned.1.call-done
  406.1 1.2 copy.50
  407.3 1.1 convert_element_type.148
  408.4 0.0 copy-done.1
  (8 shorter events, 0.0 us)
Async XLA Ops:
  7.2 96.8 %copy-start = (bf16[256,256]{1,0:T(8,128)(2,1)S(1)}, bf16[256,256]{1,0:T(8,128)(2,1)}, u32[]{:S(2)}) copy-start(bf16[256,256]{1,0:T(8,128)(2,1)} %param.9) | copy-start | bytes 393220
  7.2 134.7 %all-gather.2.cloned.1.call-start = ((), (), s32[]{:S(2)}) async-start(), calls=%async_computation.2 | async-start | bytes 3538944 | tf_op jit(solution)/shard_map/all_gather | solution.py:93
  30.0 71.4 %copy-start.4 = (u32[256]{0:T(256)S(1)}, u32[256]{0:T(256)}, u32[]{:S(2)}) copy-start(u32[256]{0:T(256)} %constant.29) | copy-start | bytes 3076
  101.4 40.6 %copy-start.2 = (bf16[256,768]{1,0:T(8,128)(2,1)S(1)}, bf16[256,768]{1,0:T(8,128)(2,1)}, u32[]{:S(2)}) copy-start(bf16[256,768]{1,0:T(8,128)(2,1)} %param.5) | copy-start | bytes 1179652
  101.4 40.6 %copy-start.3 = (f32[768]{0:T(1024)S(1)}, f32[768]{0:T(1024)}, u32[]{:S(2)}) copy-start(f32[768]{0:T(1024)} %param.6) | copy-start | bytes 9220
  108.2 204.6 %reduce-scatter.10.cloned.1.call-start = ((), (), s32[]{:S(2)}) async-start(), calls=%async_computation.4 | async-start | bytes 14155776
  194.5 211.7 %reduce-scatter.8.cloned.1.call-start = ((), (), s32[]{:S(2)}) async-start(), calls=%async_computation.3 | async-start | bytes 5308416 | tf_op jit(solution)/shard_map/reduce_scatter | solution.py:100
  332.7 75.7 %copy-start.1 = (bf16[256,256]{1,0:T(8,128)(2,1)S(1)}, bf16[256,256]{1,0:T(8,128)(2,1)}, u32[]{:S(2)}) copy-start(bf16[256,256]{1,0:T(8,128)(2,1)} %param.9) | copy-start | bytes 393220
  340.0 10.8 %collective-permute-start = (bf16[256,768]{1,0:T(8,128)(2,1)S(1)}, bf16[256,768]{1,0:T(8,128)(2,1)S(1)}, u32[]{:S(2)}, u32[]{:S(2)}) collective-permute-start(bf16[256,768]{1,0:T(8,128)(2,1)S(1)} %fusion.19), channel_id=1, source_target_pairs={{0,1},{1,0},{2,3},{3,2},{4,5},{5,4},{6,7},{7,6},{8,9},{9,8},{10,11... | collective-permute-start | bytes 1179656 | tf_op jit(solution)/shard_map/ppermute | solution.py:108
Sparse Core Ops, SparseCore 0:
  108.3 33.5 all-gather.1
  194.6 118.1 reduce-scatter.9
  332.8 60.7 reduce-scatter.7

commit v2 on v1

--- a/solution.py
+++ b/solution.py
@@ -6,6 +6,7 @@
 from jax.sharding import PartitionSpec as P
 
 PATCH = 256
+MX = ("mxx", "mxc")
 
 
 epsilon = 1e-06
@@ -30,9 +31,9 @@
 def body(inputs, ln_gain, w_qkv, qk_gain, d_out):
     token_rows = inputs.shape[0]
     width_local = inputs.shape[1]
-    width = width_local * lax.axis_size("mx")
+    width = width_local * lax.axis_size(MX)
     widened = inputs.astype(jnp.float32)
-    totals = lax.psum((jnp.sum(widened, axis=1), jnp.sum(widened * widened, axis=1)), "mx")
+    totals = lax.psum((jnp.sum(widened, axis=1), jnp.sum(widened * widened, axis=1)), MX)
     average = totals[0][:, None] / width
     spread = totals[1][:, None] / width - average * average
     inv_scale = lax.rsqrt(spread + epsilon)
@@ -42,12 +43,13 @@
     head_size = qk_gain.shape[2]
     group_heads = w_qkv.shape[2] // head_size
     weights = w_qkv.reshape(3, width_local, group_heads, head_size)
-    projected = lax.psum_scatter(
-        jnp.einsum("td,sdhe->hste", scaled, weights, preferred_element_type=jnp.float32),
-        "mx",
-        scatter_dimension=0,
-        tiled=True,
-    ).astype(jnp.bfloat16)
+    n_x = lax.axis_size("mxx")
+    n_c = lax.axis_size("mxc")
+    ordered = w_qkv.reshape(3, width_local, n_x, n_c, local_heads, head_size)
+    partial = jnp.einsum("td,sdabje->bajste", scaled, ordered, preferred_element_type=jnp.float32)
+    partial = partial.reshape(group_heads, 3, token_rows, head_size)
+    projected = lax.psum_scatter(partial, "mxc", scatter_dimension=0, tiled=True)
+    projected = lax.psum_scatter(projected, "mxx", scatter_dimension=0, tiled=True).astype(jnp.bfloat16)
     images = token_rows // PATCH
     shaped = projected.reshape(local_heads, 3, images, PATCH, head_size)
     q_hat, q_inv = head_norm(shaped[:, 0].astype(jnp.float32))
@@ -90,14 +92,19 @@
 
     block_rows = width_local // (lax.axis_size("dph") * lax.axis_size("dpz"))
     stacked = jnp.stack([head_rows(d_query), head_rows(d_key), head_rows(d_values)], axis=1)
-    gathered = lax.all_gather(stacked, "mx", axis=0, tiled=True)
+    gathered = lax.all_gather(stacked, MX, axis=0, tiled=True)
     d_scaled = jnp.einsum("hste,sdhe->td", gathered, weights, preferred_element_type=jnp.float32)
     feature_part = scaled
+    n_hi = lax.axis_size("dph")
+    n_z = lax.axis_size("dpz")
+    feature_part = (
+        feature_part.reshape(token_rows, n_hi, n_z, -1).transpose(0, 2, 1, 3).reshape(token_rows, -1)
+    )
     w_part = jnp.einsum(
         "td,hste->dshe", feature_part, gathered, preferred_element_type=jnp.float32
     ).astype(jnp.bfloat16)
-    w_half = lax.psum_scatter(w_part, "dph", scatter_dimension=0, tiled=True)
-    w_rows = lax.psum_scatter(w_half, "dpz", scatter_dimension=0, tiled=True).astype(jnp.float32)
+    w_half = lax.psum_scatter(w_part, "dpz", scatter_dimension=0, tiled=True)
+    w_rows = lax.psum_scatter(w_half, "dph", scatter_dimension=0, tiled=True).astype(jnp.float32)
     w_grad = (
         w_rows.reshape(block_rows, 3, group_heads * head_size)
         .transpose(1, 0, 2)
@@ -108,7 +115,7 @@
     d_other = lax.ppermute(d_low, "my", [(0, 1), (1, 0)])
     d_rows = d_low.astype(jnp.float32) + d_other.astype(jnp.float32)
     d_hat = d_rows * gain_row
-    stat_sums = lax.psum((jnp.sum(d_hat, axis=1), jnp.sum(d_hat * normed, axis=1)), "mx")
+    stat_sums = lax.psum((jnp.sum(d_hat, axis=1), jnp.sum(d_hat * normed, axis=1)), MX)
     sum_first = stat_sums[0]
     sum_second = stat_sums[1]
     result_rows = (
@@ -121,14 +128,14 @@
 
 def solution(mesh):
     dp = ("dph", "dpz")
-    devices = mesh.devices.reshape(2, mesh.shape["dp"] // 2, mesh.shape["mx"], mesh.shape["my"])
-    split_mesh = jax.sharding.Mesh(devices, ("dph", "dpz", "mx", "my"))
+    devices = mesh.devices.reshape(2, mesh.shape["dp"] // 2, mesh.shape["mx"] // 2, 2, mesh.shape["my"])
+    split_mesh = jax.sharding.Mesh(devices, ("dph", "dpz") + MX + ("my",))
     in_specs = (
-        P(dp, "mx"),
-        P("mx"),
-        P(None, "mx", "my"),
-        P(None, ("my", "mx"), None),
-        P(dp, ("my", "mx")),
+        P(dp, MX),
+        P(MX),
+        P(None, MX, "my"),
+        P(None, ("my",) + MX, None),
+        P(dp, ("my",) + MX),
     )
-    out_specs = (P(dp, "mx"), P(None, ("mx",) + dp, "my"), P("mx"), P(None, ("my", "mx"), None))
+    out_specs = (P(dp, MX), P(None, MX + dp, "my"), P(MX), P(None, ("my",) + MX, None))
     return jax.shard_map(body, mesh=split_mesh, in_specs=in_specs, out_specs=out_specs, check_vma=False)

time: 419 us -> 385 us (0.919)
  local copies, waits for them, and re-layouts: 68.7 us -> 44.1 us
  blocking collectives: 137 us -> 120 us
  waiting for transfers between devices: 162 us -> 173 us
    reduce_scatter x1 -> x2, waiting for transfers between devices: 0.01 us -> 106 us  [the longest x1 106 us: body(): w_half = lax.psum_scatter(w_part, 'dpz', scatter_dimension=0, tiled=True)]
    unnamed x4 -> x5, waiting for transfers between devices: 118 us -> 22 us
    unnamed x14 -> x21, local copies, waits for them, and re-layouts: 58.5 us -> 10.7 us
    reshape x0 -> x1, local copies, waits for them, and re-layouts: none -> 16 us  [body(): ordered = w_qkv.reshape(3, width_local, n_x, n_c, local_heads, head_size)]
    convert_element_type x0 -> x2, local copies, waits for them, and re-layouts: none -> 13.4 us  [the longest x1 13.2 us: body(): w_part = jnp.einsum('td,hste->dshe', feature_part, gathered, preferred_el...]
    unnamed x1, blocking collectives: 71.4 us -> 58.1 us
    reduce_scatter x2 -> x1, local copies, waits for them, and re-layouts: 7.34 us -> 1.17 us  [body(): lax.psum_scatter(w_half, 'dph', scatter_dimension=0, tiled=True)]
    ppermute x1, waiting for transfers between devices: 10.1 us -> 14.7 us  [body(): d_other = lax.ppermute(d_low, 'my', [(0, 1), (1, 0)])]
  transfers between devices with their start and end apart: 4 -> 5, of which waited for: 3 -> 4; matrix products, arithmetic and copies ran while one was open for 2% -> 3% of each run, Pallas kernels for 0% -> 0%
where the time goes in v2:
time: 385 us; the launch traced here: 382 us
  waiting for transfers between devices  173 us (45%)
  blocking collectives  120 us (31%)
  local copies, waits for them, and re-layouts  44.1 us (11%)
  matrix products  23.6 us (6%)
  between operations  14.6 us (4%)
  other arithmetic  4.72 us (1%)
    reduce_scatter x1, waiting for transfers between devices, body(): w_half = lax.psum_scatter(w_part, 'dpz', scatter_dimension=0, tiled=True)  106 us
    unnamed x1, blocking collectives  58.1 us
    psum x1, blocking collectives, body(): lax.psum((head_gain_part, feature_part), ('dph', 'dpz'))  39.4 us
    all_gather x1, waiting for transfers between devices, body(): gathered = lax.all_gather(stacked, MX, axis=0, tiled=True)  30.6 us
    unnamed x5, waiting for transfers between devices  22 us
    reshape x1, local copies, waits for them, and re-layouts, body(): ordered = w_qkv.reshape(3, width_local, n_x, n_c, local_heads, head_size)  16 us
    ppermute x1, waiting for transfers between devices, body(): d_other = lax.ppermute(d_low, 'my', [(0, 1), (1, 0)])  14.7 us
    convert_element_type x1, local copies, waits for them, and re-layouts, body(): w_part = jnp.einsum('td,hste->dshe', feature_part, gathered, preferred_el...  13.2 us
  transfers between devices with their start and end apart: 5, of which 4 were waited for; matrix products, arithmetic and copies ran while one was open for 3% of the time, Pallas kernels for 0%

profile of v2, /device:TPU:2, one launch (start us, length us, event | category | flops | bytes accessed | tf_op | source)
XLA Modules:
  0.0 382.0 jit_solution(9797525279747463257)
XLA Ops:
  7.2 0.0 copy-start
  7.2 0.0 reduce-scatter.14.cloned.1.call-start
  7.2 1.2 fusion.35
  8.4 0.0 copy-start.2
  8.5 0.0 copy-start.6
  8.5 16.0 %reshape.273 = bf16[3,768,4,2,2,128]{5,4,3,2,1,0:T(2,128)(2,1)} reshape(bf16[3,768,2048]{2,1,0:T(8,128)(2,1)} %param.7) | data formatting | bytes 18874368 | tf_op jit(solution)/shard_map/reshape | solution.py:48
  24.4 11.6 %all-reduce.3 = (f32[256]{0:T(256)S(1)}, f32[256]{0:T(256)S(1)}) all-reduce(f32[256]{0:T(256)S(1)} %get-tuple-element.18, f32[256]{0:T(256)S(1)} %get-tuple-element.17), channel_id=1, replica_groups=mesh['dph'=2,'dpz'=8,'mxx'=4,'mxc'=2,'my'=2] {'mxx','mxc'}, use_global_device_ids=true, to_apply=%region_3.0 | all-reduce | flops 512 | bytes 4096 | tf_op jit(solution)/shard_map/psum | solution.py:36
  36.1 0.0 copy-done.2
  36.1 0.0 copy-done.6
  36.1 0.2 fusion.41
  36.3 0.0 copy-start.4
  36.4 0.7 copy-done.4
  37.1 5.3 %fusion.9 = f32[2,4,2,3,256,128]{5,4,2,0,1,3:T(8,128)S(1)} fusion(bf16[3,768,4,2,2,128]{5,4,3,2,1,0:T(2,128)(2,1)} %reshape.273, bf16[256,768]{1,0:T(8,128)(2,1)S(1)} %fusion.41), kind=kOutput, calls=%fused_computation.11 | convolution fusion | flops 2415919104 | bytes 16121856 | tf_op jit(solution)/shard_map/td,sdabje->bajste/dot_general | solution.py:49
  42.4 0.7 copy.43
  43.1 6.3 %copy.112 = f32[2,8,768,128]{3,1,2,0:T(8,128)} copy(f32[2,8,768,128]{3,2,1,0:T(8,128)S(1)} %bitcast.168) | data formatting | bytes 12582912
  49.4 0.0 copy-start.8
  49.4 0.0 copy-start.7
  49.4 0.0 reduce-scatter.14.cloned.1.call-update
  49.4 0.0 all-gather.2.cloned.1.call-start
  49.4 0.6 copy-done.8
  50.0 0.6 dynamic-slice
  51.3 0.0 copy-done.7
  51.3 21.9 %reduce-scatter.14.cloned.1.call-done = f32[8,98304]{1,0:T(8,128)} async-done(((f32[16,98304]{1,0:T(8,128)}), f32[8,98304]{1,0:T(8,128)}) %reduce-scatter.14.cloned.1.call-update) | async-done | bytes 3145744
  73.2 2.4 copy.75
  75.6 58.1 %all-reduce.5 = bf16[8,3,256,128]{3,2,0,1:T(8,128)(2,1)} all-reduce(f32[8,3,256,128]{3,2,0,1:T(8,128)S(1)} %copy.75), channel_id=3, replica_groups=mesh['dph'=2,'dpz'=8,'mxx'=4,'mxc'=2,'my'=2] {'mxx'}, use_global_device_ids=true, to_apply=%region_5.0.clone | all-reduce | flops 786432 | bytes 4718592
  133.7 1.0 fusion.50
  134.8 0.3 fusion.52
  135.1 0.0 copy-done
  135.1 0.2 convolution_bitcast_fusion
  135.3 0.0 copy-start.5
  135.3 0.8 fusion.107
  136.2 0.2 fusion.28
  136.4 0.4 fusion.29
  136.8 1.1 fusion.64
  137.9 0.6 fusion.82
  138.6 0.8 pad_maximum_fusion
  139.4 0.0 all-gather.2.cloned.1.call-update
  139.4 0.2 reduce-scatter.10.cloned.1.call-start
  139.6 0.0 copy-done.5
  139.6 0.2 copy.54
  139.8 30.6 %all-gather.2.cloned.1.call-done = bf16[16,3,256,128]{3,2,0,1:T(8,128)(2,1)} async-done(((bf16[2,3,256,128]{3,2,0,1:T(8,128)(2,1)}), bf16[16,3,256,128]{3,2,0,1:T(8,128)(2,1)}) %all-gather.2.cloned.1.call-update) | async-done | bytes 3145744 | tf_op jit(solution)/shard_map/all_gather | solution.py:95
  170.4 8.2 %convert_bitcast_fusion = bf16[768,3,16,128]{0,3,1,2:T(8,128)(2,1)} fusion(bf16[256,768,1,1]{0,1,3,2:T(8,128)(2,1)S(1)} %bitcast.170, bf16[16,3,256,128]{3,2,0,1:T(8,128)(2,1)} %all-gather.2.cloned.1.call-done), kind=kOutput, calls=%fused_computation.7 | convolution fusion | flops 2420637696 | bytes 12976128 | tf_op jit(solution)/shard_map/td,hste->dshe/dot_general | solution.py:103
  178.6 13.2 %copy.58 = bf16[768,3,16,128]{3,2,1,0:T(8,128)(2,1)} copy(bf16[768,3,16,128]{0,3,1,2:T(8,128)(2,1)} %convert_bitcast_fusion) | data formatting | bytes 18874368 | tf_op jit(solution)/shard_map/convert_element_type | solution.py:105
  191.8 0.0 reduce-scatter.10.cloned.1.call-update
  191.9 0.0 reduce-scatter.12.cloned.1.call-start
  191.9 105.9 %reduce-scatter.10.cloned.1.call-done = bf16[96,3,16,128]{3,2,1,0:T(8,128)(2,1)} async-done(((bf16[768,3,16,128]{3,2,1,0:T(8,128)(2,1)}), bf16[96,3,16,128]{3,2,1,0:T(8,128)(2,1)}) %reduce-scatter.10.cloned.1.call-update) | async-done | bytes 1179664 | tf_op jit(solution)/shard_map/reduce_scatter | solution.py:106
  297.8 0.0 reduce-scatter.12.cloned.1.call-update
  297.8 0.0 copy-start.3
  297.8 0.0 copy-start.1
  297.9 7.3 %fusion.18 = bf16[256,768]{1,0:T(8,128)(2,1)S(1)} fusion(bf16[16,3,256,128]{3,2,0,1:T(8,128)(2,1)} %all-gather.2.cloned.1.call-done, bf16[3,768,2048]{2,1,0:T(8,128)(2,1)} %param.7), kind=kOutput, calls=%fused_computation.14 | convolution fusion | flops 2416115712 | bytes 12976128 | tf_op jit(solution)/shard_map/hste,sdhe->td/dot_general | solution.py:96
  305.2 1.6 collective-permute-start
  306.8 14.7 %collective-permute-done = bf16[256,768]{1,0:T(8,128)(2,1)S(1)} collective-permute-done((bf16[256,768]{1,0:T(8,128)(2,1)S(1)}, bf16[256,768]{1,0:T(8,128)(2,1)S(1)}, u32[]{:S(2)}, u32[]{:S(2)}) %collective-permute-start) | collective-permute-done | bytes 393248 | tf_op jit(solution)/shard_map/ppermute | solution.py:115
  321.4 0.0 copy-done.3
  321.4 0.4 fusion.47
  321.9 10.8 %all-reduce.2 = (f32[256]{0:T(256)S(1)}, f32[256]{0:T(256)S(1)}) all-reduce(f32[256]{0:T(256)S(1)} %get-tuple-element.5, f32[256]{0:T(256)S(1)} %get-tuple-element.6), channel_id=1, replica_groups=mesh['dph'=2,'dpz'=8,'mxx'=4,'mxc'=2,'my'=2] {'mxx','mxc'}, use_global_device_ids=true, to_apply=%region_20.0 | all-reduce | flops 512 | bytes 4096 | tf_op jit(solution)/shard_map/psum | solution.py:118
  332.7 39.4 %all-reduce.1 = (f32[768]{0:T(1024)}, f32[2,2,128]{2,1,0:T(2,128)}) all-reduce(f32[768]{0:T(1024)S(1)} %get-tuple-element.4, f32[2,2,128]{2,1,0:T(2,128)S(1)} %pad_maximum_fusion.1), channel_id=1, replica_groups=mesh['dph'=2,'dpz'=8,'mxx'=4,'mxc'=2,'my'=2] {'dph','dpz'}, use_global_device_ids=true, to_apply=%region_24.0 | all-reduce | flops 1280 | bytes 10240 | tf_op jit(solution)/shard_map/psum | solution.py:125
  372.1 1.1 fusion.46
  373.2 0.0 reduce-scatter.12.cloned.1.call-done
  373.2 1.2 copy.59
  374.4 1.1 convert_element_type.148
  375.5 0.0 copy-done.1
  (10 shorter events, 0.1 us)
Async XLA Ops:
  7.2 127.9 %copy-start = (bf16[256,256]{1,0:T(8,128)(2,1)S(1)}, bf16[256,256]{1,0:T(8,128)(2,1)}, u32[]{:S(2)}) copy-start(bf16[256,256]{1,0:T(8,128)(2,1)} %param.9) | copy-start | bytes 393220
  7.2 66.0 %reduce-scatter.14.cloned.1.call-start = ((), (), s32[]{:S(2)}) async-start(), calls=%async_computation.6 | async-start | bytes 9437184
  8.4 27.7 %copy-start.2 = (bf16[256,768]{1,0:T(8,128)(2,1)S(1)}, bf16[256,768]{1,0:T(8,128)(2,1)}, u32[]{:S(2)}) copy-start(bf16[256,768]{1,0:T(8,128)(2,1)} %param.5) | copy-start | bytes 1179652
  8.5 27.7 %copy-start.6 = (f32[768]{0:T(1024)S(1)}, f32[768]{0:T(1024)}, u32[]{:S(2)}) copy-start(f32[768]{0:T(1024)} %param.6) | copy-start | bytes 9220
  36.3 0.7 copy-start.4
  49.4 0.7 copy-start.8
  49.4 1.9 copy-start.7
  49.4 121.0 %all-gather.2.cloned.1.call-start = ((), (), s32[]{:S(2)}) async-start(), calls=%async_computation.3 | async-start | bytes 3538944 | tf_op jit(solution)/shard_map/all_gather | solution.py:95
  135.3 4.3 %copy-start.5 = (bf16[256,768]{1,0:T(8,128)(2,1)S(1)}, bf16[256,768]{1,0:T(8,128)(2,1)}, u32[]{:S(2)}) copy-start(bf16[256,768]{1,0:T(8,128)(2,1)} %copy-done.4) | copy-start | bytes 1179652
  139.4 158.4 %reduce-scatter.10.cloned.1.call-start = ((), (), s32[]{:S(2)}) async-start(), calls=%async_computation.4 | async-start | bytes 10616832 | tf_op jit(solution)/shard_map/reduce_scatter | solution.py:106
  191.9 181.4 %reduce-scatter.12.cloned.1.call-start = ((), (), s32[]{:S(2)}) async-start(), calls=%async_computation.5 | async-start | bytes 1769472 | tf_op jit(solution)/shard_map/reduce_scatter | solution.py:107
  297.8 23.6 %copy-start.3 = (bf16[256,768]{1,0:T(8,128)(2,1)S(1)}, bf16[256,768]{1,0:T(8,128)(2,1)}, u32[]{:S(2)}) copy-start(bf16[256,768]{1,0:T(8,128)(2,1)} %param.5) | copy-start | bytes 1179652
  297.8 77.6 %copy-start.1 = (bf16[256,256]{1,0:T(8,128)(2,1)S(1)}, bf16[256,256]{1,0:T(8,128)(2,1)}, u32[]{:S(2)}) copy-start(bf16[256,256]{1,0:T(8,128)(2,1)} %param.9) | copy-start | bytes 393220
  305.2 16.2 %collective-permute-start = (bf16[256,768]{1,0:T(8,128)(2,1)S(1)}, bf16[256,768]{1,0:T(8,128)(2,1)S(1)}, u32[]{:S(2)}, u32[]{:S(2)}) collective-permute-start(bf16[256,768]{1,0:T(8,128)(2,1)S(1)} %fusion.18), channel_id=1, source_target_pairs={{0,1},{1,0},{2,3},{3,2},{4,5},{5,4},{6,7},{7,6},{8,9},{9,8},{10,11... | collective-permute-start | bytes 1179656 | tf_op jit(solution)/shard_map/ppermute | solution.py:115
Sparse Core Ops, SparseCore 0:
  49.5 23.6 reduce-scatter.13
  139.5 30.8 all-gather.1
  192.0 105.7 reduce-scatter.9
  300.2 31.9 reduce-scatter.11

commit v3 on v1

--- a/solution.py
+++ b/solution.py
@@ -42,12 +42,15 @@
     head_size = qk_gain.shape[2]
     group_heads = w_qkv.shape[2] // head_size
     weights = w_qkv.reshape(3, width_local, group_heads, head_size)
-    projected = lax.psum_scatter(
-        jnp.einsum("td,sdhe->hste", scaled, weights, preferred_element_type=jnp.float32),
+    n_mx = lax.axis_size("mx")
+    partial = jnp.einsum("td,sdhe->hste", scaled, weights, preferred_element_type=jnp.float32)
+    pieces = lax.all_to_all(
+        partial.astype(jnp.bfloat16).reshape(n_mx, local_heads, 3, token_rows, head_size),
         "mx",
-        scatter_dimension=0,
-        tiled=True,
-    ).astype(jnp.bfloat16)
+        split_axis=0,
+        concat_axis=0,
+    )
+    projected = jnp.sum(pieces.astype(jnp.float32), axis=0).astype(jnp.bfloat16)
     images = token_rows // PATCH
     shaped = projected.reshape(local_heads, 3, images, PATCH, head_size)
     q_hat, q_inv = head_norm(shaped[:, 0].astype(jnp.float32))
@@ -93,16 +96,15 @@
     gathered = lax.all_gather(stacked, "mx", axis=0, tiled=True)
     d_scaled = jnp.einsum("hste,sdhe->td", gathered, weights, preferred_element_type=jnp.float32)
     feature_part = scaled
+    n_hi = lax.axis_size("dph")
+    n_z = lax.axis_size("dpz")
+    feature_part = (
+        feature_part.reshape(token_rows, n_hi, n_z, -1).transpose(0, 2, 1, 3).reshape(token_rows, -1)
+    )
     w_part = jnp.einsum(
         "td,hste->dshe", feature_part, gathered, preferred_element_type=jnp.float32
     ).astype(jnp.bfloat16)
-    w_half = lax.psum_scatter(w_part, "dph", scatter_dimension=0, tiled=True)
-    w_rows = lax.psum_scatter(w_half, "dpz", scatter_dimension=0, tiled=True).astype(jnp.float32)
-    w_grad = (
-        w_rows.reshape(block_rows, 3, group_heads * head_size)
-        .transpose(1, 0, 2)
-        .astype(jnp.bfloat16)
-    )
+    w_half = lax.psum_scatter(w_part, "dpz", scatter_dimension=0, tiled=True)
     gain_row = ln_gain[None, :]
     d_low = d_scaled.astype(jnp.bfloat16)
     d_other = lax.ppermute(d_low, "my", [(0, 1), (1, 0)])
@@ -116,6 +118,15 @@
     ).astype(jnp.bfloat16)
     feature_part = jnp.sum(d_rows * normed, axis=0)
     head_total, feature_total = lax.psum((head_gain_part, feature_part), ("dph", "dpz"))
+    w_half, result_rows, feature_total, head_total = lax.optimization_barrier(
+        (w_half, result_rows, feature_total, head_total)
+    )
+    w_rows = lax.psum_scatter(w_half, "dph", scatter_dimension=0, tiled=True).astype(jnp.float32)
+    w_grad = (
+        w_rows.reshape(block_rows, 3, group_heads * head_size)
+        .transpose(1, 0, 2)
+        .astype(jnp.bfloat16)
+    )
     return (result_rows, w_grad, feature_total, head_total)
 
 

time: 419 us -> 285 us (0.68)
  blocking collectives: 137 us -> 69.2 us
  local copies, waits for them, and re-layouts: 68.7 us -> 18.4 us
  waiting for transfers between devices: 162 us -> 137 us
  starting transfers between devices: 0.97 us -> 8.86 us
    unnamed x4 -> x3, waiting for transfers between devices: 118 us -> 0.05 us
    unnamed x1 -> x0, blocking collectives: 71.4 us -> none
    reduce_scatter x1 -> x2, waiting for transfers between devices: 0.01 us -> 58.9 us  [the longest x1 29.5 us: body(): lax.psum_scatter(w_half, 'dph', scatter_dimension=0, tiled=True)]
    unnamed x14, local copies, waits for them, and re-layouts: 58.5 us -> 0.78 us
    all_to_all x0 -> x1, waiting for transfers between devices: none -> 37 us  [body(): lax.all_to_all(partial.astype(jnp.bfloat16).reshape(n_mx, local_heads, 3,...]
    convert_element_type x0 -> x2, local copies, waits for them, and re-layouts: none -> 13.4 us  [the longest x1 13.2 us: body(): w_part = jnp.einsum('td,hste->dshe', feature_part, gathered, preferred_el...]
    all_to_all x0 -> x1, starting transfers between devices: none -> 7.03 us  [body(): lax.all_to_all(partial.astype(jnp.bfloat16).reshape(n_mx, local_heads, 3,...]
    reduce_scatter x2 -> x1, local copies, waits for them, and re-layouts: 7.34 us -> 1.17 us  [body(): lax.psum_scatter(w_half, 'dph', scatter_dimension=0, tiled=True)]
  transfers between devices with their start and end apart: 4 -> 5, of which waited for: 3 -> 5; matrix products, arithmetic and copies ran while one was open for 2% -> 3% of each run, Pallas kernels for 0% -> 0%
where the time goes in v3:
time: 285 us; the launch traced here: 283 us
  waiting for transfers between devices  137 us (48%)
  blocking collectives  69.2 us (24%)
  matrix products  28.1 us (10%)
  local copies, waits for them, and re-layouts  18.4 us (6%)
  between operations  13.9 us (5%)
  starting transfers between devices  8.86 us (3%)
  other arithmetic  8.11 us (3%)
    psum x1, blocking collectives, body(): lax.psum((head_gain_part, feature_part), ('dph', 'dpz'))  45.9 us
    all_to_all x1, waiting for transfers between devices, body(): lax.all_to_all(partial.astype(jnp.bfloat16).reshape(n_mx, local_heads, 3,...  37 us
    all_gather x1, waiting for transfers between devices, body(): gathered = lax.all_gather(stacked, 'mx', axis=0, tiled=True)  31.1 us
    reduce_scatter x1, waiting for transfers between devices, body(): lax.psum_scatter(w_half, 'dph', scatter_dimension=0, tiled=True)  29.5 us
    reduce_scatter x1, waiting for transfers between devices, body(): w_half = lax.psum_scatter(w_part, 'dpz', scatter_dimension=0, tiled=True)  29.4 us
    convert_element_type x1, local copies, waits for them, and re-layouts, body(): w_part = jnp.einsum('td,hste->dshe', feature_part, gathered, preferred_el...  13.2 us
    psum x1, blocking collectives, body(): lax.psum((jnp.sum(widened, axis=1), jnp.sum(widened * widened, axis=1)),...  11.7 us
    psum x1, blocking collectives, body(): lax.psum((jnp.sum(d_hat, axis=1), jnp.sum(d_hat * normed, axis=1)), 'mx')  11.6 us
  transfers between devices with their start and end apart: 5, of which 5 were waited for; matrix products, arithmetic and copies ran while one was open for 3% of the time, Pallas kernels for 0%

profile of v3, /device:TPU:2, one launch (start us, length us, event | category | flops | bytes accessed | tf_op | source)
XLA Modules:
  0.0 283.5 jit_solution(17377122517470437673)
XLA Ops:
  7.2 0.0 copy-start
  7.2 1.3 convert_reduce_fusion
  8.4 11.7 %all-reduce.2 = (f32[256]{0:T(256)S(1)}, f32[256]{0:T(256)S(1)}) all-reduce(f32[256]{0:T(256)S(1)} %get-tuple-element.26, f32[256]{0:T(256)S(1)} %get-tuple-element.25), channel_id=1, replica_groups=mesh['dph'=2,'dpz'=8,'mx'=8,'my'=2] {'mx'}, use_global_device_ids=true, to_apply=%region_3.0 | all-reduce | flops 512 | bytes 4096 | tf_op jit(solution)/shard_map/psum | solution.py:35
  20.1 1.2 fusion.41
  21.3 0.0 copy-start.3
  21.4 0.7 copy-done.3
  22.1 6.3 %fusion.10 = bf16[256,3,16,128]{3,0,2,1:T(8,128)(2,1)S(1)} fusion(bf16[256,768]{1,0:T(8,128)(2,1)S(1)} %fusion.41, bf16[3,768,2048]{2,1,0:T(8,128)(2,1)} %param.7), kind=kOutput, calls=%fused_computation.11 | convolution fusion | flops 2417491968 | bytes 12976128 | tf_op jit(solution)/shard_map/td,sdhe->hste/dot_general | solution.py:46
  28.4 0.0 copy-start.6
  28.4 2.0 copy.41
  30.5 7.0 %all-to-all-start = ((bf16[8,2,3,256,128]{4,3,1,2,0:T(8,128)(2,1)}), bf16[8,2,3,256,128]{4,3,1,2,0:T(8,128)(2,1)S(1)}, u32[]{:S(2)}, u32[]{:S(2)}) async-start(bf16[8,2,3,256,128]{4,3,1,2,0:T(8,128)(2,1)} %copy.41), calls=%async_computation | async-start | bytes 6291456 | tf_op jit(solution)/shard_map/all_to_all | solution.py:47
  37.5 0.0 all-gather.2.cloned.1.call-start
  37.5 0.0 copy-done.6
  37.5 37.0 %all-to-all-done = bf16[8,2,3,256,128]{4,3,1,2,0:T(8,128)(2,1)S(1)} async-done(((bf16[8,2,3,256,128]{4,3,1,2,0:T(8,128)(2,1)}), bf16[8,2,3,256,128]{4,3,1,2,0:T(8,128)(2,1)S(1)}, u32[]{:S(2)}, u32[]{:S(2)}) %all-to-all-start) | async-done | bytes 3145760 | tf_op jit(solution)/shard_map/all_to_all | solution.py:47
  74.5 1.3 reduce_sum.167
  75.8 0.0 copy-start.2
  75.8 0.0 copy-start.4
  75.8 1.3 fusion.52
  77.1 0.0 copy-done
  77.1 1.1 convolution_bitcast_fusion
  78.3 1.6 fusion.107
  79.8 0.2 fusion.29
  80.1 1.3 fusion.30
  81.4 2.1 fusion.64
  83.5 0.0 copy-done.2
  83.5 0.6 fusion.82
  84.2 0.8 pad_maximum_fusion
  85.0 0.0 all-gather.2.cloned.1.call-update
  85.0 0.0 reduce-scatter.3.cloned.1.call-start
  85.0 0.0 copy-done.4
  85.0 0.2 copy.49
  85.2 31.1 %all-gather.2.cloned.1.call-done = bf16[16,3,256,128]{3,2,0,1:T(8,128)(2,1)} async-done(((bf16[2,3,256,128]{3,2,0,1:T(8,128)(2,1)}), bf16[16,3,256,128]{3,2,0,1:T(8,128)(2,1)}) %all-gather.2.cloned.1.call-update) | async-done | bytes 3145744 | tf_op jit(solution)/shard_map/all_gather | solution.py:96
  116.4 8.2 %convert_bitcast_fusion = bf16[768,3,16,128]{0,3,1,2:T(8,128)(2,1)} fusion(bf16[256,768,1,1]{0,1,3,2:T(8,128)(2,1)S(1)} %bitcast.162, bf16[16,3,256,128]{3,2,0,1:T(8,128)(2,1)} %all-gather.2.cloned.1.call-done), kind=kOutput, calls=%fused_computation.8 | convolution fusion | flops 2420637696 | bytes 12976128 | tf_op jit(solution)/shard_map/td,hste->dshe/dot_general | solution.py:104
  124.6 13.2 %copy.53 = bf16[768,3,16,128]{3,2,1,0:T(8,128)(2,1)} copy(bf16[768,3,16,128]{0,3,1,2:T(8,128)(2,1)} %convert_bitcast_fusion) | data formatting | bytes 18874368 | tf_op jit(solution)/shard_map/convert_element_type | solution.py:106
  137.8 0.0 reduce-scatter.3.cloned.1.call-update
  137.8 0.0 copy-start.1
  137.8 0.0 copy-start.5
  137.8 0.2 reduce-scatter.5.cloned.1.call-start
  138.1 7.3 %fusion.19 = bf16[256,768]{1,0:T(8,128)(2,1)S(1)} fusion(bf16[16,3,256,128]{3,2,0,1:T(8,128)(2,1)} %all-gather.2.cloned.1.call-done, bf16[3,768,2048]{2,1,0:T(8,128)(2,1)} %param.7), kind=kOutput, calls=%fused_computation.14 | convolution fusion | flops 2416115712 | bytes 12976128 | tf_op jit(solution)/shard_map/hste,sdhe->td/dot_general | solution.py:97
  145.4 1.6 collective-permute-start
  146.9 9.8 %collective-permute-done = bf16[256,768]{1,0:T(8,128)(2,1)S(1)} collective-permute-done((bf16[256,768]{1,0:T(8,128)(2,1)S(1)}, bf16[256,768]{1,0:T(8,128)(2,1)S(1)}, u32[]{:S(2)}, u32[]{:S(2)}) %collective-permute-start) | collective-permute-done | bytes 393248 | tf_op jit(solution)/shard_map/ppermute | solution.py:110
  156.7 0.0 copy-done.1
  156.7 0.0 copy-done.5
  156.7 0.4 fusion.47
  157.1 11.6 %all-reduce.1 = (f32[256]{0:T(256)S(1)}, f32[256]{0:T(256)S(1)}) all-reduce(f32[256]{0:T(256)S(1)} %get-tuple-element.13, f32[256]{0:T(256)S(1)} %get-tuple-element.14), channel_id=1, replica_groups=mesh['dph'=2,'dpz'=8,'mx'=8,'my'=2] {'mx'}, use_global_device_ids=true, to_apply=%region_20.0 | all-reduce | flops 512 | bytes 4096 | tf_op jit(solution)/shard_map/psum | solution.py:113
  168.7 45.9 %all-reduce = (f32[768]{0:T(1024)}, f32[2,2,128]{2,1,0:T(2,128)}) all-reduce(f32[768]{0:T(1024)S(1)} %get-tuple-element.12, f32[2,2,128]{2,1,0:T(2,128)S(1)} %pad_maximum_fusion.1), channel_id=1, replica_groups=mesh['dph'=2,'dpz'=8,'mx'=8,'my'=2] {'dph','dpz'}, use_global_device_ids=true, to_apply=%region_22.0 | all-reduce | flops 1280 | bytes 10240 | tf_op jit(solution)/shard_map/psum | solution.py:120
  214.6 1.1 fusion.46
  215.7 29.4 %reduce-scatter.3.cloned.1.call-done = bf16[96,3,16,128]{3,2,1,0:T(8,128)(2,1)} async-done(((bf16[768,3,16,128]{3,2,1,0:T(8,128)(2,1)}), bf16[96,3,16,128]{3,2,1,0:T(8,128)(2,1)}) %reduce-scatter.3.cloned.1.call-update) | async-done | bytes 1179664 | tf_op jit(solution)/shard_map/reduce_scatter | solution.py:107
  245.2 0.0 reduce-scatter.5.cloned.1.call-update
  245.2 29.5 %reduce-scatter.5.cloned.1.call-done = bf16[48,3,16,128]{3,2,1,0:T(8,128)(2,1)} async-done(((bf16[96,3,16,128]{3,2,1,0:T(8,128)(2,1)}), bf16[48,3,16,128]{3,2,1,0:T(8,128)(2,1)}) %reduce-scatter.5.cloned.1.call-update) | async-done | bytes 589840 | tf_op jit(solution)/shard_map/reduce_scatter | solution.py:124
  274.7 1.2 copy.58
  275.9 1.1 convert_element_type.154
  (10 shorter events, 0.1 us)
Async XLA Ops:
  7.2 69.9 %copy-start = (bf16[256,256]{1,0:T(8,128)(2,1)S(1)}, bf16[256,256]{1,0:T(8,128)(2,1)}, u32[]{:S(2)}) copy-start(bf16[256,256]{1,0:T(8,128)(2,1)} %param.9) | copy-start | bytes 393220
  21.3 0.7 copy-start.3
  28.4 9.1 %copy-start.6 = (f32[2,2,128]{2,1,0:T(2,128)S(1)}, f32[2,2,128]{2,1,0:T(2,128)}, u32[]{:S(2)}) copy-start(f32[2,2,128]{2,1,0:T(2,128)} %param.8) | copy-start | bytes 6148
  30.5 44.0 %all-to-all-start = ((bf16[8,2,3,256,128]{4,3,1,2,0:T(8,128)(2,1)}), bf16[8,2,3,256,128]{4,3,1,2,0:T(8,128)(2,1)S(1)}, u32[]{:S(2)}, u32[]{:S(2)}) async-start(bf16[8,2,3,256,128]{4,3,1,2,0:T(8,128)(2,1)} %copy.41), calls=%async_computation | async-start | bytes 6291456 | tf_op jit(solution)/shard_map/all_to_all | solution.py:47
  37.5 78.9 %all-gather.2.cloned.1.call-start = ((), (), s32[]{:S(2)}) async-start(), calls=%async_computation.3 | async-start | bytes 3538944 | tf_op jit(solution)/shard_map/all_gather | solution.py:96
  75.8 7.8 %copy-start.2 = (bf16[2,3,256,128]{3,2,0,1:T(8,128)(2,1)S(1)}, bf16[2,3,256,128]{3,2,0,1:T(8,128)(2,1)}, u32[]{:S(2)}) copy-start(bf16[2,3,256,128]{3,2,0,1:T(8,128)(2,1)} %reduce_sum.167) | copy-start | bytes 1179652
  75.8 9.2 %copy-start.4 = (bf16[256,768]{1,0:T(8,128)(2,1)S(1)}, bf16[256,768]{1,0:T(8,128)(2,1)}, u32[]{:S(2)}) copy-start(bf16[256,768]{1,0:T(8,128)(2,1)} %copy-done.3) | copy-start | bytes 1179652
  85.0 160.2 %reduce-scatter.3.cloned.1.call-start = ((), (), s32[]{:S(2)}) async-start(), calls=%async_computation.4 | async-start | bytes 10616832 | tf_op jit(solution)/shard_map/reduce_scatter | solution.py:107
  137.8 18.9 %copy-start.1 = (bf16[256,768]{1,0:T(8,128)(2,1)S(1)}, bf16[256,768]{1,0:T(8,128)(2,1)}, u32[]{:S(2)}) copy-start(bf16[256,768]{1,0:T(8,128)(2,1)} %param.5) | copy-start | bytes 1179652
  137.8 18.9 %copy-start.5 = (f32[768]{0:T(1024)S(1)}, f32[768]{0:T(1024)}, u32[]{:S(2)}) copy-start(f32[768]{0:T(1024)} %param.6) | copy-start | bytes 9220
  137.8 136.9 %reduce-scatter.5.cloned.1.call-start = ((), (), s32[]{:S(2)}) async-start(), calls=%async_computation.5 | async-start | bytes 1769472 | tf_op jit(solution)/shard_map/reduce_scatter | solution.py:124
  145.4 11.3 %collective-permute-start = (bf16[256,768]{1,0:T(8,128)(2,1)S(1)}, bf16[256,768]{1,0:T(8,128)(2,1)S(1)}, u32[]{:S(2)}, u32[]{:S(2)}) collective-permute-start(bf16[256,768]{1,0:T(8,128)(2,1)S(1)} %fusion.19), channel_id=1, source_target_pairs={{0,1},{1,0},{2,3},{3,2},{4,5},{5,4},{6,7},{7,6},{8,9},{9,8},{10,11... | collective-permute-start | bytes 1179656 | tf_op jit(solution)/shard_map/ppermute | solution.py:110
Sparse Core Ops, SparseCore 0:
  85.1 31.2 all-gather.1
  137.9 107.1 reduce-scatter.2
  247.7 26.9 reduce-scatter.4

commit v4 on v3

--- a/solution.py
+++ b/solution.py
@@ -45,12 +45,12 @@
     n_mx = lax.axis_size("mx")
     partial = jnp.einsum("td,sdhe->hste", scaled, weights, preferred_element_type=jnp.float32)
     pieces = lax.all_to_all(
-        partial.astype(jnp.bfloat16).reshape(n_mx, local_heads, 3, token_rows, head_size),
+        partial.reshape(n_mx, local_heads, 3, token_rows, head_size),
         "mx",
         split_axis=0,
         concat_axis=0,
     )
-    projected = jnp.sum(pieces.astype(jnp.float32), axis=0).astype(jnp.bfloat16)
+    projected = jnp.sum(pieces, axis=0).astype(jnp.bfloat16)
     images = token_rows // PATCH
     shaped = projected.reshape(local_heads, 3, images, PATCH, head_size)
     q_hat, q_inv = head_norm(shaped[:, 0].astype(jnp.float32))

time: 285 us -> 316 us (1.11)
  waiting for transfers between devices: 137 us -> 171 us
  matrix products: 28.1 us -> 23.5 us
    all_to_all x1, waiting for transfers between devices: 37 us -> 70.8 us  [body(): lax.all_to_all(partial.reshape(n_mx, local_heads, 3, token_rows, head_siz...]
where the time goes in v4:
time: 316 us; the launch traced here: 315 us
  waiting for transfers between devices  171 us (54%)
  blocking collectives  69.2 us (22%)
  matrix products  23.5 us (7%)
  local copies, waits for them, and re-layouts  19 us (6%)
  between operations  13.9 us (4%)
  starting transfers between devices  9.75 us (3%)
  other arithmetic  8.94 us (3%)
    all_to_all x1, waiting for transfers between devices, body(): lax.all_to_all(partial.reshape(n_mx, local_heads, 3, token_rows, head_siz...  70.8 us
    psum x1, blocking collectives, body(): lax.psum((head_gain_part, feature_part), ('dph', 'dpz'))  45.9 us
    all_gather x1, waiting for transfers between devices, body(): gathered = lax.all_gather(stacked, 'mx', axis=0, tiled=True)  31.1 us
    reduce_scatter x1, waiting for transfers between devices, body(): w_half = lax.psum_scatter(w_part, 'dpz', scatter_dimension=0, tiled=True)  29.6 us
    reduce_scatter x1, waiting for transfers between devices, body(): lax.psum_scatter(w_half, 'dph', scatter_dimension=0, tiled=True)  29.5 us
    convert_element_type x1, local copies, waits for them, and re-layouts, body(): w_part = jnp.einsum('td,hste->dshe', feature_part, gathered, preferred_el...  13.2 us
    psum x1, blocking collectives, body(): lax.psum((jnp.sum(widened, axis=1), jnp.sum(widened * widened, axis=1)),...  11.7 us
    psum x1, blocking collectives, body(): lax.psum((jnp.sum(d_hat, axis=1), jnp.sum(d_hat * normed, axis=1)), 'mx')  11.6 us
  transfers between devices with their start and end apart: 5, of which 5 were waited for; matrix products, arithmetic and copies ran while one was open for 3% of the time, Pallas kernels for 0%

profile of v4, /device:TPU:2, one launch (start us, length us, event | category | flops | bytes accessed | tf_op | source)
XLA Modules:
  0.0 315.1 jit_solution(18215664076476645847)
XLA Ops:
  7.2 0.0 copy-start
  7.2 1.3 convert_reduce_fusion
  8.4 11.7 %all-reduce.2 = (f32[256]{0:T(256)S(1)}, f32[256]{0:T(256)S(1)}) all-reduce(f32[256]{0:T(256)S(1)} %get-tuple-element.26, f32[256]{0:T(256)S(1)} %get-tuple-element.25), channel_id=1, replica_groups=mesh['dph'=2,'dpz'=8,'mx'=8,'my'=2] {'mx'}, use_global_device_ids=true, to_apply=%region_3.0 | all-reduce | flops 512 | bytes 4096 | tf_op jit(solution)/shard_map/psum | solution.py:35
  20.1 1.2 fusion.38
  21.3 5.3 %fusion.5 = f32[256,3,16,128]{3,0,2,1:T(8,128)S(1)} fusion(bf16[256,768]{1,0:T(8,128)(2,1)S(1)} %fusion.38, bf16[3,768,2048]{2,1,0:T(8,128)(2,1)} %param.7), kind=kOutput, calls=%fused_computation.5 | convolution fusion | flops 2415919104 | bytes 16121856 | tf_op jit(solution)/shard_map/td,sdhe->hste/dot_general | solution.py:46
  26.6 0.0 copy-start.3
  26.6 3.4 %copy.41 = f32[8,2,3,256,128]{4,3,1,2,0:T(8,128)} copy(f32[8,2,3,256,128]{4,3,1,0,2:T(8,128)S(1)} %bitcast.155) | data formatting | bytes 12582912 | tf_op jit(solution)/shard_map/reshape | solution.py:48
  30.0 8.1 %all-to-all-start = ((f32[8,2,3,256,128]{4,3,1,2,0:T(8,128)}), f32[8,2,3,256,128]{4,3,1,2,0:T(8,128)}, u32[]{:S(2)}, u32[]{:S(2)}) async-start(f32[8,2,3,256,128]{4,3,1,2,0:T(8,128)} %copy.41), calls=%async_computation | async-start | bytes 12582912 | tf_op jit(solution)/shard_map/all_to_all | solution.py:47
  38.1 0.0 all-gather.2.cloned.1.call-start
  38.1 0.0 copy-done.3
  38.1 70.8 %all-to-all-done = f32[8,2,3,256,128]{4,3,1,2,0:T(8,128)} async-done(((f32[8,2,3,256,128]{4,3,1,2,0:T(8,128)}), f32[8,2,3,256,128]{4,3,1,2,0:T(8,128)}, u32[]{:S(2)}, u32[]{:S(2)}) %all-to-all-start) | async-done | bytes 6291488 | tf_op jit(solution)/shard_map/all_to_all | solution.py:47
  108.9 3.2 %reduce_sum.164 = bf16[2,3,256,128]{3,2,0,1:T(8,128)(2,1)S(1)} reduce(f32[8,2,3,256,128]{4,3,1,2,0:T(8,128)} %all-to-all-done, f32[]{:T(128)} %constant.20.clone.1), dimensions={0}, to_apply=%region_4.0 | reduce | flops 1376256 | bytes 6684676 | tf_op jit(solution)/shard_map/reduce_sum | solution.py:53
  112.0 0.3 fusion.49
  112.3 0.0 copy-done
  112.3 0.2 convolution_bitcast_fusion
  112.6 0.8 fusion.104
  113.4 0.2 fusion.26
  113.7 0.4 fusion.27
  114.1 1.1 fusion.61
  115.2 0.6 fusion.79
  115.8 0.8 pad_maximum_fusion
  116.6 0.0 all-gather.2.cloned.1.call-update
  116.6 0.0 reduce-scatter.3.cloned.1.call-start
  116.7 0.2 copy.49
  116.9 31.1 %all-gather.2.cloned.1.call-done = bf16[16,3,256,128]{3,2,0,1:T(8,128)(2,1)} async-done(((bf16[2,3,256,128]{3,2,0,1:T(8,128)(2,1)}), bf16[16,3,256,128]{3,2,0,1:T(8,128)(2,1)}) %all-gather.2.cloned.1.call-update) | async-done | bytes 3145744 | tf_op jit(solution)/shard_map/all_gather | solution.py:96
  148.0 8.2 %convert_bitcast_fusion = bf16[768,3,16,128]{0,3,1,2:T(8,128)(2,1)} fusion(bf16[256,768,1,1]{0,1,3,2:T(8,128)(2,1)S(1)} %bitcast.162, bf16[16,3,256,128]{3,2,0,1:T(8,128)(2,1)} %all-gather.2.cloned.1.call-done), kind=kOutput, calls=%fused_computation.8 | convolution fusion | flops 2420637696 | bytes 12976128 | tf_op jit(solution)/shard_map/td,hste->dshe/dot_general | solution.py:104
  156.2 13.2 %copy.53 = bf16[768,3,16,128]{3,2,1,0:T(8,128)(2,1)} copy(bf16[768,3,16,128]{0,3,1,2:T(8,128)(2,1)} %convert_bitcast_fusion) | data formatting | bytes 18874368 | tf_op jit(solution)/shard_map/convert_element_type | solution.py:106
  169.4 0.0 reduce-scatter.3.cloned.1.call-update
  169.5 0.0 copy-start.1
  169.5 0.0 copy-start.2
  169.5 0.0 reduce-scatter.5.cloned.1.call-start
  169.5 7.3 %fusion.16 = bf16[256,768]{1,0:T(8,128)(2,1)S(1)} fusion(bf16[16,3,256,128]{3,2,0,1:T(8,128)(2,1)} %all-gather.2.cloned.1.call-done, bf16[3,768,2048]{2,1,0:T(8,128)(2,1)} %param.7), kind=kOutput, calls=%fused_computation.13 | convolution fusion | flops 2416115712 | bytes 12976128 | tf_op jit(solution)/shard_map/hste,sdhe->td/dot_general | solution.py:97
  176.9 1.6 collective-permute-start
  178.4 9.8 %collective-permute-done = bf16[256,768]{1,0:T(8,128)(2,1)S(1)} collective-permute-done((bf16[256,768]{1,0:T(8,128)(2,1)S(1)}, bf16[256,768]{1,0:T(8,128)(2,1)S(1)}, u32[]{:S(2)}, u32[]{:S(2)}) %collective-permute-start) | collective-permute-done | bytes 393248 | tf_op jit(solution)/shard_map/ppermute | solution.py:110
  188.2 0.0 copy-done.1
  188.2 0.0 copy-done.2
  188.2 0.4 fusion.44
  188.6 11.6 %all-reduce.1 = (f32[256]{0:T(256)S(1)}, f32[256]{0:T(256)S(1)}) all-reduce(f32[256]{0:T(256)S(1)} %get-tuple-element.13, f32[256]{0:T(256)S(1)} %get-tuple-element.14), channel_id=1, replica_groups=mesh['dph'=2,'dpz'=8,'mx'=8,'my'=2] {'mx'}, use_global_device_ids=true, to_apply=%region_20.0 | all-reduce | flops 512 | bytes 4096 | tf_op jit(solution)/shard_map/psum | solution.py:113
  200.2 45.9 %all-reduce = (f32[768]{0:T(1024)}, f32[2,2,128]{2,1,0:T(2,128)}) all-reduce(f32[768]{0:T(1024)S(1)} %get-tuple-element.12, f32[2,2,128]{2,1,0:T(2,128)S(1)} %pad_maximum_fusion.1), channel_id=1, replica_groups=mesh['dph'=2,'dpz'=8,'mx'=8,'my'=2] {'dph','dpz'}, use_global_device_ids=true, to_apply=%region_22.0 | all-reduce | flops 1280 | bytes 10240 | tf_op jit(solution)/shard_map/psum | solution.py:120
  246.2 1.1 fusion.43
  247.3 29.6 %reduce-scatter.3.cloned.1.call-done = bf16[96,3,16,128]{3,2,1,0:T(8,128)(2,1)} async-done(((bf16[768,3,16,128]{3,2,1,0:T(8,128)(2,1)}), bf16[96,3,16,128]{3,2,1,0:T(8,128)(2,1)}) %reduce-scatter.3.cloned.1.call-update) | async-done | bytes 1179664 | tf_op jit(solution)/shard_map/reduce_scatter | solution.py:107
  276.8 0.0 reduce-scatter.5.cloned.1.call-update
  276.8 29.5 %reduce-scatter.5.cloned.1.call-done = bf16[48,3,16,128]{3,2,1,0:T(8,128)(2,1)} async-done(((bf16[96,3,16,128]{3,2,1,0:T(8,128)(2,1)}), bf16[48,3,16,128]{3,2,1,0:T(8,128)(2,1)}) %reduce-scatter.5.cloned.1.call-update) | async-done | bytes 589840 | tf_op jit(solution)/shard_map/reduce_scatter | solution.py:124
  306.4 1.2 copy.58
  307.5 1.1 convert_element_type.159
  (10 shorter events, 0.1 us)
Async XLA Ops:
  7.2 105.2 %copy-start = (bf16[256,256]{1,0:T(8,128)(2,1)S(1)}, bf16[256,256]{1,0:T(8,128)(2,1)}, u32[]{:S(2)}) copy-start(bf16[256,256]{1,0:T(8,128)(2,1)} %param.9) | copy-start | bytes 393220
  26.6 11.5 %copy-start.3 = (f32[2,2,128]{2,1,0:T(2,128)S(1)}, f32[2,2,128]{2,1,0:T(2,128)}, u32[]{:S(2)}) copy-start(f32[2,2,128]{2,1,0:T(2,128)} %param.8) | copy-start | bytes 6148
  30.0 78.9 %all-to-all-start = ((f32[8,2,3,256,128]{4,3,1,2,0:T(8,128)}), f32[8,2,3,256,128]{4,3,1,2,0:T(8,128)}, u32[]{:S(2)}, u32[]{:S(2)}) async-start(f32[8,2,3,256,128]{4,3,1,2,0:T(8,128)} %copy.41), calls=%async_computation | async-start | bytes 12582912 | tf_op jit(solution)/shard_map/all_to_all | solution.py:47
  38.1 109.9 %all-gather.2.cloned.1.call-start = ((), (), s32[]{:S(2)}) async-start(), calls=%async_computation.3 | async-start | bytes 3538944 | tf_op jit(solution)/shard_map/all_gather | solution.py:96
  116.6 160.2 %reduce-scatter.3.cloned.1.call-start = ((), (), s32[]{:S(2)}) async-start(), calls=%async_computation.4 | async-start | bytes 10616832 | tf_op jit(solution)/shard_map/reduce_scatter | solution.py:107
  169.5 18.7 %copy-start.1 = (bf16[256,768]{1,0:T(8,128)(2,1)S(1)}, bf16[256,768]{1,0:T(8,128)(2,1)}, u32[]{:S(2)}) copy-start(bf16[256,768]{1,0:T(8,128)(2,1)} %param.5) | copy-start | bytes 1179652
  169.5 18.7 %copy-start.2 = (f32[768]{0:T(1024)S(1)}, f32[768]{0:T(1024)}, u32[]{:S(2)}) copy-start(f32[768]{0:T(1024)} %param.6) | copy-start | bytes 9220
  169.5 136.9 %reduce-scatter.5.cloned.1.call-start = ((), (), s32[]{:S(2)}) async-start(), calls=%async_computation.5 | async-start | bytes 1769472 | tf_op jit(solution)/shard_map/reduce_scatter | solution.py:124
  176.9 11.3 %collective-permute-start = (bf16[256,768]{1,0:T(8,128)(2,1)S(1)}, bf16[256,768]{1,0:T(8,128)(2,1)S(1)}, u32[]{:S(2)}, u32[]{:S(2)}) collective-permute-start(bf16[256,768]{1,0:T(8,128)(2,1)S(1)} %fusion.16), channel_id=1, source_target_pairs={{0,1},{1,0},{2,3},{3,2},{4,5},{5,4},{6,7},{7,6},{8,9},{9,8},{10,11... | collective-permute-start | bytes 1179656 | tf_op jit(solution)/shard_map/ppermute | solution.py:110
Sparse Core Ops, SparseCore 0:
  116.8 31.2 all-gather.1
  169.6 107.1 reduce-scatter.2
  279.3 26.9 reduce-scatter.4

commit v5 on v4

--- a/solution.py
+++ b/solution.py
@@ -44,13 +44,12 @@
     weights = w_qkv.reshape(3, width_local, group_heads, head_size)
     n_mx = lax.axis_size("mx")
     partial = jnp.einsum("td,sdhe->hste", scaled, weights, preferred_element_type=jnp.float32)
-    pieces = lax.all_to_all(
-        partial.reshape(n_mx, local_heads, 3, token_rows, head_size),
-        "mx",
-        split_axis=0,
-        concat_axis=0,
-    )
-    projected = jnp.sum(pieces, axis=0).astype(jnp.bfloat16)
+    partial = partial.reshape(n_mx, local_heads, 3, token_rows, head_size)
+    qk_pieces = lax.all_to_all(partial[:, :, :2], "mx", split_axis=0, concat_axis=0)
+    v_pieces = lax.all_to_all(partial[:, :, 2:].astype(jnp.bfloat16), "mx", split_axis=0, concat_axis=0)
+    projected = jnp.concatenate(
+        [jnp.sum(qk_pieces, axis=0), jnp.sum(v_pieces.astype(jnp.float32), axis=0)], axis=1
+    ).astype(jnp.bfloat16)
     images = token_rows // PATCH
     shaped = projected.reshape(local_heads, 3, images, PATCH, head_size)
     q_hat, q_inv = head_norm(shaped[:, 0].astype(jnp.float32))

time: 316 us -> 311 us (0.984)
  waiting for transfers between devices: 171 us -> 158 us
  local copies, waits for them, and re-layouts: 19 us -> 24.4 us
  starting transfers between devices: 9.75 us -> 14.5 us
    all_to_all x1 -> x2, waiting for transfers between devices: 70.8 us -> 57.7 us  [the longest x1 47.9 us: body(): lax.all_to_all(partial[:, :, :2], 'mx', split_axis=0, concat_axis=0)]
    unnamed x8 -> x12, local copies, waits for them, and re-layouts: 0.03 us -> 5.97 us
    all_to_all x1 -> x2, starting transfers between devices: 8.09 us -> 12.8 us  [the longest x1 6.94 us: body(): lax.all_to_all(partial[:, :, 2:].astype(jnp.bfloat16), 'mx', split_axis=0...]
    reshape x1 -> x0, local copies, waits for them, and re-layouts: 3.36 us -> none  [body(): partial.reshape(n_mx, local_heads, 3, token_rows, head_size)]
  transfers between devices with their start and end apart: 5 -> 6, of which waited for: 5 -> 6; matrix products, arithmetic and copies ran while one was open for 3% -> 5% of each run, Pallas kernels for 0% -> 0%
where the time goes in v5:
time: 311 us; the launch traced here: 310 us
  waiting for transfers between devices  158 us (51%)
  blocking collectives  69.2 us (22%)
  local copies, waits for them, and re-layouts  24.4 us (8%)
  matrix products  22.6 us (7%)
  starting transfers between devices  14.5 us (5%)
  between operations  13.9 us (4%)
  other arithmetic  7.71 us (2%)
    all_to_all x1, waiting for transfers between devices, body(): lax.all_to_all(partial[:, :, :2], 'mx', split_axis=0, concat_axis=0)  47.9 us
    psum x1, blocking collectives, body(): lax.psum((head_gain_part, feature_part), ('dph', 'dpz'))  45.9 us
    all_gather x1, waiting for transfers between devices, body(): gathered = lax.all_gather(stacked, 'mx', axis=0, tiled=True)  31.1 us
    reduce_scatter x1, waiting for transfers between devices, body(): w_half = lax.psum_scatter(w_part, 'dpz', scatter_dimension=0, tiled=True)  29.5 us
    reduce_scatter x1, waiting for transfers between devices, body(): lax.psum_scatter(w_half, 'dph', scatter_dimension=0, tiled=True)  29.5 us
    convert_element_type x1, local copies, waits for them, and re-layouts, body(): w_part = jnp.einsum('td,hste->dshe', feature_part, gathered, preferred_el...  13.2 us
    psum x1, blocking collectives, body(): lax.psum((jnp.sum(widened, axis=1), jnp.sum(widened * widened, axis=1)),...  11.7 us
    psum x1, blocking collectives, body(): lax.psum((jnp.sum(d_hat, axis=1), jnp.sum(d_hat * normed, axis=1)), 'mx')  11.6 us
  transfers between devices with their start and end apart: 6, of which 6 were waited for; matrix products, arithmetic and copies ran while one was open for 5% of the time, Pallas kernels for 0%

profile of v5, /device:TPU:2, one launch (start us, length us, event | category | flops | bytes accessed | tf_op | source)
XLA Modules:
  0.0 310.0 jit_solution(3160204545140581381)
XLA Ops:
  7.2 0.0 copy-start
  7.2 1.3 convert_reduce_fusion
  8.4 11.7 %all-reduce.2 = (f32[256]{0:T(256)S(1)}, f32[256]{0:T(256)S(1)}) all-reduce(f32[256]{0:T(256)S(1)} %get-tuple-element.20, f32[256]{0:T(256)S(1)} %get-tuple-element.19), channel_id=1, replica_groups=mesh['dph'=2,'dpz'=8,'mx'=8,'my'=2] {'mx'}, use_global_device_ids=true, to_apply=%region_3.0 | all-reduce | flops 512 | bytes 4096 | tf_op jit(solution)/shard_map/psum | solution.py:35
  20.1 1.2 fusion.38
  21.3 5.3 %fusion.5 = f32[256,3,16,128]{3,0,2,1:T(8,128)S(1)} fusion(bf16[256,768]{1,0:T(8,128)(2,1)S(1)} %fusion.38, bf16[3,768,2048]{2,1,0:T(8,128)(2,1)} %param.7), kind=kOutput, calls=%fused_computation.5 | convolution fusion | flops 2415919104 | bytes 16121856 | tf_op jit(solution)/shard_map/td,sdhe->hste/dot_general | solution.py:46
  26.6 0.0 copy-start.2
  26.6 2.7 copy-done.2
  29.3 0.2 slice.31
  29.5 1.1 copy.99
  30.5 6.9 %all-to-all-start.1 = ((bf16[8,2,1,256,128]{4,3,1,2,0:T(8,128)(2,1)}), bf16[8,2,1,256,128]{4,3,1,2,0:T(8,128)(2,1)S(1)}, u32[]{:S(2)}, u32[]{:S(2)}) async-start(bf16[8,2,1,256,128]{4,3,1,2,0:T(8,128)(2,1)} %copy.99), calls=%async_computation.1 | async-start | bytes 2097152 | tf_op jit(solution)/shard_map/all_to_all | solution.py:49
  37.5 2.5 slice.28
  39.9 0.0 copy-start.4
  40.0 2.2 copy.65
  42.2 9.8 %all-to-all-done.1 = bf16[8,2,1,256,128]{4,3,1,2,0:T(8,128)(2,1)S(1)} async-done(((bf16[8,2,1,256,128]{4,3,1,2,0:T(8,128)(2,1)}), bf16[8,2,1,256,128]{4,3,1,2,0:T(8,128)(2,1)S(1)}, u32[]{:S(2)}, u32[]{:S(2)}) %all-to-all-start.1) | async-done | bytes 1048608 | tf_op jit(solution)/shard_map/all_to_all | solution.py:49
  52.0 5.9 %all-to-all-start = ((f32[8,2,2,256,128]{4,3,1,2,0:T(8,128)}), f32[8,2,2,256,128]{4,3,1,2,0:T(8,128)}, u32[]{:S(2)}, u32[]{:S(2)}) async-start(f32[8,2,2,256,128]{4,3,1,2,0:T(8,128)} %copy.65), calls=%async_computation | async-start | bytes 8388608 | tf_op jit(solution)/shard_map/all_to_all | solution.py:48
  57.9 0.0 all-gather.2.cloned.1.call-start
  57.9 0.0 copy-done.4
  57.9 0.1 reduce.27
  58.0 0.0 copy-done
  58.0 0.2 convolution_bitcast_fusion
  58.3 47.9 %all-to-all-done = f32[8,2,2,256,128]{4,3,1,2,0:T(8,128)} async-done(((f32[8,2,2,256,128]{4,3,1,2,0:T(8,128)}), f32[8,2,2,256,128]{4,3,1,2,0:T(8,128)}, u32[]{:S(2)}, u32[]{:S(2)}) %all-to-all-start) | async-done | bytes 4194336 | tf_op jit(solution)/shard_map/all_to_all | solution.py:48
  106.2 2.4 reduce_sum.173
  108.6 0.1 copy.37
  108.8 0.1 fusion.49
  108.9 0.5 fusion.104
  109.4 0.2 fusion.26
  109.6 0.4 fusion.27
  110.0 0.5 fusion.61
  110.6 0.2 fusion.79
  110.7 0.8 pad_maximum_fusion
  111.5 0.0 all-gather.2.cloned.1.call-update
  111.5 0.0 reduce-scatter.3.cloned.1.call-start
  111.6 0.2 copy.45
  111.8 31.1 %all-gather.2.cloned.1.call-done = bf16[16,3,256,128]{2,3,0,1:T(8,128)(2,1)} async-done(((bf16[2,3,256,128]{2,3,0,1:T(8,128)(2,1)}), bf16[16,3,256,128]{2,3,0,1:T(8,128)(2,1)}) %all-gather.2.cloned.1.call-update) | async-done | bytes 3145744 | tf_op jit(solution)/shard_map/all_gather | solution.py:95
  142.9 8.2 %convert_bitcast_fusion = bf16[768,3,16,128]{0,3,1,2:T(8,128)(2,1)} fusion(bf16[256,768,1,1]{0,1,3,2:T(8,128)(2,1)S(1)} %bitcast.160, bf16[16,3,256,128]{2,3,0,1:T(8,128)(2,1)} %all-gather.2.cloned.1.call-done), kind=kOutput, calls=%fused_computation.8 | convolution fusion | flops 2420637696 | bytes 12976128 | tf_op jit(solution)/shard_map/td,hste->dshe/dot_general | solution.py:103
  151.1 13.2 %copy.49 = bf16[768,3,16,128]{3,2,1,0:T(8,128)(2,1)} copy(bf16[768,3,16,128]{0,3,1,2:T(8,128)(2,1)} %convert_bitcast_fusion) | data formatting | bytes 18874368 | tf_op jit(solution)/shard_map/convert_element_type | solution.py:105
  164.3 0.0 reduce-scatter.3.cloned.1.call-update
  164.4 0.0 copy-start.1
  164.4 0.0 copy-start.3
  164.4 0.0 reduce-scatter.5.cloned.1.call-start
  164.4 7.3 %fusion.16 = bf16[256,768]{1,0:T(8,128)(2,1)S(1)} fusion(bf16[16,3,256,128]{2,3,0,1:T(8,128)(2,1)} %all-gather.2.cloned.1.call-done, bf16[3,768,2048]{2,1,0:T(8,128)(2,1)} %param.7), kind=kOutput, calls=%fused_computation.14 | convolution fusion | flops 2416115712 | bytes 12976128 | tf_op jit(solution)/shard_map/hste,sdhe->td/dot_general | solution.py:96
  171.8 1.6 collective-permute-start
  173.4 9.8 %collective-permute-done = bf16[256,768]{1,0:T(8,128)(2,1)S(1)} collective-permute-done((bf16[256,768]{1,0:T(8,128)(2,1)S(1)}, bf16[256,768]{1,0:T(8,128)(2,1)S(1)}, u32[]{:S(2)}, u32[]{:S(2)}) %collective-permute-start) | collective-permute-done | bytes 393248 | tf_op jit(solution)/shard_map/ppermute | solution.py:109
  183.1 0.0 copy-done.1
  183.1 0.0 copy-done.3
  183.1 0.4 fusion.44
  183.6 11.6 %all-reduce.1 = (f32[256]{0:T(256)S(1)}, f32[256]{0:T(256)S(1)}) all-reduce(f32[256]{0:T(256)S(1)} %get-tuple-element.13, f32[256]{0:T(256)S(1)} %get-tuple-element.14), channel_id=1, replica_groups=mesh['dph'=2,'dpz'=8,'mx'=8,'my'=2] {'mx'}, use_global_device_ids=true, to_apply=%region_21.0 | all-reduce | flops 512 | bytes 4096 | tf_op jit(solution)/shard_map/psum | solution.py:112
  195.2 45.9 %all-reduce = (f32[768]{0:T(1024)}, f32[2,2,128]{2,1,0:T(2,128)}) all-reduce(f32[768]{0:T(1024)S(1)} %get-tuple-element.12, f32[2,2,128]{2,1,0:T(2,128)S(1)} %pad_maximum_fusion.1), channel_id=1, replica_groups=mesh['dph'=2,'dpz'=8,'mx'=8,'my'=2] {'dph','dpz'}, use_global_device_ids=true, to_apply=%region_23.0 | all-reduce | flops 1280 | bytes 10240 | tf_op jit(solution)/shard_map/psum | solution.py:119
  241.1 1.1 fusion.43
  242.2 29.5 %reduce-scatter.3.cloned.1.call-done = bf16[96,3,16,128]{3,2,1,0:T(8,128)(2,1)} async-done(((bf16[768,3,16,128]{3,2,1,0:T(8,128)(2,1)}), bf16[96,3,16,128]{3,2,1,0:T(8,128)(2,1)}) %reduce-scatter.3.cloned.1.call-update) | async-done | bytes 1179664 | tf_op jit(solution)/shard_map/reduce_scatter | solution.py:106
  271.7 0.0 reduce-scatter.5.cloned.1.call-update
  271.7 29.5 %reduce-scatter.5.cloned.1.call-done = bf16[48,3,16,128]{3,2,1,0:T(8,128)(2,1)} async-done(((bf16[96,3,16,128]{3,2,1,0:T(8,128)(2,1)}), bf16[48,3,16,128]{3,2,1,0:T(8,128)(2,1)}) %reduce-scatter.5.cloned.1.call-update) | async-done | bytes 589840 | tf_op jit(solution)/shard_map/reduce_scatter | solution.py:123
  301.2 1.2 copy.52
  302.4 1.1 convert_element_type.157
  (10 shorter events, 0.1 us)
Async XLA Ops:
  7.2 50.9 %copy-start = (bf16[256,256]{1,0:T(8,128)(2,1)S(1)}, bf16[256,256]{1,0:T(8,128)(2,1)}, u32[]{:S(2)}) copy-start(bf16[256,256]{1,0:T(8,128)(2,1)} %param.9) | copy-start | bytes 393220
  26.6 2.7 copy-start.2
  30.5 21.4 %all-to-all-start.1 = ((bf16[8,2,1,256,128]{4,3,1,2,0:T(8,128)(2,1)}), bf16[8,2,1,256,128]{4,3,1,2,0:T(8,128)(2,1)S(1)}, u32[]{:S(2)}, u32[]{:S(2)}) async-start(bf16[8,2,1,256,128]{4,3,1,2,0:T(8,128)(2,1)} %copy.99), calls=%async_computation.1 | async-start | bytes 2097152 | tf_op jit(solution)/shard_map/all_to_all | solution.py:49
  39.9 17.9 %copy-start.4 = (f32[2,2,128]{2,1,0:T(2,128)S(1)}, f32[2,2,128]{2,1,0:T(2,128)}, u32[]{:S(2)}) copy-start(f32[2,2,128]{2,1,0:T(2,128)} %param.8) | copy-start | bytes 6148
  52.0 54.2 %all-to-all-start = ((f32[8,2,2,256,128]{4,3,1,2,0:T(8,128)}), f32[8,2,2,256,128]{4,3,1,2,0:T(8,128)}, u32[]{:S(2)}, u32[]{:S(2)}) async-start(f32[8,2,2,256,128]{4,3,1,2,0:T(8,128)} %copy.65), calls=%async_computation | async-start | bytes 8388608 | tf_op jit(solution)/shard_map/all_to_all | solution.py:48
  57.9 85.1 %all-gather.2.cloned.1.call-start = ((), (), s32[]{:S(2)}) async-start(), calls=%async_computation.4 | async-start | bytes 3538944 | tf_op jit(solution)/shard_map/all_gather | solution.py:95
  111.5 160.2 %reduce-scatter.3.cloned.1.call-start = ((), (), s32[]{:S(2)}) async-start(), calls=%async_computation.5 | async-start | bytes 10616832 | tf_op jit(solution)/shard_map/reduce_scatter | solution.py:106
  164.4 18.8 %copy-start.1 = (bf16[256,768]{1,0:T(8,128)(2,1)S(1)}, bf16[256,768]{1,0:T(8,128)(2,1)}, u32[]{:S(2)}) copy-start(bf16[256,768]{1,0:T(8,128)(2,1)} %param.5) | copy-start | bytes 1179652
  164.4 18.7 %copy-start.3 = (f32[768]{0:T(1024)S(1)}, f32[768]{0:T(1024)}, u32[]{:S(2)}) copy-start(f32[768]{0:T(1024)} %param.6) | copy-start | bytes 9220
  164.4 136.8 %reduce-scatter.5.cloned.1.call-start = ((), (), s32[]{:S(2)}) async-start(), calls=%async_computation.6 | async-start | bytes 1769472 | tf_op jit(solution)/shard_map/reduce_scatter | solution.py:123
  171.8 11.3 %collective-permute-start = (bf16[256,768]{1,0:T(8,128)(2,1)S(1)}, bf16[256,768]{1,0:T(8,128)(2,1)S(1)}, u32[]{:S(2)}, u32[]{:S(2)}) collective-permute-start(bf16[256,768]{1,0:T(8,128)(2,1)S(1)} %fusion.16), channel_id=1, source_target_pairs={{0,1},{1,0},{2,3},{3,2},{4,5},{5,4},{6,7},{7,6},{8,9},{9,8},{10,11... | collective-permute-start | bytes 1179656 | tf_op jit(solution)/shard_map/ppermute | solution.py:109
Sparse Core Ops, SparseCore 0:
  111.7 31.2 all-gather.1
  164.5 107.1 reduce-scatter.2
  274.2 26.9 reduce-scatter.4

commit v6 on v5

--- a/solution.py
+++ b/solution.py
@@ -97,12 +97,19 @@
     feature_part = scaled
     n_hi = lax.axis_size("dph")
     n_z = lax.axis_size("dpz")
-    feature_part = (
+    z_first = (
         feature_part.reshape(token_rows, n_hi, n_z, -1).transpose(0, 2, 1, 3).reshape(token_rows, -1)
     )
+    split = group_heads // 2
     w_part = jnp.einsum(
-        "td,hste->dshe", feature_part, gathered, preferred_element_type=jnp.float32
+        "td,hste->dshe", z_first, gathered[:split], preferred_element_type=jnp.float32
     ).astype(jnp.bfloat16)
+    w_other = jnp.einsum(
+        "td,hste->dshe", feature_part, gathered[split:], preferred_element_type=jnp.float32
+    ).astype(jnp.bfloat16)
+    hi_rows = w_other.reshape(n_hi, width_local // n_hi, 3, group_heads - split, head_size)
+    hi_index = lax.axis_index("dph")
+    swapped = lax.ppermute(hi_rows[1 - hi_index], "dph", [(0, 1), (1, 0)])
     w_half = lax.psum_scatter(w_part, "dpz", scatter_dimension=0, tiled=True)
     gain_row = ln_gain[None, :]
     d_low = d_scaled.astype(jnp.bfloat16)
@@ -117,10 +124,13 @@
     ).astype(jnp.bfloat16)
     feature_part = jnp.sum(d_rows * normed, axis=0)
     head_total, feature_total = lax.psum((head_gain_part, feature_part), ("dph", "dpz"))
-    w_half, result_rows, feature_total, head_total = lax.optimization_barrier(
-        (w_half, result_rows, feature_total, head_total)
+    w_half, swapped, result_rows, feature_total, head_total = lax.optimization_barrier(
+        (w_half, swapped, result_rows, feature_total, head_total)
     )
-    w_rows = lax.psum_scatter(w_half, "dph", scatter_dimension=0, tiled=True).astype(jnp.float32)
+    hi_sum = (hi_rows[hi_index].astype(jnp.float32) + swapped.astype(jnp.float32)).astype(jnp.bfloat16)
+    w_late = lax.psum_scatter(hi_sum, "dpz", scatter_dimension=0, tiled=True)
+    w_rows = lax.psum_scatter(w_half, "dph", scatter_dimension=0, tiled=True)
+    w_rows = jnp.concatenate([w_rows, w_late], axis=2).astype(jnp.float32)
     w_grad = (
         w_rows.reshape(block_rows, 3, group_heads * head_size)
         .transpose(1, 0, 2)

time: 311 us -> 363 us (1.17)
  waiting for transfers between devices: 158 us -> 202 us
  local copies, waits for them, and re-layouts: 24.4 us -> 30.5 us
  other arithmetic: 7.71 us -> 13.6 us
  blocking collectives: 69.2 us -> 65.2 us
    ppermute x1, waiting for transfers between devices: 9.76 us -> 53.3 us  [body(): d_other = lax.ppermute(d_low, 'my', [(0, 1), (1, 0)])]
    reduce_scatter x1 -> x2, waiting for transfers between devices: 29.5 us -> 59.5 us  [the longest x1 45.5 us: body(): w_late = lax.psum_scatter(hi_sum, 'dpz', scatter_dimension=0, tiled=True)]
    reduce_scatter x1, waiting for transfers between devices: 29.5 us -> 0.01 us  [body(): w_half = lax.psum_scatter(w_part, 'dpz', scatter_dimension=0, tiled=True)]
    convert_element_type x0 -> x1, other arithmetic: none -> 3.73 us  [body(): (hi_rows[hi_index].astype(jnp.float32) + swapped.astype(jnp.float32)).ast...]
    squeeze x0 -> x1, local copies, waits for them, and re-layouts: none -> 3.64 us  [body(): swapped = lax.ppermute(hi_rows[1 - hi_index], 'dph', [(0, 1), (1, 0)])]
    dot_general x1 -> x2, matrix products: 8.19 us -> 7.22 us  [the longest x1 3.63 us: body(): jnp.einsum('td,hste->dshe', feature_part, gathered[split:], preferred_ele...]
    convert_element_type x1 -> x2, local copies, waits for them, and re-layouts: 13.2 us -> 13.8 us  [the longest x1 6.97 us: body(): w_other = jnp.einsum('td,hste->dshe', feature_part, gathered[split:], pre...]
  transfers between devices with their start and end apart: 6 -> 8, of which waited for: 6 -> 6; matrix products, arithmetic and copies ran while one was open for 5% -> 9% of each run, Pallas kernels for 0% -> 0%
where the time goes in v6:
time: 363 us
  waiting for transfers between devices  202 us (56%)
  blocking collectives  65.2 us (18%)
  local copies, waits for them, and re-layouts  30.5 us (8%)
  matrix products  20.9 us (6%)
  starting transfers between devices  16.6 us (5%)
  between operations  14 us (4%)
  other arithmetic  13.6 us (4%)
    ppermute x1, waiting for transfers between devices, body(): d_other = lax.ppermute(d_low, 'my', [(0, 1), (1, 0)])  53.3 us
    all_to_all x1, waiting for transfers between devices, body(): lax.all_to_all(partial[:, :, :2], 'mx', split_axis=0, concat_axis=0)  47.9 us
    reduce_scatter x1, waiting for transfers between devices, body(): w_late = lax.psum_scatter(hi_sum, 'dpz', scatter_dimension=0, tiled=True)  45.5 us
    psum x1, blocking collectives, body(): lax.psum((head_gain_part, feature_part), ('dph', 'dpz'))  42.5 us
    all_gather x1, waiting for transfers between devices, body(): gathered = lax.all_gather(stacked, 'mx', axis=0, tiled=True)  31.1 us
    reduce_scatter x1, waiting for transfers between devices, body(): w_rows = lax.psum_scatter(w_half, 'dph', scatter_dimension=0, tiled=True)  14 us
    psum x1, blocking collectives, body(): lax.psum((jnp.sum(widened, axis=1), jnp.sum(widened * widened, axis=1)),...  11.7 us
    psum x1, blocking collectives, body(): lax.psum((jnp.sum(d_hat, axis=1), jnp.sum(d_hat * normed, axis=1)), 'mx')  11.1 us
  transfers between devices with their start and end apart: 8, of which 6 were waited for; matrix products, arithmetic and copies ran while one was open for 9% of the time, Pallas kernels for 0%

profile of v6, /device:TPU:2, one launch (start us, length us, event | category | flops | bytes accessed | tf_op | source)
XLA Modules:
  0.0 362.6 jit_solution(1474456172276335444)
XLA Ops:
  7.2 0.0 copy-start
  7.2 1.3 convert_reduce_fusion
  8.4 11.7 %all-reduce.2 = (f32[256]{0:T(256)S(1)}, f32[256]{0:T(256)S(1)}) all-reduce(f32[256]{0:T(256)S(1)} %get-tuple-element.22, f32[256]{0:T(256)S(1)} %get-tuple-element.21), channel_id=1, replica_groups=mesh['dph'=2,'dpz'=8,'mx'=8,'my'=2] {'mx'}, use_global_device_ids=true, to_apply=%region_3.0 | all-reduce | flops 512 | bytes 4096 | tf_op jit(solution)/shard_map/psum | solution.py:35
  20.1 1.2 fusion.40
  21.3 5.3 %fusion.5 = f32[256,3,16,128]{3,0,2,1:T(8,128)S(1)} fusion(bf16[256,768]{1,0:T(8,128)(2,1)S(1)} %fusion.40, bf16[3,768,2048]{2,1,0:T(8,128)(2,1)} %param.7), kind=kOutput, calls=%fused_computation.5 | convolution fusion | flops 2415919104 | bytes 16121856 | tf_op jit(solution)/shard_map/td,sdhe->hste/dot_general | solution.py:46
  26.6 0.0 copy-start.3
  26.6 2.7 copy-done.3
  29.3 0.2 slice.39
  29.5 1.1 copy.108
  30.5 6.9 %all-to-all-start.1 = ((bf16[8,2,1,256,128]{4,3,1,2,0:T(8,128)(2,1)}), bf16[8,2,1,256,128]{4,3,1,2,0:T(8,128)(2,1)S(1)}, u32[]{:S(2)}, u32[]{:S(2)}) async-start(bf16[8,2,1,256,128]{4,3,1,2,0:T(8,128)(2,1)} %copy.108), calls=%async_computation.1 | async-start | bytes 2097152 | tf_op jit(solution)/shard_map/all_to_all | solution.py:49
  37.5 2.5 slice.36
  39.9 2.2 copy.72
  42.2 9.8 %all-to-all-done.1 = bf16[8,2,1,256,128]{4,3,1,2,0:T(8,128)(2,1)S(1)} async-done(((bf16[8,2,1,256,128]{4,3,1,2,0:T(8,128)(2,1)}), bf16[8,2,1,256,128]{4,3,1,2,0:T(8,128)(2,1)S(1)}, u32[]{:S(2)}, u32[]{:S(2)}) %all-to-all-start.1) | async-done | bytes 1048608 | tf_op jit(solution)/shard_map/all_to_all | solution.py:49
  52.0 5.9 %all-to-all-start = ((f32[8,2,2,256,128]{4,3,1,2,0:T(8,128)}), f32[8,2,2,256,128]{4,3,1,2,0:T(8,128)}, u32[]{:S(2)}, u32[]{:S(2)}) async-start(f32[8,2,2,256,128]{4,3,1,2,0:T(8,128)} %copy.72), calls=%async_computation | async-start | bytes 8388608 | tf_op jit(solution)/shard_map/all_to_all | solution.py:48
  57.9 0.0 all-gather.2.cloned.1.call-start
  57.9 0.0 copy-done.7
  57.9 0.1 reduce.27
  58.0 0.0 copy-done
  58.0 0.2 convolution_bitcast_fusion
  58.3 47.9 %all-to-all-done = f32[8,2,2,256,128]{4,3,1,2,0:T(8,128)} async-done(((f32[8,2,2,256,128]{4,3,1,2,0:T(8,128)}), f32[8,2,2,256,128]{4,3,1,2,0:T(8,128)}, u32[]{:S(2)}, u32[]{:S(2)}) %all-to-all-start) | async-done | bytes 4194336 | tf_op jit(solution)/shard_map/all_to_all | solution.py:48
  106.2 2.4 reduce_sum.173
  108.6 0.1 copy.42
  108.8 0.1 fusion.52
  108.9 0.5 fusion.108
  109.4 0.2 fusion.28
  109.6 0.4 fusion.29
  110.0 0.5 fusion.64
  110.6 0.2 fusion.82
  110.7 0.8 pad_maximum_fusion.1
  111.5 0.0 all-gather.2.cloned.1.call-update
  111.6 0.0 reduce-scatter.4.cloned.1.call-start
  111.6 0.2 copy.50
  111.8 31.1 %all-gather.2.cloned.1.call-done = bf16[16,3,256,128]{2,3,0,1:T(8,128)(2,1)} async-done(((bf16[2,3,256,128]{2,3,0,1:T(8,128)(2,1)}), bf16[16,3,256,128]{2,3,0,1:T(8,128)(2,1)}) %all-gather.2.cloned.1.call-update) | async-done | bytes 3145744 | tf_op jit(solution)/shard_map/all_gather | solution.py:95
  142.9 2.2 fusion.107
  145.1 3.6 convert_bitcast_fusion.1
  148.7 6.9 %copy.54 = bf16[768,3,8,128]{3,2,1,0:T(8,128)(2,1)} copy(bf16[768,3,8,128]{0,3,1,2:T(8,128)(2,1)} %convert_bitcast_fusion.1) | data formatting | bytes 9437184 | tf_op jit(solution)/shard_map/convert_element_type | solution.py:106
  155.6 0.0 reduce-scatter.4.cloned.1.call-update
  155.6 0.0 reduce-scatter.6.cloned.1.call-start
  155.7 3.6 %convert_bitcast_fusion = bf16[768,3,8,128]{0,3,1,2:T(8,128)(2,1)} fusion(bf16[8,3,256,128]{2,3,0,1:T(8,128)(2,1)S(1)} %get-tuple-element.38, bf16[256,768]{1,0:T(8,128)(2,1)S(1)} %fusion.40), kind=kOutput, calls=%fused_computation.10 | convolution fusion | flops 1210318848 | bytes 6684672 | tf_op jit(solution)/shard_map/td,hste->dshe/dot_general | solution.py:107
  159.3 7.0 %copy.56 = bf16[768,3,8,128]{3,2,1,0:T(8,128)(2,1)} copy(bf16[768,3,8,128]{0,3,1,2:T(8,128)(2,1)} %convert_bitcast_fusion) | data formatting | bytes 9437184 | tf_op jit(solution)/shard_map/convert_element_type | solution.py:109
  166.3 3.6 %dynamic-slice_bitcast_fusion = bf16[384,3,8,128]{3,2,1,0:T(8,128)(2,1)} fusion(bf16[2,384,3,8,128]{4,3,2,1,0:T(8,128)(2,1)} %bitcast.163, s32[]{:T(128)S(6)} %select_n.6), kind=kLoop, calls=%fused_computation.13 | loop fusion | bytes 4718596 | tf_op jit(solution)/shard_map/squeeze | solution.py:112
  169.9 3.0 collective-permute-start
  172.9 0.0 copy-done.4
  172.9 6.6 %fusion.18 = bf16[256,768]{1,0:T(8,128)(2,1)S(1)} fusion(bf16[16,3,256,128]{2,3,0,1:T(8,128)(2,1)S(1)} %copy-done.4, bf16[3,768,2048]{2,1,0:T(8,128)(2,1)} %param.7), kind=kOutput, calls=%fused_computation.19 | convolution fusion | flops 2416115712 | bytes 12976128 | tf_op jit(solution)/shard_map/hste,sdhe->td/dot_general | solution.py:96
  179.5 0.7 collective-permute-start.1
  180.2 53.3 %collective-permute-done.1 = bf16[256,768]{1,0:T(8,128)(2,1)S(1)} collective-permute-done((bf16[256,768]{1,0:T(8,128)(2,1)S(1)}, bf16[256,768]{1,0:T(8,128)(2,1)S(1)}, u32[]{:S(2)}, u32[]{:S(2)}) %collective-permute-start.1) | collective-permute-done | bytes 393248 | tf_op jit(solution)/shard_map/ppermute | solution.py:116
  233.5 0.7 copy-done.5
  234.3 0.0 copy-done.2
  234.3 0.0 copy-done.6
  234.3 0.4 fusion.46
  234.7 11.1 %all-reduce.1 = (f32[256]{0:T(256)S(1)}, f32[256]{0:T(256)S(1)}) all-reduce(f32[256]{0:T(256)S(1)} %get-tuple-element.15, f32[256]{0:T(256)S(1)} %get-tuple-element.16), channel_id=1, replica_groups=mesh['dph'=2,'dpz'=8,'mx'=8,'my'=2] {'mx'}, use_global_device_ids=true, to_apply=%region_21.0 | all-reduce | flops 512 | bytes 4096 | tf_op jit(solution)/shard_map/psum | solution.py:119
  245.8 42.5 %all-reduce = (f32[768]{0:T(1024)}, f32[2,2,128]{2,1,0:T(2,128)}) all-reduce(f32[768]{0:T(1024)S(1)} %get-tuple-element.14, f32[2,2,128]{2,1,0:T(2,128)S(1)} %pad_maximum_fusion.2), channel_id=1, replica_groups=mesh['dph'=2,'dpz'=8,'mx'=8,'my'=2] {'dph','dpz'}, use_global_device_ids=true, to_apply=%region_23.0 | all-reduce | flops 1280 | bytes 10240 | tf_op jit(solution)/shard_map/psum | solution.py:126
  288.3 2.1 fusion.45
  290.4 0.0 collective-permute-done
  290.4 0.0 reduce-scatter.6.cloned.1.call-update
  290.4 0.0 reduce-scatter.8.cloned.1.call-start
  290.5 0.0 copy-start.1
  290.5 3.7 %fusion.8 = bf16[384,3,8,128]{3,2,1,0:T(8,128)(2,1)} fusion(bf16[384,3,8,128]{3,2,1,0:T(8,128)(2,1)S(1)} %collective-permute-done, bf16[2,384,3,8,128]{4,3,2,1,0:T(8,128)(2,1)} %bitcast.164, s32[]{:T(128)S(6)} %select_n.7), kind=kLoop, calls=%fused_computation.9 | loop fusion | flops 4718592 | bytes 7077892 | tf_op jit(solution)/shard_map/convert_element_type | solution.py:130
  294.2 0.0 reduce-scatter.8.cloned.1.call-update
  294.2 14.0 %reduce-scatter.6.cloned.1.call-done = bf16[48,3,8,128]{3,2,1,0:T(8,128)(2,1)} async-done(((bf16[96,3,8,128]{3,2,1,0:T(8,128)(2,1)}), bf16[48,3,8,128]{3,2,1,0:T(8,128)(2,1)}) %reduce-scatter.6.cloned.1.call-update) | async-done | bytes 294928 | tf_op jit(solution)/shard_map/reduce_scatter | solution.py:132
  308.2 45.5 %reduce-scatter.8.cloned.1.call-done = bf16[48,3,8,128]{3,2,1,0:T(8,128)(2,1)} async-done(((bf16[384,3,8,128]{3,2,1,0:T(8,128)(2,1)}), bf16[48,3,8,128]{3,2,1,0:T(8,128)(2,1)}) %reduce-scatter.8.cloned.1.call-update) | async-done | bytes 294928 | tf_op jit(solution)/shard_map/reduce_scatter | solution.py:131
  353.8 1.2 pad_maximum_fusion
  354.9 0.1 copy.59
  355.0 1.1 convert_element_type.183
  (17 shorter events, 0.1 us)
Async XLA Ops:
  7.2 50.9 %copy-start = (bf16[256,256]{1,0:T(8,128)(2,1)S(1)}, bf16[256,256]{1,0:T(8,128)(2,1)}, u32[]{:S(2)}) copy-start(bf16[256,256]{1,0:T(8,128)(2,1)} %param.9) | copy-start | bytes 393220
  26.6 2.7 copy-start.3
  30.5 21.4 %all-to-all-start.1 = ((bf16[8,2,1,256,128]{4,3,1,2,0:T(8,128)(2,1)}), bf16[8,2,1,256,128]{4,3,1,2,0:T(8,128)(2,1)S(1)}, u32[]{:S(2)}, u32[]{:S(2)}) async-start(bf16[8,2,1,256,128]{4,3,1,2,0:T(8,128)(2,1)} %copy.108), calls=%async_computation.1 | async-start | bytes 2097152 | tf_op jit(solution)/shard_map/all_to_all | solution.py:49
  42.2 15.7 %copy-start.7 = (f32[2,2,128]{2,1,0:T(2,128)S(1)}, f32[2,2,128]{2,1,0:T(2,128)}, u32[]{:S(2)}) copy-start(f32[2,2,128]{2,1,0:T(2,128)} %param.8) | copy-start | bytes 6148
  52.0 54.2 %all-to-all-start = ((f32[8,2,2,256,128]{4,3,1,2,0:T(8,128)}), f32[8,2,2,256,128]{4,3,1,2,0:T(8,128)}, u32[]{:S(2)}, u32[]{:S(2)}) async-start(f32[8,2,2,256,128]{4,3,1,2,0:T(8,128)} %copy.72), calls=%async_computation | async-start | bytes 8388608 | tf_op jit(solution)/shard_map/all_to_all | solution.py:48
  57.9 85.1 %all-gather.2.cloned.1.call-start = ((), (), s32[]{:S(2)}) async-start(), calls=%async_computation.5 | async-start | bytes 3538944 | tf_op jit(solution)/shard_map/all_gather | solution.py:95
  111.6 178.8 %reduce-scatter.4.cloned.1.call-start = ((), (), s32[]{:S(2)}) async-start(), calls=%async_computation.6 | async-start | bytes 5308416 | tf_op jit(solution)/shard_map/reduce_scatter | solution.py:113
  155.6 152.6 %reduce-scatter.6.cloned.1.call-start = ((), (), s32[]{:S(2)}) async-start(), calls=%async_computation.7 | async-start | bytes 884736 | tf_op jit(solution)/shard_map/reduce_scatter | solution.py:132
  166.3 6.7 %copy-start.4 = (bf16[16,3,256,128]{2,3,0,1:T(8,128)(2,1)S(1)}, bf16[16,3,256,128]{2,3,0,1:T(8,128)(2,1)}, u32[]{:S(2)}) copy-start(bf16[16,3,256,128]{2,3,0,1:T(8,128)(2,1)} %all-gather.2.cloned.1.call-done) | copy-start | bytes 9437188
  169.9 64.4 %copy-start.2 = (bf16[256,768]{1,0:T(8,128)(2,1)S(1)}, bf16[256,768]{1,0:T(8,128)(2,1)}, u32[]{:S(2)}) copy-start(bf16[256,768]{1,0:T(8,128)(2,1)} %param.5) | copy-start | bytes 1179652
  169.9 64.4 %copy-start.6 = (f32[768]{0:T(1024)S(1)}, f32[768]{0:T(1024)}, u32[]{:S(2)}) copy-start(f32[768]{0:T(1024)} %param.6) | copy-start | bytes 9220
  169.9 120.5 %collective-permute-start = (bf16[384,3,8,128]{3,2,1,0:T(8,128)(2,1)}, bf16[384,3,8,128]{3,2,1,0:T(8,128)(2,1)S(1)}, u32[]{:S(2)}, u32[]{:S(2)}) collective-permute-start(bf16[384,3,8,128]{3,2,1,0:T(8,128)(2,1)} %dynamic-slice_bitcast_fusion), channel_id=1, source_target_pairs={{0,128},{128,0},{1,129},{129,1},{2,130},{130,2},{3,131},{131,3},{4... | collective-permute-start | bytes 7077896 | tf_op jit(solution)/shard_map/ppermute | solution.py:112
  179.5 54.0 %collective-permute-start.1 = (bf16[256,768]{1,0:T(8,128)(2,1)S(1)}, bf16[256,768]{1,0:T(8,128)(2,1)S(1)}, u32[]{:S(2)}, u32[]{:S(2)}) collective-permute-start(bf16[256,768]{1,0:T(8,128)(2,1)S(1)} %fusion.18), channel_id=1, source_target_pairs={{0,1},{1,0},{2,3},{3,2},{4,5},{5,4},{6,7},{7,6},{8,9},{9,8},{10,11... | collective-permute-start | bytes 1179656 | tf_op jit(solution)/shard_map/ppermute | solution.py:116
  233.5 0.7 copy-start.5
  290.4 63.3 %reduce-scatter.8.cloned.1.call-start = ((), (), s32[]{:S(2)}) async-start(), calls=%async_computation.8 | async-start | bytes 2654208 | tf_op jit(solution)/shard_map/reduce_scatter | solution.py:131
  290.5 65.6 %copy-start.1 = (bf16[256,256]{1,0:T(8,128)(2,1)S(1)}, bf16[256,256]{1,0:T(8,128)(2,1)}, u32[]{:S(2)}) copy-start(bf16[256,256]{1,0:T(8,128)(2,1)} %param.9) | copy-start | bytes 393220
Sparse Core Ops, SparseCore 0:
  111.7 31.2 all-gather.1
  155.7 61.2 reduce-scatter.3
  290.5 17.6 reduce-scatter.5
  310.6 43.0 reduce-scatter.7

commit v7 on v2

--- a/solution.py
+++ b/solution.py
@@ -47,9 +47,9 @@
     n_c = lax.axis_size("mxc")
     ordered = w_qkv.reshape(3, width_local, n_x, n_c, local_heads, head_size)
     partial = jnp.einsum("td,sdabje->bajste", scaled, ordered, preferred_element_type=jnp.float32)
-    partial = partial.reshape(group_heads, 3, token_rows, head_size)
-    projected = lax.psum_scatter(partial, "mxc", scatter_dimension=0, tiled=True)
-    projected = lax.psum_scatter(projected, "mxx", scatter_dimension=0, tiled=True).astype(jnp.bfloat16)
+    on_chip = jnp.sum(lax.all_to_all(partial, "mxc", split_axis=0, concat_axis=0), axis=0)
+    projected = jnp.sum(lax.all_to_all(on_chip, "mxx", split_axis=0, concat_axis=0), axis=0)
+    projected = projected.astype(jnp.bfloat16)
     images = token_rows // PATCH
     shaped = projected.reshape(local_heads, 3, images, PATCH, head_size)
     q_hat, q_inv = head_norm(shaped[:, 0].astype(jnp.float32))
@@ -104,12 +104,6 @@
         "td,hste->dshe", feature_part, gathered, preferred_element_type=jnp.float32
     ).astype(jnp.bfloat16)
     w_half = lax.psum_scatter(w_part, "dpz", scatter_dimension=0, tiled=True)
-    w_rows = lax.psum_scatter(w_half, "dph", scatter_dimension=0, tiled=True).astype(jnp.float32)
-    w_grad = (
-        w_rows.reshape(block_rows, 3, group_heads * head_size)
-        .transpose(1, 0, 2)
-        .astype(jnp.bfloat16)
-    )
     gain_row = ln_gain[None, :]
     d_low = d_scaled.astype(jnp.bfloat16)
     d_other = lax.ppermute(d_low, "my", [(0, 1), (1, 0)])
@@ -123,6 +117,15 @@
     ).astype(jnp.bfloat16)
     feature_part = jnp.sum(d_rows * normed, axis=0)
     head_total, feature_total = lax.psum((head_gain_part, feature_part), ("dph", "dpz"))
+    w_half, result_rows, feature_total, head_total = lax.optimization_barrier(
+        (w_half, result_rows, feature_total, head_total)
+    )
+    w_rows = lax.psum_scatter(w_half, "dph", scatter_dimension=0, tiled=True).astype(jnp.float32)
+    w_grad = (
+        w_rows.reshape(block_rows, 3, group_heads * head_size)
+        .transpose(1, 0, 2)
+        .astype(jnp.bfloat16)
+    )
     return (result_rows, w_grad, feature_total, head_total)
 
 

time: 385 us -> 312 us (0.81)
  blocking collectives: 120 us -> 79.1 us
  waiting for transfers between devices: 173 us -> 137 us
  local copies, waits for them, and re-layouts: 44.1 us -> 35 us
  starting transfers between devices: 1.92 us -> 8.97 us
  other arithmetic: 4.72 us -> 10.3 us
    reduce_scatter x1, waiting for transfers between devices: 106 us -> 29.4 us  [body(): w_half = lax.psum_scatter(w_part, 'dpz', scatter_dimension=0, tiled=True)]
    unnamed x1 -> x0, blocking collectives: 58.1 us -> none
    all_to_all x0 -> x1, waiting for transfers between devices: none -> 36.7 us  [body(): lax.all_to_all(on_chip, 'mxx', split_axis=0, concat_axis=0)]
    reduce_scatter x1, waiting for transfers between devices: 0.01 us -> 29.5 us  [body(): lax.psum_scatter(w_half, 'dph', scatter_dimension=0, tiled=True)]
    unnamed x5 -> x3, waiting for transfers between devices: 22 us -> 0.05 us
    all_to_all x0 -> x1, blocking collectives: none -> 9.99 us  [body(): lax.all_to_all(partial, 'mxc', split_axis=0, concat_axis=0)]
    unnamed x21 -> x18, local copies, waits for them, and re-layouts: 10.7 us -> 0.79 us
    all_to_all x0 -> x1, starting transfers between devices: none -> 7.14 us  [body(): lax.all_to_all(on_chip, 'mxx', split_axis=0, concat_axis=0)]
  transfers between devices with their start and end apart: 5 -> 5, of which waited for: 4 -> 5; matrix products, arithmetic and copies ran while one was open for 3% -> 3% of each run, Pallas kernels for 0% -> 0%
where the time goes in v7:
time: 312 us; the launch traced here: 310 us
  waiting for transfers between devices  137 us (44%)
  blocking collectives  79.1 us (25%)
  local copies, waits for them, and re-layouts  35 us (11%)
  matrix products  26.1 us (8%)
  between operations  14 us (4%)
  other arithmetic  10.3 us (3%)
  starting transfers between devices  8.97 us (3%)
    psum x1, blocking collectives, body(): lax.psum((head_gain_part, feature_part), ('dph', 'dpz'))  45.9 us
    all_to_all x1, waiting for transfers between devices, body(): lax.all_to_all(on_chip, 'mxx', split_axis=0, concat_axis=0)  36.7 us
    all_gather x1, waiting for transfers between devices, body(): gathered = lax.all_gather(stacked, MX, axis=0, tiled=True)  31.2 us
    reduce_scatter x1, waiting for transfers between devices, body(): lax.psum_scatter(w_half, 'dph', scatter_dimension=0, tiled=True)  29.5 us
    reduce_scatter x1, waiting for transfers between devices, body(): w_half = lax.psum_scatter(w_part, 'dpz', scatter_dimension=0, tiled=True)  29.4 us
    reshape x1, local copies, waits for them, and re-layouts, body(): ordered = w_qkv.reshape(3, width_local, n_x, n_c, local_heads, head_size)  16 us
    convert_element_type x1, local copies, waits for them, and re-layouts, body(): w_part = jnp.einsum('td,hste->dshe', feature_part, gathered, preferred_el...  13.2 us
    psum x1, blocking collectives, body(): lax.psum((jnp.sum(widened, axis=1), jnp.sum(widened * widened, axis=1)), MX)  11.6 us
  transfers between devices with their start and end apart: 5, of which 5 were waited for; matrix products, arithmetic and copies ran while one was open for 3% of the time, Pallas kernels for 0%

profile of v7, /device:TPU:2, one launch (start us, length us, event | category | flops | bytes accessed | tf_op | source)
XLA Modules:
  0.0 310.1 jit_solution(9953603789232122918)
XLA Ops:
  7.2 0.0 copy-start
  7.2 1.3 convert_reduce_fusion
  8.4 0.0 copy-start.2
  8.5 0.0 copy-start.7
  8.5 16.0 %reshape.276 = bf16[3,768,4,2,2,128]{5,4,3,2,1,0:T(2,128)(2,1)} reshape(bf16[3,768,2048]{2,1,0:T(8,128)(2,1)} %param.7) | data formatting | bytes 18874368 | tf_op jit(solution)/shard_map/reshape | solution.py:48
  24.4 11.6 %all-reduce.2 = (f32[256]{0:T(256)S(1)}, f32[256]{0:T(256)S(1)}) all-reduce(f32[256]{0:T(256)S(1)} %get-tuple-element.26, f32[256]{0:T(256)S(1)} %get-tuple-element.25), channel_id=1, replica_groups=mesh['dph'=2,'dpz'=8,'mxx'=4,'mxc'=2,'my'=2] {'mxx','mxc'}, use_global_device_ids=true, to_apply=%region_3.0 | all-reduce | flops 512 | bytes 4096 | tf_op jit(solution)/shard_map/psum | solution.py:36
  36.1 0.0 copy-done.2
  36.1 0.0 copy-done.7
  36.1 0.2 fusion.40
  36.3 0.0 copy-start.5
  36.4 0.7 copy-done.5
  37.1 5.3 %fusion.9 = f32[2,4,2,3,256,128]{5,4,2,0,1,3:T(8,128)S(1)} fusion(bf16[3,768,4,2,2,128]{5,4,3,2,1,0:T(2,128)(2,1)} %reshape.276, bf16[256,768]{1,0:T(8,128)(2,1)S(1)} %fusion.40), kind=kOutput, calls=%fused_computation.10 | convolution fusion | flops 2415919104 | bytes 16121856 | tf_op jit(solution)/shard_map/td,sdabje->bajste/dot_general | solution.py:49
  42.3 0.7 copy.61
  43.1 10.0 %all_to_all.10 = f32[2,4,2,3,256,128]{5,4,2,1,3,0:T(8,128)} all-to-all(f32[2,4,2,3,256,128]{5,4,2,1,3,0:T(8,128)S(1)} %copy.61), channel_id=1, replica_groups=mesh['dph'=2,'dpz'=8,'mxx'=4,'mxc'=2,'my'=2] {'mxc'}, dimensions={0} | all-to-all | bytes 12582912 | tf_op jit(solution)/shard_map/all_to_all | solution.py:50
  53.0 3.5 %reduce_sum.173 = f32[4,2,3,256,128]{4,3,1,0,2:T(8,128)S(1)} reduce(f32[2,4,2,3,256,128]{5,4,2,1,3,0:T(8,128)} %all_to_all.10, f32[]{:T(128)} %constant.20.clone.1), dimensions={0}, to_apply=%region_4.0 | reduce | flops 786432 | bytes 9437188 | tf_op jit(solution)/shard_map/reduce_sum | solution.py:50
  56.6 0.0 copy-start.8
  56.6 1.9 copy.63
  58.5 7.1 %all-to-all-start.1 = ((f32[4,2,3,256,128]{4,3,1,2,0:T(8,128)}), f32[4,2,3,256,128]{4,3,1,2,0:T(8,128)S(1)}, u32[]{:S(2)}, u32[]{:S(2)}) async-start(f32[4,2,3,256,128]{4,3,1,2,0:T(8,128)} %copy.63), calls=%async_computation.1 | async-start | bytes 6291456 | tf_op jit(solution)/shard_map/all_to_all | solution.py:51
  65.6 0.0 all-gather.2.cloned.1.call-start
  65.6 0.0 copy-done.8
  65.6 36.7 %all-to-all-done.1 = f32[4,2,3,256,128]{4,3,1,2,0:T(8,128)S(1)} async-done(((f32[4,2,3,256,128]{4,3,1,2,0:T(8,128)}), f32[4,2,3,256,128]{4,3,1,2,0:T(8,128)S(1)}, u32[]{:S(2)}, u32[]{:S(2)}) %all-to-all-start.1) | async-done | bytes 3145760 | tf_op jit(solution)/shard_map/all_to_all | solution.py:51
  102.3 1.0 reduce_sum.174
  103.3 0.0 copy-start.4
  103.3 1.3 fusion.51
  104.6 0.0 copy-done
  104.6 1.1 convolution_bitcast_fusion
  105.8 0.0 copy-start.6
  105.8 1.6 fusion.106
  107.4 0.2 fusion.28
  107.6 1.3 fusion.29
  109.0 0.0 copy-done.4
  109.0 1.1 fusion.63
  110.1 0.6 fusion.81
  110.7 0.8 pad_maximum_fusion
  111.5 0.0 all-gather.2.cloned.1.call-update
  111.5 0.0 reduce-scatter.3.cloned.1.call-start
  111.6 0.0 copy-done.6
  111.6 0.2 copy.71
  111.8 31.2 %all-gather.2.cloned.1.call-done = bf16[16,3,256,128]{3,2,0,1:T(8,128)(2,1)} async-done(((bf16[2,3,256,128]{3,2,0,1:T(8,128)(2,1)}), bf16[16,3,256,128]{3,2,0,1:T(8,128)(2,1)}) %all-gather.2.cloned.1.call-update) | async-done | bytes 3145744 | tf_op jit(solution)/shard_map/all_gather | solution.py:95
  143.0 8.2 %convert_bitcast_fusion = bf16[768,3,16,128]{0,3,1,2:T(8,128)(2,1)} fusion(bf16[256,768,1,1]{0,1,3,2:T(8,128)(2,1)S(1)} %bitcast.153, bf16[16,3,256,128]{3,2,0,1:T(8,128)(2,1)} %all-gather.2.cloned.1.call-done), kind=kOutput, calls=%fused_computation.7 | convolution fusion | flops 2420637696 | bytes 12976128 | tf_op jit(solution)/shard_map/td,hste->dshe/dot_general | solution.py:103
  151.2 13.2 %copy.75 = bf16[768,3,16,128]{3,2,1,0:T(8,128)(2,1)} copy(bf16[768,3,16,128]{0,3,1,2:T(8,128)(2,1)} %convert_bitcast_fusion) | data formatting | bytes 18874368 | tf_op jit(solution)/shard_map/convert_element_type | solution.py:105
  164.4 0.0 reduce-scatter.3.cloned.1.call-update
  164.4 0.0 copy-start.3
  164.4 0.2 reduce-scatter.5.cloned.1.call-start
  164.7 0.0 copy-start.1
  164.7 7.3 %fusion.18 = bf16[256,768]{1,0:T(8,128)(2,1)S(1)} fusion(bf16[16,3,256,128]{3,2,0,1:T(8,128)(2,1)} %all-gather.2.cloned.1.call-done, bf16[3,768,2048]{2,1,0:T(8,128)(2,1)} %param.7), kind=kOutput, calls=%fused_computation.13 | convolution fusion | flops 2416115712 | bytes 12976128 | tf_op jit(solution)/shard_map/hste,sdhe->td/dot_general | solution.py:96
  172.0 1.6 collective-permute-start
  173.6 9.8 %collective-permute-done = bf16[256,768]{1,0:T(8,128)(2,1)S(1)} collective-permute-done((bf16[256,768]{1,0:T(8,128)(2,1)S(1)}, bf16[256,768]{1,0:T(8,128)(2,1)S(1)}, u32[]{:S(2)}, u32[]{:S(2)}) %collective-permute-start) | collective-permute-done | bytes 393248 | tf_op jit(solution)/shard_map/ppermute | solution.py:109
  183.3 0.0 copy-done.3
  183.3 0.4 fusion.46
  183.8 11.6 %all-reduce.1 = (f32[256]{0:T(256)S(1)}, f32[256]{0:T(256)S(1)}) all-reduce(f32[256]{0:T(256)S(1)} %get-tuple-element.13, f32[256]{0:T(256)S(1)} %get-tuple-element.14), channel_id=1, replica_groups=mesh['dph'=2,'dpz'=8,'mxx'=4,'mxc'=2,'my'=2] {'mxx','mxc'}, use_global_device_ids=true, to_apply=%region_21.0 | all-reduce | flops 512 | bytes 4096 | tf_op jit(solution)/shard_map/psum | solution.py:112
  195.4 45.9 %all-reduce = (f32[768]{0:T(1024)}, f32[2,2,128]{2,1,0:T(2,128)}) all-reduce(f32[768]{0:T(1024)S(1)} %get-tuple-element.12, f32[2,2,128]{2,1,0:T(2,128)S(1)} %pad_maximum_fusion.1), channel_id=1, replica_groups=mesh['dph'=2,'dpz'=8,'mxx'=4,'mxc'=2,'my'=2] {'dph','dpz'}, use_global_device_ids=true, to_apply=%region_23.0 | all-reduce | flops 1280 | bytes 10240 | tf_op jit(solution)/shard_map/psum | solution.py:119
  241.3 1.1 fusion.45
  242.4 29.4 %reduce-scatter.3.cloned.1.call-done = bf16[96,3,16,128]{3,2,1,0:T(8,128)(2,1)} async-done(((bf16[768,3,16,128]{3,2,1,0:T(8,128)(2,1)}), bf16[96,3,16,128]{3,2,1,0:T(8,128)(2,1)}) %reduce-scatter.3.cloned.1.call-update) | async-done | bytes 1179664 | tf_op jit(solution)/shard_map/reduce_scatter | solution.py:106
  271.8 0.0 reduce-scatter.5.cloned.1.call-update
  271.8 29.5 %reduce-scatter.5.cloned.1.call-done = bf16[48,3,16,128]{3,2,1,0:T(8,128)(2,1)} async-done(((bf16[96,3,16,128]{3,2,1,0:T(8,128)(2,1)}), bf16[48,3,16,128]{3,2,1,0:T(8,128)(2,1)}) %reduce-scatter.5.cloned.1.call-update) | async-done | bytes 589840 | tf_op jit(solution)/shard_map/reduce_scatter | solution.py:123
  301.3 1.2 copy.80
  302.5 1.1 convert_element_type.159
  303.5 0.0 copy-done.1
  (10 shorter events, 0.1 us)
Async XLA Ops:
  7.2 97.5 %copy-start = (bf16[256,256]{1,0:T(8,128)(2,1)S(1)}, bf16[256,256]{1,0:T(8,128)(2,1)}, u32[]{:S(2)}) copy-start(bf16[256,256]{1,0:T(8,128)(2,1)} %param.9) | copy-start | bytes 393220
  8.4 27.7 %copy-start.2 = (bf16[256,768]{1,0:T(8,128)(2,1)S(1)}, bf16[256,768]{1,0:T(8,128)(2,1)}, u32[]{:S(2)}) copy-start(bf16[256,768]{1,0:T(8,128)(2,1)} %param.5) | copy-start | bytes 1179652
  8.5 27.7 %copy-start.7 = (f32[768]{0:T(1024)S(1)}, f32[768]{0:T(1024)}, u32[]{:S(2)}) copy-start(f32[768]{0:T(1024)} %param.6) | copy-start | bytes 9220
  36.3 0.7 copy-start.5
  56.6 9.0 %copy-start.8 = (f32[2,2,128]{2,1,0:T(2,128)S(1)}, f32[2,2,128]{2,1,0:T(2,128)}, u32[]{:S(2)}) copy-start(f32[2,2,128]{2,1,0:T(2,128)} %param.8) | copy-start | bytes 6148
  58.5 43.8 %all-to-all-start.1 = ((f32[4,2,3,256,128]{4,3,1,2,0:T(8,128)}), f32[4,2,3,256,128]{4,3,1,2,0:T(8,128)S(1)}, u32[]{:S(2)}, u32[]{:S(2)}) async-start(f32[4,2,3,256,128]{4,3,1,2,0:T(8,128)} %copy.63), calls=%async_computation.1 | async-start | bytes 6291456 | tf_op jit(solution)/shard_map/all_to_all | solution.py:51
  65.6 77.3 %all-gather.2.cloned.1.call-start = ((), (), s32[]{:S(2)}) async-start(), calls=%async_computation.4 | async-start | bytes 3538944 | tf_op jit(solution)/shard_map/all_gather | solution.py:95
  103.3 5.7 %copy-start.4 = (bf16[2,3,256,128]{3,2,0,1:T(8,128)(2,1)S(1)}, bf16[2,3,256,128]{3,2,0,1:T(8,128)(2,1)}, u32[]{:S(2)}) copy-start(bf16[2,3,256,128]{3,2,0,1:T(8,128)(2,1)} %reduce_sum.174) | copy-start | bytes 1179652
  105.8 5.8 %copy-start.6 = (bf16[256,768]{1,0:T(8,128)(2,1)S(1)}, bf16[256,768]{1,0:T(8,128)(2,1)}, u32[]{:S(2)}) copy-start(bf16[256,768]{1,0:T(8,128)(2,1)} %copy-done.5) | copy-start | bytes 1179652
  111.5 160.2 %reduce-scatter.3.cloned.1.call-start = ((), (), s32[]{:S(2)}) async-start(), calls=%async_computation.5 | async-start | bytes 10616832 | tf_op jit(solution)/shard_map/reduce_scatter | solution.py:106
  164.4 18.9 %copy-start.3 = (bf16[256,768]{1,0:T(8,128)(2,1)S(1)}, bf16[256,768]{1,0:T(8,128)(2,1)}, u32[]{:S(2)}) copy-start(bf16[256,768]{1,0:T(8,128)(2,1)} %param.5) | copy-start | bytes 1179652
  164.4 136.9 %reduce-scatter.5.cloned.1.call-start = ((), (), s32[]{:S(2)}) async-start(), calls=%async_computation.6 | async-start | bytes 1769472 | tf_op jit(solution)/shard_map/reduce_scatter | solution.py:123
  164.7 138.9 %copy-start.1 = (bf16[256,256]{1,0:T(8,128)(2,1)S(1)}, bf16[256,256]{1,0:T(8,128)(2,1)}, u32[]{:S(2)}) copy-start(bf16[256,256]{1,0:T(8,128)(2,1)} %param.9) | copy-start | bytes 393220
  172.0 11.3 %collective-permute-start = (bf16[256,768]{1,0:T(8,128)(2,1)S(1)}, bf16[256,768]{1,0:T(8,128)(2,1)S(1)}, u32[]{:S(2)}, u32[]{:S(2)}) collective-permute-start(bf16[256,768]{1,0:T(8,128)(2,1)S(1)} %fusion.18), channel_id=1, source_target_pairs={{0,1},{1,0},{2,3},{3,2},{4,5},{5,4},{6,7},{7,6},{8,9},{9,8},{10,11... | collective-permute-start | bytes 1179656 | tf_op jit(solution)/shard_map/ppermute | solution.py:109
Sparse Core Ops, SparseCore 0:
  111.7 31.2 all-gather.1
  164.5 107.1 reduce-scatter.2
  274.3 26.9 reduce-scatter.4

commit v8 on v7

--- a/solution.py
+++ b/solution.py
@@ -45,8 +45,8 @@
     weights = w_qkv.reshape(3, width_local, group_heads, head_size)
     n_x = lax.axis_size("mxx")
     n_c = lax.axis_size("mxc")
-    ordered = w_qkv.reshape(3, width_local, n_x, n_c, local_heads, head_size)
-    partial = jnp.einsum("td,sdabje->bajste", scaled, ordered, preferred_element_type=jnp.float32)
+    partial = jnp.einsum("td,sdhe->hste", scaled, weights, preferred_element_type=jnp.float32)
+    partial = partial.reshape(n_x, n_c, local_heads, 3, token_rows, head_size).transpose(1, 0, 2, 3, 4, 5)
     on_chip = jnp.sum(lax.all_to_all(partial, "mxc", split_axis=0, concat_axis=0), axis=0)
     projected = jnp.sum(lax.all_to_all(on_chip, "mxx", split_axis=0, concat_axis=0), axis=0)
     projected = projected.astype(jnp.bfloat16)

time: 312 us -> 297 us (0.952)
  local copies, waits for them, and re-layouts: 35 us -> 18.3 us
    reshape x1, local copies, waits for them, and re-layouts: 16 us -> 0.7 us  [body(): partial.reshape(n_x, n_c, local_heads, 3, token_rows, head_size)]
where the time goes in v8:
time: 297 us; the launch traced here: 295 us
  waiting for transfers between devices  137 us (46%)
  blocking collectives  79.2 us (27%)
  matrix products  27.2 us (9%)
  local copies, waits for them, and re-layouts  18.3 us (6%)
  between operations  13.9 us (5%)
  other arithmetic  11.4 us (4%)
  starting transfers between devices  8.97 us (3%)
    psum x1, blocking collectives, body(): lax.psum((head_gain_part, feature_part), ('dph', 'dpz'))  45.9 us
    all_to_all x1, waiting for transfers between devices, body(): lax.all_to_all(on_chip, 'mxx', split_axis=0, concat_axis=0)  36.7 us
    all_gather x1, waiting for transfers between devices, body(): gathered = lax.all_gather(stacked, MX, axis=0, tiled=True)  31.2 us
    reduce_scatter x1, waiting for transfers between devices, body(): lax.psum_scatter(w_half, 'dph', scatter_dimension=0, tiled=True)  29.5 us
    reduce_scatter x1, waiting for transfers between devices, body(): w_half = lax.psum_scatter(w_part, 'dpz', scatter_dimension=0, tiled=True)  29.4 us
    convert_element_type x1, local copies, waits for them, and re-layouts, body(): w_part = jnp.einsum('td,hste->dshe', feature_part, gathered, preferred_el...  13.2 us
    psum x1, blocking collectives, body(): lax.psum((jnp.sum(widened, axis=1), jnp.sum(widened * widened, axis=1)), MX)  11.7 us
    psum x1, blocking collectives, body(): lax.psum((jnp.sum(d_hat, axis=1), jnp.sum(d_hat * normed, axis=1)), MX)  11.6 us
  transfers between devices with their start and end apart: 5, of which 5 were waited for; matrix products, arithmetic and copies ran while one was open for 3% of the time, Pallas kernels for 0%

profile of v8, /device:TPU:2, one launch (start us, length us, event | category | flops | bytes accessed | tf_op | source)
XLA Modules:
  0.0 295.5 jit_solution(9349661465724672654)
XLA Ops:
  7.2 0.0 copy-start
  7.2 1.3 convert_reduce_fusion
  8.4 11.7 %all-reduce.2 = (f32[256]{0:T(256)S(1)}, f32[256]{0:T(256)S(1)}) all-reduce(f32[256]{0:T(256)S(1)} %get-tuple-element.26, f32[256]{0:T(256)S(1)} %get-tuple-element.25), channel_id=1, replica_groups=mesh['dph'=2,'dpz'=8,'mxx'=4,'mxc'=2,'my'=2] {'mxx','mxc'}, use_global_device_ids=true, to_apply=%region_3.0 | all-reduce | flops 512 | bytes 4096 | tf_op jit(solution)/shard_map/psum | solution.py:36
  20.1 1.2 fusion.38
  21.3 0.0 copy-start.3
  21.4 5.4 %fusion.5 = f32[256,3,16,128]{3,0,2,1:T(8,128)S(1)} fusion(bf16[256,768]{1,0:T(8,128)(2,1)S(1)} %fusion.38, bf16[3,768,2048]{2,1,0:T(8,128)(2,1)} %param.7), kind=kOutput, calls=%fused_computation.5 | convolution fusion | flops 2415919104 | bytes 16121856 | tf_op jit(solution)/shard_map/td,sdhe->hste/dot_general | solution.py:48
  26.8 0.0 copy-done.3
  26.8 0.7 copy.126
  27.5 10.0 %all_to_all.10 = f32[2,4,2,3,256,128]{5,4,2,1,3,0:T(8,128)} all-to-all(f32[2,4,2,3,256,128]{5,4,2,1,3,0:T(8,128)S(1)} %bitcast.158), channel_id=1, replica_groups=mesh['dph'=2,'dpz'=8,'mxx'=4,'mxc'=2,'my'=2] {'mxc'}, dimensions={0} | all-to-all | bytes 12582912 | tf_op jit(solution)/shard_map/all_to_all | solution.py:50
  37.5 0.0 copy-start.6
  37.5 3.5 %reduce_sum.173 = f32[4,2,3,256,128]{4,3,1,0,2:T(8,128)S(1)} reduce(f32[2,4,2,3,256,128]{5,4,2,1,3,0:T(8,128)} %all_to_all.10, f32[]{:T(128)} %constant.20.clone.1), dimensions={0}, to_apply=%region_4.0 | reduce | flops 786432 | bytes 9437188 | tf_op jit(solution)/shard_map/reduce_sum | solution.py:50
  41.0 1.9 copy.63
  42.9 7.1 %all-to-all-start.1 = ((f32[4,2,3,256,128]{4,3,1,2,0:T(8,128)}), f32[4,2,3,256,128]{4,3,1,2,0:T(8,128)S(1)}, u32[]{:S(2)}, u32[]{:S(2)}) async-start(f32[4,2,3,256,128]{4,3,1,2,0:T(8,128)} %copy.63), calls=%async_computation.1 | async-start | bytes 6291456 | tf_op jit(solution)/shard_map/all_to_all | solution.py:51
  50.0 0.0 all-gather.2.cloned.1.call-start
  50.0 0.0 copy-done.6
  50.0 36.7 %all-to-all-done.1 = f32[4,2,3,256,128]{4,3,1,2,0:T(8,128)S(1)} async-done(((f32[4,2,3,256,128]{4,3,1,2,0:T(8,128)}), f32[4,2,3,256,128]{4,3,1,2,0:T(8,128)S(1)}, u32[]{:S(2)}, u32[]{:S(2)}) %all-to-all-start.1) | async-done | bytes 3145760 | tf_op jit(solution)/shard_map/all_to_all | solution.py:51
  86.7 1.0 reduce_sum.174
  87.7 0.0 copy-start.2
  87.7 0.0 copy-start.4
  87.7 1.3 fusion.49
  89.1 0.0 copy-done
  89.1 1.1 convolution_bitcast_fusion
  90.2 1.6 fusion.104
  91.8 0.2 fusion.26
  92.0 1.3 fusion.27
  93.4 2.1 fusion.61
  95.5 0.0 copy-done.2
  95.5 0.6 fusion.79
  96.1 0.8 pad_maximum_fusion
  96.9 0.0 all-gather.2.cloned.1.call-update
  96.9 0.0 reduce-scatter.3.cloned.1.call-start
  97.0 0.0 copy-done.4
  97.0 0.2 copy.71
  97.2 31.2 %all-gather.2.cloned.1.call-done = bf16[16,3,256,128]{3,2,0,1:T(8,128)(2,1)} async-done(((bf16[2,3,256,128]{3,2,0,1:T(8,128)(2,1)}), bf16[16,3,256,128]{3,2,0,1:T(8,128)(2,1)}) %all-gather.2.cloned.1.call-update) | async-done | bytes 3145744 | tf_op jit(solution)/shard_map/all_gather | solution.py:95
  128.4 8.2 %convert_bitcast_fusion = bf16[768,3,16,128]{0,3,1,2:T(8,128)(2,1)} fusion(bf16[256,768,1,1]{0,1,3,2:T(8,128)(2,1)S(1)} %bitcast.166, bf16[16,3,256,128]{3,2,0,1:T(8,128)(2,1)} %all-gather.2.cloned.1.call-done), kind=kOutput, calls=%fused_computation.8 | convolution fusion | flops 2420637696 | bytes 12976128 | tf_op jit(solution)/shard_map/td,hste->dshe/dot_general | solution.py:103
  136.6 13.2 %copy.75 = bf16[768,3,16,128]{3,2,1,0:T(8,128)(2,1)} copy(bf16[768,3,16,128]{0,3,1,2:T(8,128)(2,1)} %convert_bitcast_fusion) | data formatting | bytes 18874368 | tf_op jit(solution)/shard_map/convert_element_type | solution.py:105
  149.8 0.0 reduce-scatter.3.cloned.1.call-update
  149.8 0.0 copy-start.1
  149.8 0.0 copy-start.5
  149.8 0.2 reduce-scatter.5.cloned.1.call-start
  150.1 7.3 %fusion.16 = bf16[256,768]{1,0:T(8,128)(2,1)S(1)} fusion(bf16[16,3,256,128]{3,2,0,1:T(8,128)(2,1)} %all-gather.2.cloned.1.call-done, bf16[3,768,2048]{2,1,0:T(8,128)(2,1)} %param.7), kind=kOutput, calls=%fused_computation.14 | convolution fusion | flops 2416115712 | bytes 12976128 | tf_op jit(solution)/shard_map/hste,sdhe->td/dot_general | solution.py:96
  157.3 1.6 collective-permute-start
  158.9 9.8 %collective-permute-done = bf16[256,768]{1,0:T(8,128)(2,1)S(1)} collective-permute-done((bf16[256,768]{1,0:T(8,128)(2,1)S(1)}, bf16[256,768]{1,0:T(8,128)(2,1)S(1)}, u32[]{:S(2)}, u32[]{:S(2)}) %collective-permute-start) | collective-permute-done | bytes 393248 | tf_op jit(solution)/shard_map/ppermute | solution.py:109
  168.7 0.0 copy-done.1
  168.7 0.0 copy-done.5
  168.7 0.4 fusion.44
  169.1 11.6 %all-reduce.1 = (f32[256]{0:T(256)S(1)}, f32[256]{0:T(256)S(1)}) all-reduce(f32[256]{0:T(256)S(1)} %get-tuple-element.13, f32[256]{0:T(256)S(1)} %get-tuple-element.14), channel_id=1, replica_groups=mesh['dph'=2,'dpz'=8,'mxx'=4,'mxc'=2,'my'=2] {'mxx','mxc'}, use_global_device_ids=true, to_apply=%region_21.0 | all-reduce | flops 512 | bytes 4096 | tf_op jit(solution)/shard_map/psum | solution.py:112
  180.8 45.9 %all-reduce = (f32[768]{0:T(1024)}, f32[2,2,128]{2,1,0:T(2,128)}) all-reduce(f32[768]{0:T(1024)S(1)} %get-tuple-element.12, f32[2,2,128]{2,1,0:T(2,128)S(1)} %pad_maximum_fusion.1), channel_id=1, replica_groups=mesh['dph'=2,'dpz'=8,'mxx'=4,'mxc'=2,'my'=2] {'dph','dpz'}, use_global_device_ids=true, to_apply=%region_23.0 | all-reduce | flops 1280 | bytes 10240 | tf_op jit(solution)/shard_map/psum | solution.py:119
  226.7 1.1 fusion.43
  227.8 29.4 %reduce-scatter.3.cloned.1.call-done = bf16[96,3,16,128]{3,2,1,0:T(8,128)(2,1)} async-done(((bf16[768,3,16,128]{3,2,1,0:T(8,128)(2,1)}), bf16[96,3,16,128]{3,2,1,0:T(8,128)(2,1)}) %reduce-scatter.3.cloned.1.call-update) | async-done | bytes 1179664 | tf_op jit(solution)/shard_map/reduce_scatter | solution.py:106
  257.2 0.0 reduce-scatter.5.cloned.1.call-update
  257.2 29.5 %reduce-scatter.5.cloned.1.call-done = bf16[48,3,16,128]{3,2,1,0:T(8,128)(2,1)} async-done(((bf16[96,3,16,128]{3,2,1,0:T(8,128)(2,1)}), bf16[48,3,16,128]{3,2,1,0:T(8,128)(2,1)}) %reduce-scatter.5.cloned.1.call-update) | async-done | bytes 589840 | tf_op jit(solution)/shard_map/reduce_scatter | solution.py:123
  286.7 1.2 copy.80
  287.9 1.1 convert_element_type.159
  (10 shorter events, 0.1 us)
Async XLA Ops:
  7.2 81.9 %copy-start = (bf16[256,256]{1,0:T(8,128)(2,1)S(1)}, bf16[256,256]{1,0:T(8,128)(2,1)}, u32[]{:S(2)}) copy-start(bf16[256,256]{1,0:T(8,128)(2,1)} %param.9) | copy-start | bytes 393220
  21.3 5.4 %copy-start.3 = (bf16[256,768]{1,0:T(8,128)(2,1)}, bf16[256,768]{1,0:T(8,128)(2,1)S(1)}, u32[]{:S(2)}) copy-start(bf16[256,768]{1,0:T(8,128)(2,1)S(1)} %fusion.38) | copy-start | bytes 1179652
  37.5 12.6 %copy-start.6 = (f32[2,2,128]{2,1,0:T(2,128)S(1)}, f32[2,2,128]{2,1,0:T(2,128)}, u32[]{:S(2)}) copy-start(f32[2,2,128]{2,1,0:T(2,128)} %param.8) | copy-start | bytes 6148
  42.9 43.8 %all-to-all-start.1 = ((f32[4,2,3,256,128]{4,3,1,2,0:T(8,128)}), f32[4,2,3,256,128]{4,3,1,2,0:T(8,128)S(1)}, u32[]{:S(2)}, u32[]{:S(2)}) async-start(f32[4,2,3,256,128]{4,3,1,2,0:T(8,128)} %copy.63), calls=%async_computation.1 | async-start | bytes 6291456 | tf_op jit(solution)/shard_map/all_to_all | solution.py:51
  50.0 78.3 %all-gather.2.cloned.1.call-start = ((), (), s32[]{:S(2)}) async-start(), calls=%async_computation.4 | async-start | bytes 3538944 | tf_op jit(solution)/shard_map/all_gather | solution.py:95
  87.7 7.8 %copy-start.2 = (bf16[2,3,256,128]{3,2,0,1:T(8,128)(2,1)S(1)}, bf16[2,3,256,128]{3,2,0,1:T(8,128)(2,1)}, u32[]{:S(2)}) copy-start(bf16[2,3,256,128]{3,2,0,1:T(8,128)(2,1)} %reduce_sum.174) | copy-start | bytes 1179652
  87.7 9.2 %copy-start.4 = (bf16[256,768]{1,0:T(8,128)(2,1)S(1)}, bf16[256,768]{1,0:T(8,128)(2,1)}, u32[]{:S(2)}) copy-start(bf16[256,768]{1,0:T(8,128)(2,1)} %copy-done.3) | copy-start | bytes 1179652
  96.9 160.2 %reduce-scatter.3.cloned.1.call-start = ((), (), s32[]{:S(2)}) async-start(), calls=%async_computation.5 | async-start | bytes 10616832 | tf_op jit(solution)/shard_map/reduce_scatter | solution.py:106
  149.8 18.9 %copy-start.1 = (bf16[256,768]{1,0:T(8,128)(2,1)S(1)}, bf16[256,768]{1,0:T(8,128)(2,1)}, u32[]{:S(2)}) copy-start(bf16[256,768]{1,0:T(8,128)(2,1)} %param.5) | copy-start | bytes 1179652
  149.8 18.9 %copy-start.5 = (f32[768]{0:T(1024)S(1)}, f32[768]{0:T(1024)}, u32[]{:S(2)}) copy-start(f32[768]{0:T(1024)} %param.6) | copy-start | bytes 9220
  149.8 136.9 %reduce-scatter.5.cloned.1.call-start = ((), (), s32[]{:S(2)}) async-start(), calls=%async_computation.6 | async-start | bytes 1769472 | tf_op jit(solution)/shard_map/reduce_scatter | solution.py:123
  157.3 11.3 %collective-permute-start = (bf16[256,768]{1,0:T(8,128)(2,1)S(1)}, bf16[256,768]{1,0:T(8,128)(2,1)S(1)}, u32[]{:S(2)}, u32[]{:S(2)}) collective-permute-start(bf16[256,768]{1,0:T(8,128)(2,1)S(1)} %fusion.16), channel_id=1, source_target_pairs={{0,1},{1,0},{2,3},{3,2},{4,5},{5,4},{6,7},{7,6},{8,9},{9,8},{10,11... | collective-permute-start | bytes 1179656 | tf_op jit(solution)/shard_map/ppermute | solution.py:109
Sparse Core Ops, SparseCore 0:
  97.1 31.2 all-gather.1
  149.9 107.1 reduce-scatter.2
  259.7 26.9 reduce-scatter.4

commit v9 on v8

--- a/solution.py
+++ b/solution.py
@@ -92,7 +92,9 @@
 
     block_rows = width_local // (lax.axis_size("dph") * lax.axis_size("dpz"))
     stacked = jnp.stack([head_rows(d_query), head_rows(d_key), head_rows(d_values)], axis=1)
-    gathered = lax.all_gather(stacked, MX, axis=0, tiled=True)
+    across = lax.all_gather(stacked, "mxx", axis=0, tiled=False)
+    paired = lax.all_gather(across, "mxc", axis=0, tiled=False)
+    gathered = paired.transpose(1, 0, *range(2, paired.ndim)).reshape((-1,) + stacked.shape[1:])
     d_scaled = jnp.einsum("hste,sdhe->td", gathered, weights, preferred_element_type=jnp.float32)
     feature_part = scaled
     n_hi = lax.axis_size("dph")

time: 297 us -> 317 us (1.067)
  waiting for transfers between devices: 137 us -> 155 us
  local copies, waits for them, and re-layouts: 18.3 us -> 22.2 us
    all_gather x1 -> x2, waiting for transfers between devices: 31.2 us -> 49.4 us  [the longest x1 30.1 us: body(): across = lax.all_gather(stacked, 'mxx', axis=0, tiled=False)]
    all_gather x0 -> x1, local copies, waits for them, and re-layouts: none -> 3.19 us  [body(): paired = lax.all_gather(across, 'mxc', axis=0, tiled=False)]
  transfers between devices with their start and end apart: 5 -> 6, of which waited for: 5 -> 6; matrix products, arithmetic and copies ran while one was open for 3% -> 3% of each run, Pallas kernels for 0% -> 0%
where the time goes in v9:
time: 317 us; the launch traced here: 316 us
  waiting for transfers between devices  155 us (49%)
  blocking collectives  79.3 us (25%)
  matrix products  24.1 us (8%)
  local copies, waits for them, and re-layouts  22.2 us (7%)
  between operations  14 us (4%)
  other arithmetic  12.5 us (4%)
  starting transfers between devices  8.84 us (3%)
    psum x1, blocking collectives, body(): lax.psum((head_gain_part, feature_part), ('dph', 'dpz'))  45.9 us
    all_to_all x1, waiting for transfers between devices, body(): lax.all_to_all(on_chip, 'mxx', split_axis=0, concat_axis=0)  36.7 us
    all_gather x1, waiting for transfers between devices, body(): across = lax.all_gather(stacked, 'mxx', axis=0, tiled=False)  30.1 us
    reduce_scatter x1, waiting for transfers between devices, body(): w_half = lax.psum_scatter(w_part, 'dpz', scatter_dimension=0, tiled=True)  29.4 us
    reduce_scatter x1, waiting for transfers between devices, body(): lax.psum_scatter(w_half, 'dph', scatter_dimension=0, tiled=True)  29.3 us
    all_gather x1, waiting for transfers between devices, body(): paired = lax.all_gather(across, 'mxc', axis=0, tiled=False)  19.3 us
    convert_element_type x1, local copies, waits for them, and re-layouts, body(): w_part = jnp.einsum('td,hste->dshe', feature_part, gathered, preferred_el...  13.2 us
    psum x1, blocking collectives, body(): lax.psum((jnp.sum(d_hat, axis=1), jnp.sum(d_hat * normed, axis=1)), MX)  11.7 us
  transfers between devices with their start and end apart: 6, of which 6 were waited for; matrix products, arithmetic and copies ran while one was open for 3% of the time, Pallas kernels for 0%

profile of v9, /device:TPU:2, one launch (start us, length us, event | category | flops | bytes accessed | tf_op | source)
XLA Modules:
  0.0 315.6 jit_solution(14892534454774228772)
XLA Ops:
  7.2 0.0 copy-start
  7.2 1.3 convert_reduce_fusion
  8.4 11.7 %all-reduce.2 = (f32[256]{0:T(256)S(1)}, f32[256]{0:T(256)S(1)}) all-reduce(f32[256]{0:T(256)S(1)} %get-tuple-element.26, f32[256]{0:T(256)S(1)} %get-tuple-element.25), channel_id=1, replica_groups=mesh['dph'=2,'dpz'=8,'mxx'=4,'mxc'=2,'my'=2] {'mxx','mxc'}, use_global_device_ids=true, to_apply=%region_3.0 | all-reduce | flops 512 | bytes 4096 | tf_op jit(solution)/shard_map/psum | solution.py:36
  20.1 1.2 fusion.32
  21.3 0.0 copy-start.3
  21.4 5.4 %fusion.5 = f32[256,3,16,128]{3,0,2,1:T(8,128)S(1)} fusion(bf16[256,768]{1,0:T(8,128)(2,1)S(1)} %fusion.32, bf16[3,768,2048]{2,1,0:T(8,128)(2,1)} %param.7), kind=kOutput, calls=%fused_computation.5 | convolution fusion | flops 2415919104 | bytes 16121856 | tf_op jit(solution)/shard_map/td,sdhe->hste/dot_general | solution.py:48
  26.8 0.0 copy-done.3
  26.8 0.7 copy.117
  27.5 10.0 %all_to_all.10 = f32[2,4,2,3,256,128]{5,4,2,1,3,0:T(8,128)} all-to-all(f32[2,4,2,3,256,128]{5,4,2,1,3,0:T(8,128)S(1)} %bitcast.165), channel_id=1, replica_groups=mesh['dph'=2,'dpz'=8,'mxx'=4,'mxc'=2,'my'=2] {'mxc'}, dimensions={0} | all-to-all | bytes 12582912 | tf_op jit(solution)/shard_map/all_to_all | solution.py:50
  37.5 0.0 copy-start.7
  37.5 3.5 %reduce_sum.173 = f32[4,2,3,256,128]{4,3,1,0,2:T(8,128)S(1)} reduce(f32[2,4,2,3,256,128]{5,4,2,1,3,0:T(8,128)} %all_to_all.10, f32[]{:T(128)} %constant.20.clone.1), dimensions={0}, to_apply=%region_4.0 | reduce | flops 786432 | bytes 9437188 | tf_op jit(solution)/shard_map/reduce_sum | solution.py:50
  41.0 1.9 copy.63
  42.9 7.1 %all-to-all-start.1 = ((f32[4,2,3,256,128]{4,3,1,2,0:T(8,128)}), f32[4,2,3,256,128]{4,3,1,2,0:T(8,128)S(1)}, u32[]{:S(2)}, u32[]{:S(2)}) async-start(f32[4,2,3,256,128]{4,3,1,2,0:T(8,128)} %copy.63), calls=%async_computation.1 | async-start | bytes 6291456 | tf_op jit(solution)/shard_map/all_to_all | solution.py:51
  50.0 0.0 all-gather.5.cloned.1.call-start
  50.0 0.0 copy-done.7
  50.1 36.7 %all-to-all-done.1 = f32[4,2,3,256,128]{4,3,1,2,0:T(8,128)S(1)} async-done(((f32[4,2,3,256,128]{4,3,1,2,0:T(8,128)}), f32[4,2,3,256,128]{4,3,1,2,0:T(8,128)S(1)}, u32[]{:S(2)}, u32[]{:S(2)}) %all-to-all-start.1) | async-done | bytes 3145760 | tf_op jit(solution)/shard_map/all_to_all | solution.py:51
  86.7 1.0 reduce_sum.174
  87.8 0.0 copy-start.2
  87.8 0.0 copy-start.4
  87.8 1.3 fusion.43
  89.1 0.0 copy-done
  89.1 1.1 convolution_bitcast_fusion
  90.3 1.6 fusion.98
  91.8 0.2 fusion.20
  92.0 1.3 fusion.21
  93.4 2.1 fusion.55
  95.5 0.0 copy-done.2
  95.5 0.6 fusion.73
  96.1 0.8 pad_maximum_fusion
  96.9 0.0 all-gather.5.cloned.1.call-update
  96.9 0.0 all-gather.7.cloned.1.call-start
  96.9 30.1 %all-gather.5.cloned.1.call-done = bf16[8,3,256,128]{3,2,0,1:T(8,128)(2,1)} async-done(((bf16[2,3,256,128]{3,2,0,1:T(8,128)(2,1)}), bf16[8,3,256,128]{3,2,0,1:T(8,128)(2,1)}) %all-gather.5.cloned.1.call-update) | async-done | bytes 1572880 | tf_op jit(solution)/shard_map/all_gather | solution.py:95
  127.1 0.0 all-gather.7.cloned.1.call-update
  127.1 0.0 reduce-scatter.3.cloned.1.call-start
  127.1 0.0 copy-done.4
  127.2 0.2 copy.72
  127.3 0.8 copy.73
  128.1 19.3 %all-gather.7.cloned.1.call-done = bf16[8,2,3,256,128]{4,3,1,0,2:T(8,128)(2,1)} async-done(((bf16[4,2,3,256,128]{4,3,1,0,2:T(8,128)(2,1)}), bf16[8,2,3,256,128]{4,3,1,0,2:T(8,128)(2,1)}) %all-gather.7.cloned.1.call-update) | async-done | bytes 3145744 | tf_op jit(solution)/shard_map/all_gather | solution.py:96
  147.4 3.2 %copy.71 = bf16[2,4,2,3,256,128]{4,5,3,2,0,1:T(8,128)(2,1)S(1)} copy(bf16[2,4,2,3,256,128]{5,4,2,1,0,3:T(8,128)(2,1)} %bitcast.169) | data formatting | bytes 6291456 | tf_op jit(solution)/shard_map/all_gather | solution.py:96
  150.6 6.0 %convert_bitcast_fusion = bf16[768,3,16,128]{0,3,1,2:T(8,128)(2,1)} fusion(bf16[16,3,256,128]{2,3,1,0:T(8,128)(2,1)S(1)} %bitcast.166, bf16[256,768,1,1]{0,1,3,2:T(8,128)(2,1)} %bitcast.176), kind=kOutput, calls=%fused_computation.8 | convolution fusion | flops 2420637696 | bytes 12976128 | tf_op jit(solution)/shard_map/td,hste->dshe/dot_general | solution.py:105
  156.6 13.2 %copy.75 = bf16[768,3,16,128]{3,2,1,0:T(8,128)(2,1)} copy(bf16[768,3,16,128]{0,3,1,2:T(8,128)(2,1)} %convert_bitcast_fusion) | data formatting | bytes 18874368 | tf_op jit(solution)/shard_map/convert_element_type | solution.py:107
  169.8 0.0 reduce-scatter.3.cloned.1.call-update
  169.8 0.0 copy-start.6
  169.8 0.0 reduce-scatter.5.cloned.1.call-start
  169.9 0.0 copy-start.1
  169.9 6.4 %fusion.12 = bf16[256,768]{1,0:T(8,128)(2,1)S(1)} fusion(bf16[16,3,256,128]{2,3,1,0:T(8,128)(2,1)S(1)} %bitcast.167, bf16[3,768,2048]{2,1,0:T(8,128)(2,1)} %param.7), kind=kOutput, calls=%fused_computation.12 | convolution fusion | flops 2416115712 | bytes 12976128 | tf_op jit(solution)/shard_map/hste,sdhe->td/dot_general | solution.py:98
  176.3 0.0 copy-start.5
  176.3 1.6 collective-permute-start
  177.9 9.8 %collective-permute-done = bf16[256,768]{1,0:T(8,128)(2,1)S(1)} collective-permute-done((bf16[256,768]{1,0:T(8,128)(2,1)S(1)}, bf16[256,768]{1,0:T(8,128)(2,1)S(1)}, u32[]{:S(2)}, u32[]{:S(2)}) %collective-permute-start) | collective-permute-done | bytes 393248 | tf_op jit(solution)/shard_map/ppermute | solution.py:111
  187.7 0.0 copy-done.6
  187.7 0.0 copy-done.1
  187.7 0.5 fusion.38
  188.2 0.0 copy-done.5
  188.2 11.7 %all-reduce.1 = (f32[256]{0:T(256)S(1)}, f32[256]{0:T(256)S(1)}) all-reduce(f32[256]{0:T(256)S(1)} %get-tuple-element.13, f32[256]{0:T(256)S(1)} %get-tuple-element.14), channel_id=1, replica_groups=mesh['dph'=2,'dpz'=8,'mxx'=4,'mxc'=2,'my'=2] {'mxx','mxc'}, use_global_device_ids=true, to_apply=%region_21.0 | all-reduce | flops 512 | bytes 4096 | tf_op jit(solution)/shard_map/psum | solution.py:114
  199.9 45.9 %all-reduce = (f32[768]{0:T(1024)}, f32[2,2,128]{2,1,0:T(2,128)}) all-reduce(f32[768]{0:T(1024)S(1)} %get-tuple-element.12, f32[2,2,128]{2,1,0:T(2,128)S(1)} %pad_maximum_fusion.1), channel_id=1, replica_groups=mesh['dph'=2,'dpz'=8,'mxx'=4,'mxc'=2,'my'=2] {'dph','dpz'}, use_global_device_ids=true, to_apply=%region_23.0 | all-reduce | flops 1280 | bytes 10240 | tf_op jit(solution)/shard_map/psum | solution.py:121
  245.8 2.2 fusion.37
  248.1 29.4 %reduce-scatter.3.cloned.1.call-done = bf16[96,3,16,128]{3,2,1,0:T(8,128)(2,1)} async-done(((bf16[768,3,16,128]{3,2,1,0:T(8,128)(2,1)}), bf16[96,3,16,128]{3,2,1,0:T(8,128)(2,1)}) %reduce-scatter.3.cloned.1.call-update) | async-done | bytes 1179664 | tf_op jit(solution)/shard_map/reduce_scatter | solution.py:108
  277.5 0.0 reduce-scatter.5.cloned.1.call-update
  277.5 29.3 %reduce-scatter.5.cloned.1.call-done = bf16[48,3,16,128]{3,2,1,0:T(8,128)(2,1)} async-done(((bf16[96,3,16,128]{3,2,1,0:T(8,128)(2,1)}), bf16[48,3,16,128]{3,2,1,0:T(8,128)(2,1)}) %reduce-scatter.5.cloned.1.call-update) | async-done | bytes 589840 | tf_op jit(solution)/shard_map/reduce_scatter | solution.py:125
  306.9 1.2 copy.80
  308.0 1.1 convert_element_type.159
  (9 shorter events, 0.0 us)
Async XLA Ops:
  7.2 81.9 %copy-start = (bf16[256,256]{1,0:T(8,128)(2,1)S(1)}, bf16[256,256]{1,0:T(8,128)(2,1)}, u32[]{:S(2)}) copy-start(bf16[256,256]{1,0:T(8,128)(2,1)} %param.9) | copy-start | bytes 393220
  21.3 5.4 %copy-start.3 = (bf16[256,768]{1,0:T(8,128)(2,1)}, bf16[256,768]{1,0:T(8,128)(2,1)S(1)}, u32[]{:S(2)}) copy-start(bf16[256,768]{1,0:T(8,128)(2,1)S(1)} %fusion.32) | copy-start | bytes 1179652
  37.5 12.6 %copy-start.7 = (f32[2,2,128]{2,1,0:T(2,128)S(1)}, f32[2,2,128]{2,1,0:T(2,128)}, u32[]{:S(2)}) copy-start(f32[2,2,128]{2,1,0:T(2,128)} %param.8) | copy-start | bytes 6148
  42.9 43.8 %all-to-all-start.1 = ((f32[4,2,3,256,128]{4,3,1,2,0:T(8,128)}), f32[4,2,3,256,128]{4,3,1,2,0:T(8,128)S(1)}, u32[]{:S(2)}, u32[]{:S(2)}) async-start(f32[4,2,3,256,128]{4,3,1,2,0:T(8,128)} %copy.63), calls=%async_computation.1 | async-start | bytes 6291456 | tf_op jit(solution)/shard_map/all_to_all | solution.py:51
  50.0 77.0 %all-gather.5.cloned.1.call-start = ((), (), s32[]{:S(2)}) async-start(), calls=%async_computation.6 | async-start | bytes 1966080 | tf_op jit(solution)/shard_map/all_gather | solution.py:95
  87.8 7.7 %copy-start.2 = (bf16[2,3,256,128]{3,2,0,1:T(8,128)(2,1)S(1)}, bf16[2,3,256,128]{3,2,0,1:T(8,128)(2,1)}, u32[]{:S(2)}) copy-start(bf16[2,3,256,128]{3,2,0,1:T(8,128)(2,1)} %reduce_sum.174) | copy-start | bytes 1179652
  87.8 39.4 %copy-start.4 = (bf16[256,768]{1,0:T(8,128)(2,1)S(1)}, bf16[256,768]{1,0:T(8,128)(2,1)}, u32[]{:S(2)}) copy-start(bf16[256,768]{1,0:T(8,128)(2,1)} %copy-done.3) | copy-start | bytes 1179652
  96.9 50.5 %all-gather.7.cloned.1.call-start = ((), (), s32[]{:S(2)}) async-start(), calls=%async_computation.7 | async-start | bytes 4718592 | tf_op jit(solution)/shard_map/all_gather | solution.py:96
  127.1 150.4 %reduce-scatter.3.cloned.1.call-start = ((), (), s32[]{:S(2)}) async-start(), calls=%async_computation.4 | async-start | bytes 10616832 | tf_op jit(solution)/shard_map/reduce_scatter | solution.py:108
  169.8 17.9 %copy-start.6 = (f32[768]{0:T(1024)S(1)}, f32[768]{0:T(1024)}, u32[]{:S(2)}) copy-start(f32[768]{0:T(1024)} %param.6) | copy-start | bytes 9220
  169.8 137.0 %reduce-scatter.5.cloned.1.call-start = ((), (), s32[]{:S(2)}) async-start(), calls=%async_computation.5 | async-start | bytes 1769472 | tf_op jit(solution)/shard_map/reduce_scatter | solution.py:125
  169.9 17.8 %copy-start.1 = (bf16[256,768]{1,0:T(8,128)(2,1)S(1)}, bf16[256,768]{1,0:T(8,128)(2,1)}, u32[]{:S(2)}) copy-start(bf16[256,768]{1,0:T(8,128)(2,1)} %param.5) | copy-start | bytes 1179652
  176.3 11.9 %copy-start.5 = (bf16[256,768]{1,0:T(8,128)(2,1)}, bf16[256,768]{1,0:T(8,128)(2,1)S(1)}, u32[]{:S(2)}) copy-start(bf16[256,768]{1,0:T(8,128)(2,1)S(1)} %fusion.12) | copy-start | bytes 1179652
  176.3 11.4 %collective-permute-start = (bf16[256,768]{1,0:T(8,128)(2,1)S(1)}, bf16[256,768]{1,0:T(8,128)(2,1)S(1)}, u32[]{:S(2)}, u32[]{:S(2)}) collective-permute-start(bf16[256,768]{1,0:T(8,128)(2,1)S(1)} %fusion.12), channel_id=1, source_target_pairs={{0,1},{1,0},{2,3},{3,2},{4,5},{5,4},{6,7},{7,6},{8,9},{9,8},{10,11... | collective-permute-start | bytes 1179656 | tf_op jit(solution)/shard_map/ppermute | solution.py:111
Sparse Core Ops, SparseCore 0:
  97.0 30.0 all-gather.4
  128.9 18.4 all-gather.6
  169.9 107.5 reduce-scatter.2
  279.9 26.9 reduce-scatter.4

commit v10 on v8

--- a/solution.py
+++ b/solution.py
@@ -120,7 +120,10 @@
     w_half, result_rows, feature_total, head_total = lax.optimization_barrier(
         (w_half, result_rows, feature_total, head_total)
     )
-    w_rows = lax.psum_scatter(w_half, "dph", scatter_dimension=0, tiled=True).astype(jnp.float32)
+    hi_index = lax.axis_index("dph")
+    halves = w_half.reshape((n_hi, -1) + w_half.shape[1:])
+    swapped = lax.ppermute(halves[1 - hi_index], "dph", [(0, 1), (1, 0)])
+    w_rows = halves[hi_index].astype(jnp.float32) + swapped.astype(jnp.float32)
     w_grad = (
         w_rows.reshape(block_rows, 3, group_heads * head_size)
         .transpose(1, 0, 2)

time: 297 us -> 284 us (0.956)
  waiting for transfers between devices: 137 us -> 121 us
  starting transfers between devices: 8.97 us -> 12 us
    reduce_scatter x1 -> x0, waiting for transfers between devices: 29.5 us -> none  [body(): lax.psum_scatter(w_half, 'dph', scatter_dimension=0, tiled=True)]
    ppermute x0 -> x1, waiting for transfers between devices: none -> 13.5 us  [body(): swapped = lax.ppermute(halves[1 - hi_index], 'dph', [(0, 1), (1, 0)])]
    ppermute x0 -> x1, starting transfers between devices: none -> 3.1 us  [body(): swapped = lax.ppermute(halves[1 - hi_index], 'dph', [(0, 1), (1, 0)])]
where the time goes in v10:
time: 284 us; the launch traced here: 283 us
  waiting for transfers between devices  121 us (43%)
  blocking collectives  79.1 us (28%)
  matrix products  26.3 us (9%)
  local copies, waits for them, and re-layouts  18.3 us (6%)
  between operations  14.3 us (5%)
  other arithmetic  12.6 us (4%)
  starting transfers between devices  12 us (4%)
    psum x1, blocking collectives, body(): lax.psum((head_gain_part, feature_part), ('dph', 'dpz'))  45.9 us
    all_to_all x1, waiting for transfers between devices, body(): lax.all_to_all(on_chip, 'mxx', split_axis=0, concat_axis=0)  36.7 us
    all_gather x1, waiting for transfers between devices, body(): gathered = lax.all_gather(stacked, MX, axis=0, tiled=True)  31 us
    reduce_scatter x1, waiting for transfers between devices, body(): w_half = lax.psum_scatter(w_part, 'dpz', scatter_dimension=0, tiled=True)  29.6 us
    ppermute x1, waiting for transfers between devices, body(): swapped = lax.ppermute(halves[1 - hi_index], 'dph', [(0, 1), (1, 0)])  13.5 us
    convert_element_type x1, local copies, waits for them, and re-layouts, body(): w_part = jnp.einsum('td,hste->dshe', feature_part, gathered, preferred_el...  13.2 us
    psum x1, blocking collectives, body(): lax.psum((jnp.sum(widened, axis=1), jnp.sum(widened * widened, axis=1)), MX)  11.7 us
    psum x1, blocking collectives, body(): lax.psum((jnp.sum(d_hat, axis=1), jnp.sum(d_hat * normed, axis=1)), MX)  11.6 us
  transfers between devices with their start and end apart: 5, of which 5 were waited for; matrix products, arithmetic and copies ran while one was open for 3% of the time, Pallas kernels for 0%

profile of v10, /device:TPU:2, one launch (start us, length us, event | category | flops | bytes accessed | tf_op | source)
XLA Modules:
  0.0 283.1 jit_solution(4475641054077432971)
XLA Ops:
  7.2 0.0 copy-start
  7.2 1.3 convert_reduce_fusion
  8.4 11.7 %all-reduce.2 = (f32[256]{0:T(256)S(1)}, f32[256]{0:T(256)S(1)}) all-reduce(f32[256]{0:T(256)S(1)} %get-tuple-element.26, f32[256]{0:T(256)S(1)} %get-tuple-element.25), channel_id=1, replica_groups=mesh['dph'=2,'dpz'=8,'mxx'=4,'mxc'=2,'my'=2] {'mxx','mxc'}, use_global_device_ids=true, to_apply=%region_3.0 | all-reduce | flops 512 | bytes 4096 | tf_op jit(solution)/shard_map/psum | solution.py:36
  20.1 1.2 fusion.39
  21.3 0.0 copy-start.4
  21.4 5.4 %fusion.5 = f32[256,3,16,128]{3,0,2,1:T(8,128)S(1)} fusion(bf16[256,768]{1,0:T(8,128)(2,1)S(1)} %fusion.39, bf16[3,768,2048]{2,1,0:T(8,128)(2,1)} %param.7), kind=kOutput, calls=%fused_computation.5 | convolution fusion | flops 2415919104 | bytes 16121856 | tf_op jit(solution)/shard_map/td,sdhe->hste/dot_general | solution.py:48
  26.8 0.0 copy-done.4
  26.8 0.7 copy.146
  27.5 10.0 %all_to_all.10 = f32[2,4,2,3,256,128]{5,4,2,1,3,0:T(8,128)} all-to-all(f32[2,4,2,3,256,128]{5,4,2,1,3,0:T(8,128)S(1)} %bitcast.164), channel_id=1, replica_groups=mesh['dph'=2,'dpz'=8,'mxx'=4,'mxc'=2,'my'=2] {'mxc'}, dimensions={0} | all-to-all | bytes 12582912 | tf_op jit(solution)/shard_map/all_to_all | solution.py:50
  37.5 3.5 %reduce_sum.173 = f32[4,2,3,256,128]{4,3,1,0,2:T(8,128)S(1)} reduce(f32[2,4,2,3,256,128]{5,4,2,1,3,0:T(8,128)} %all_to_all.10, f32[]{:T(128)} %constant.28.clone.1), dimensions={0}, to_apply=%region_4.0 | reduce | flops 786432 | bytes 9437188 | tf_op jit(solution)/shard_map/reduce_sum | solution.py:50
  41.0 0.0 copy-start.7
  41.0 1.9 copy.83
  42.9 7.1 %all-to-all-start.1 = ((f32[4,2,3,256,128]{4,3,1,2,0:T(8,128)}), f32[4,2,3,256,128]{4,3,1,2,0:T(8,128)S(1)}, u32[]{:S(2)}, u32[]{:S(2)}) async-start(f32[4,2,3,256,128]{4,3,1,2,0:T(8,128)} %copy.83), calls=%async_computation.1 | async-start | bytes 6291456 | tf_op jit(solution)/shard_map/all_to_all | solution.py:51
  50.1 0.0 all-gather.2.cloned.1.call-start
  50.1 0.0 copy-done.7
  50.1 36.7 %all-to-all-done.1 = f32[4,2,3,256,128]{4,3,1,2,0:T(8,128)S(1)} async-done(((f32[4,2,3,256,128]{4,3,1,2,0:T(8,128)}), f32[4,2,3,256,128]{4,3,1,2,0:T(8,128)S(1)}, u32[]{:S(2)}, u32[]{:S(2)}) %all-to-all-start.1) | async-done | bytes 3145760 | tf_op jit(solution)/shard_map/all_to_all | solution.py:51
  86.7 1.0 reduce_sum.174
  87.8 0.0 copy-start.3
  87.8 1.3 fusion.50
  89.1 0.0 copy-done
  89.1 1.1 convolution_bitcast_fusion
  90.2 0.0 copy-start.5
  90.2 1.6 fusion.105
  91.8 0.2 fusion.27
  92.1 1.3 fusion.28
  93.4 0.0 copy-done.3
  93.4 1.1 fusion.62
  94.5 0.6 fusion.80
  95.2 0.8 pad_maximum_fusion
  95.9 0.0 all-gather.2.cloned.1.call-update
  96.0 0.2 reduce-scatter.2.cloned.1.call-start
  96.2 0.0 copy-done.5
  96.2 0.2 copy.91
  96.4 31.0 %all-gather.2.cloned.1.call-done = bf16[16,3,256,128]{3,2,0,1:T(8,128)(2,1)} async-done(((bf16[2,3,256,128]{3,2,0,1:T(8,128)(2,1)}), bf16[16,3,256,128]{3,2,0,1:T(8,128)(2,1)}) %all-gather.2.cloned.1.call-update) | async-done | bytes 3145744 | tf_op jit(solution)/shard_map/all_gather | solution.py:95
  127.4 8.2 %convert_bitcast_fusion = bf16[768,3,16,128]{0,3,1,2:T(8,128)(2,1)} fusion(bf16[256,768,1,1]{0,1,3,2:T(8,128)(2,1)S(1)} %bitcast.172, bf16[16,3,256,128]{3,2,0,1:T(8,128)(2,1)} %all-gather.2.cloned.1.call-done), kind=kOutput, calls=%fused_computation.8 | convolution fusion | flops 2420637696 | bytes 12976128 | tf_op jit(solution)/shard_map/td,hste->dshe/dot_general | solution.py:103
  135.6 13.2 %copy.95 = bf16[768,3,16,128]{3,2,1,0:T(8,128)(2,1)} copy(bf16[768,3,16,128]{0,3,1,2:T(8,128)(2,1)} %convert_bitcast_fusion) | data formatting | bytes 18874368 | tf_op jit(solution)/shard_map/convert_element_type | solution.py:105
  148.8 0.0 reduce-scatter.2.cloned.1.call-update
  148.8 0.0 copy-start.2
  148.9 0.0 copy-start.6
  148.9 0.0 copy-start.1
  148.9 7.3 %fusion.16 = bf16[256,768]{1,0:T(8,128)(2,1)S(1)} fusion(bf16[16,3,256,128]{3,2,0,1:T(8,128)(2,1)} %all-gather.2.cloned.1.call-done, bf16[3,768,2048]{2,1,0:T(8,128)(2,1)} %param.7), kind=kOutput, calls=%fused_computation.14 | convolution fusion | flops 2416115712 | bytes 12976128 | tf_op jit(solution)/shard_map/hste,sdhe->td/dot_general | solution.py:96
  156.2 1.6 collective-permute-start
  157.8 9.8 %collective-permute-done = bf16[256,768]{1,0:T(8,128)(2,1)S(1)} collective-permute-done((bf16[256,768]{1,0:T(8,128)(2,1)S(1)}, bf16[256,768]{1,0:T(8,128)(2,1)S(1)}, u32[]{:S(2)}, u32[]{:S(2)}) %collective-permute-start) | collective-permute-done | bytes 393248 | tf_op jit(solution)/shard_map/ppermute | solution.py:109
  167.5 0.0 copy-done.2
  167.6 0.0 copy-done.6
  167.6 0.4 fusion.45
  168.0 11.6 %all-reduce.1 = (f32[256]{0:T(256)S(1)}, f32[256]{0:T(256)S(1)}) all-reduce(f32[256]{0:T(256)S(1)} %get-tuple-element.13, f32[256]{0:T(256)S(1)} %get-tuple-element.14), channel_id=1, replica_groups=mesh['dph'=2,'dpz'=8,'mxx'=4,'mxc'=2,'my'=2] {'mxx','mxc'}, use_global_device_ids=true, to_apply=%region_21.0 | all-reduce | flops 512 | bytes 4096 | tf_op jit(solution)/shard_map/psum | solution.py:112
  179.6 45.9 %all-reduce = (f32[768]{0:T(1024)}, f32[2,2,128]{2,1,0:T(2,128)}) all-reduce(f32[768]{0:T(1024)S(1)} %get-tuple-element.12, f32[2,2,128]{2,1,0:T(2,128)S(1)} %pad_maximum_fusion.1), channel_id=1, replica_groups=mesh['dph'=2,'dpz'=8,'mxx'=4,'mxc'=2,'my'=2] {'dph','dpz'}, use_global_device_ids=true, to_apply=%region_23.0 | all-reduce | flops 1280 | bytes 10240 | tf_op jit(solution)/shard_map/psum | solution.py:119
  225.5 1.1 fusion.44
  226.6 29.6 %reduce-scatter.2.cloned.1.call-done = bf16[96,3,16,128]{3,2,1,0:T(8,128)(2,1)} async-done(((bf16[768,3,16,128]{3,2,1,0:T(8,128)(2,1)}), bf16[96,3,16,128]{3,2,1,0:T(8,128)(2,1)}) %reduce-scatter.2.cloned.1.call-update) | async-done | bytes 1179664 | tf_op jit(solution)/shard_map/reduce_scatter | solution.py:106
  256.2 1.1 dynamic-slice_bitcast_fusion
  257.3 3.1 %collective-permute-start.1 = (bf16[48,3,16,128]{3,2,1,0:T(8,128)(2,1)S(1)}, bf16[48,3,16,128]{3,2,1,0:T(8,128)(2,1)S(1)}, u32[]{:S(2)}, u32[]{:S(2)}) collective-permute-start(bf16[48,3,16,128]{3,2,1,0:T(8,128)(2,1)S(1)} %dynamic-slice_bitcast_fusion), channel_id=1, source_target_pairs={{0,128},{128,0},{1,129},{129,1},{2,130},{130,2},{3,131},{131,3},{4... | collective-permute-start | bytes 1769480 | tf_op jit(solution)/shard_map/ppermute | solution.py:125
  260.4 13.5 %collective-permute-done.1 = bf16[48,3,16,128]{3,2,1,0:T(8,128)(2,1)S(1)} collective-permute-done((bf16[48,3,16,128]{3,2,1,0:T(8,128)(2,1)S(1)}, bf16[48,3,16,128]{3,2,1,0:T(8,128)(2,1)S(1)}, u32[]{:S(2)}, u32[]{:S(2)}) %collective-permute-start.1) | collective-permute-done | bytes 589856 | tf_op jit(solution)/shard_map/ppermute | solution.py:125
  273.9 1.2 fusion.26
  275.1 0.1 copy.100
  275.2 1.1 convert_element_type.173
  276.3 0.0 copy-done.1
  (10 shorter events, 0.1 us)
Async XLA Ops:
  7.2 81.9 %copy-start = (bf16[256,256]{1,0:T(8,128)(2,1)S(1)}, bf16[256,256]{1,0:T(8,128)(2,1)}, u32[]{:S(2)}) copy-start(bf16[256,256]{1,0:T(8,128)(2,1)} %param.9) | copy-start | bytes 393220
  21.3 5.4 %copy-start.4 = (bf16[256,768]{1,0:T(8,128)(2,1)}, bf16[256,768]{1,0:T(8,128)(2,1)S(1)}, u32[]{:S(2)}) copy-start(bf16[256,768]{1,0:T(8,128)(2,1)S(1)} %fusion.39) | copy-start | bytes 1179652
  41.0 9.0 %copy-start.7 = (f32[2,2,128]{2,1,0:T(2,128)S(1)}, f32[2,2,128]{2,1,0:T(2,128)}, u32[]{:S(2)}) copy-start(f32[2,2,128]{2,1,0:T(2,128)} %param.8) | copy-start | bytes 6148
  42.9 43.8 %all-to-all-start.1 = ((f32[4,2,3,256,128]{4,3,1,2,0:T(8,128)}), f32[4,2,3,256,128]{4,3,1,2,0:T(8,128)S(1)}, u32[]{:S(2)}, u32[]{:S(2)}) async-start(f32[4,2,3,256,128]{4,3,1,2,0:T(8,128)} %copy.83), calls=%async_computation.1 | async-start | bytes 6291456 | tf_op jit(solution)/shard_map/all_to_all | solution.py:51
  50.1 77.3 %all-gather.2.cloned.1.call-start = ((), (), s32[]{:S(2)}) async-start(), calls=%async_computation.3 | async-start | bytes 3538944 | tf_op jit(solution)/shard_map/all_gather | solution.py:95
  87.8 5.7 %copy-start.3 = (bf16[2,3,256,128]{3,2,0,1:T(8,128)(2,1)S(1)}, bf16[2,3,256,128]{3,2,0,1:T(8,128)(2,1)}, u32[]{:S(2)}) copy-start(bf16[2,3,256,128]{3,2,0,1:T(8,128)(2,1)} %reduce_sum.174) | copy-start | bytes 1179652
  90.2 6.0 %copy-start.5 = (bf16[256,768]{1,0:T(8,128)(2,1)S(1)}, bf16[256,768]{1,0:T(8,128)(2,1)}, u32[]{:S(2)}) copy-start(bf16[256,768]{1,0:T(8,128)(2,1)} %copy-done.4) | copy-start | bytes 1179652
  96.0 160.2 %reduce-scatter.2.cloned.1.call-start = ((), (), s32[]{:S(2)}) async-start(), calls=%async_computation.4 | async-start | bytes 10616832 | tf_op jit(solution)/shard_map/reduce_scatter | solution.py:106
  148.8 18.7 %copy-start.2 = (bf16[256,768]{1,0:T(8,128)(2,1)S(1)}, bf16[256,768]{1,0:T(8,128)(2,1)}, u32[]{:S(2)}) copy-start(bf16[256,768]{1,0:T(8,128)(2,1)} %param.5) | copy-start | bytes 1179652
  148.9 18.7 %copy-start.6 = (f32[768]{0:T(1024)S(1)}, f32[768]{0:T(1024)}, u32[]{:S(2)}) copy-start(f32[768]{0:T(1024)} %param.6) | copy-start | bytes 9220
  148.9 127.4 %copy-start.1 = (bf16[256,256]{1,0:T(8,128)(2,1)S(1)}, bf16[256,256]{1,0:T(8,128)(2,1)}, u32[]{:S(2)}) copy-start(bf16[256,256]{1,0:T(8,128)(2,1)} %param.9) | copy-start | bytes 393220
  156.2 11.3 %collective-permute-start = (bf16[256,768]{1,0:T(8,128)(2,1)S(1)}, bf16[256,768]{1,0:T(8,128)(2,1)S(1)}, u32[]{:S(2)}, u32[]{:S(2)}) collective-permute-start(bf16[256,768]{1,0:T(8,128)(2,1)S(1)} %fusion.16), channel_id=1, source_target_pairs={{0,1},{1,0},{2,3},{3,2},{4,5},{5,4},{6,7},{7,6},{8,9},{9,8},{10,11... | collective-permute-start | bytes 1179656 | tf_op jit(solution)/shard_map/ppermute | solution.py:109
  257.3 16.6 %collective-permute-start.1 = (bf16[48,3,16,128]{3,2,1,0:T(8,128)(2,1)S(1)}, bf16[48,3,16,128]{3,2,1,0:T(8,128)(2,1)S(1)}, u32[]{:S(2)}, u32[]{:S(2)}) collective-permute-start(bf16[48,3,16,128]{3,2,1,0:T(8,128)(2,1)S(1)} %dynamic-slice_bitcast_fusion), channel_id=1, source_target_pairs={{0,128},{128,0},{1,129},{129,1},{2,130},{130,2},{3,131},{131,3},{4... | collective-permute-start | bytes 1769480 | tf_op jit(solution)/shard_map/ppermute | solution.py:125
Sparse Core Ops, SparseCore 0:
  96.1 31.2 all-gather.1
  149.0 107.1 reduce-scatter.1

commit v11 on v10

--- a/solution.py
+++ b/solution.py
@@ -33,7 +33,8 @@
     width_local = inputs.shape[1]
     width = width_local * lax.axis_size(MX)
     widened = inputs.astype(jnp.float32)
-    totals = lax.psum((jnp.sum(widened, axis=1), jnp.sum(widened * widened, axis=1)), MX)
+    totals = lax.psum((jnp.sum(widened, axis=1), jnp.sum(widened * widened, axis=1)), "mxc")
+    totals = lax.psum(totals, "mxx")
     average = totals[0][:, None] / width
     spread = totals[1][:, None] / width - average * average
     inv_scale = lax.rsqrt(spread + epsilon)

time: 284 us -> 282 us (level)
    psum x1 -> x2, blocking collectives: 11.7 us -> 12.4 us  [the longest x1 9.94 us: body(): totals = lax.psum(totals, 'mxx')]
where the time goes in v11:
time: 282 us; the launch traced here: 281 us
  waiting for transfers between devices  121 us (43%)
  blocking collectives  79.9 us (28%)
  matrix products  26.3 us (9%)
  local copies, waits for them, and re-layouts  18.3 us (6%)
  between operations  14.3 us (5%)
  other arithmetic  12.6 us (4%)
  starting transfers between devices  9.63 us (3%)
    psum x1, blocking collectives, body(): lax.psum((head_gain_part, feature_part), ('dph', 'dpz'))  45.9 us
    all_to_all x1, waiting for transfers between devices, body(): lax.all_to_all(on_chip, 'mxx', split_axis=0, concat_axis=0)  36.7 us
    all_gather x1, waiting for transfers between devices, body(): gathered = lax.all_gather(stacked, MX, axis=0, tiled=True)  31 us
    reduce_scatter x1, waiting for transfers between devices, body(): w_half = lax.psum_scatter(w_part, 'dpz', scatter_dimension=0, tiled=True)  29.6 us
    ppermute x1, waiting for transfers between devices, body(): swapped = lax.ppermute(halves[1 - hi_index], 'dph', [(0, 1), (1, 0)])  13.5 us
    convert_element_type x1, local copies, waits for them, and re-layouts, body(): w_part = jnp.einsum('td,hste->dshe', feature_part, gathered, preferred_el...  13.2 us
    psum x1, blocking collectives, body(): lax.psum((jnp.sum(d_hat, axis=1), jnp.sum(d_hat * normed, axis=1)), MX)  11.6 us
    all_to_all x1, blocking collectives, body(): lax.all_to_all(partial, 'mxc', split_axis=0, concat_axis=0)  9.99 us
  transfers between devices with their start and end apart: 5, of which 5 were waited for; matrix products, arithmetic and copies ran while one was open for 3% of the time, Pallas kernels for 0%

profile of v11, /device:TPU:2, one launch (start us, length us, event | category | flops | bytes accessed | tf_op | source)
XLA Modules:
  0.0 281.5 jit_solution(8188719756416054861)
XLA Ops:
  7.2 0.0 copy-start
  7.2 1.3 convert_reduce_fusion
  8.4 2.5 all-reduce.3
  10.9 9.9 %all-reduce.2 = (f32[256]{0:T(256)S(1)}, f32[256]{0:T(256)S(1)}) all-reduce(f32[256]{0:T(256)S(1)} %get-tuple-element.35, f32[256]{0:T(256)S(1)} %get-tuple-element.36), channel_id=1, replica_groups=mesh['dph'=2,'dpz'=8,'mxx'=4,'mxc'=2,'my'=2] {'mxx'}, use_global_device_ids=true, to_apply=%region_5.0 | all-reduce | flops 512 | bytes 4096 | tf_op jit(solution)/shard_map/psum | solution.py:37
  20.9 1.2 fusion.39
  22.1 0.0 copy-start.4
  22.1 5.4 %fusion.5 = f32[256,3,16,128]{3,0,2,1:T(8,128)S(1)} fusion(bf16[256,768]{1,0:T(8,128)(2,1)S(1)} %fusion.39, bf16[3,768,2048]{2,1,0:T(8,128)(2,1)} %param.7), kind=kOutput, calls=%fused_computation.5 | convolution fusion | flops 2415919104 | bytes 16121856 | tf_op jit(solution)/shard_map/td,sdhe->hste/dot_general | solution.py:49
  27.5 0.0 copy-done.4
  27.5 0.7 copy.146
  28.2 10.0 %all_to_all.10 = f32[2,4,2,3,256,128]{5,4,2,1,3,0:T(8,128)} all-to-all(f32[2,4,2,3,256,128]{5,4,2,1,3,0:T(8,128)S(1)} %bitcast.164), channel_id=1, replica_groups=mesh['dph'=2,'dpz'=8,'mxx'=4,'mxc'=2,'my'=2] {'mxc'}, dimensions={0} | all-to-all | bytes 12582912 | tf_op jit(solution)/shard_map/all_to_all | solution.py:51
  38.2 3.5 %reduce_sum.173 = f32[4,2,3,256,128]{4,3,1,0,2:T(8,128)S(1)} reduce(f32[2,4,2,3,256,128]{5,4,2,1,3,0:T(8,128)} %all_to_all.10, f32[]{:T(128)} %constant.28.clone.1), dimensions={0}, to_apply=%region_6.0 | reduce | flops 786432 | bytes 9437188 | tf_op jit(solution)/shard_map/reduce_sum | solution.py:51
  41.8 0.0 copy-start.7
  41.8 1.9 copy.83
  43.6 4.7 %all-to-all-start.1 = ((f32[4,2,3,256,128]{4,3,1,2,0:T(8,128)}), f32[4,2,3,256,128]{4,3,1,2,0:T(8,128)S(1)}, u32[]{:S(2)}, u32[]{:S(2)}) async-start(f32[4,2,3,256,128]{4,3,1,2,0:T(8,128)} %copy.83), calls=%async_computation.1 | async-start | bytes 6291456 | tf_op jit(solution)/shard_map/all_to_all | solution.py:52
  48.4 0.0 all-gather.2.cloned.1.call-start
  48.4 0.0 copy-done.7
  48.4 36.7 %all-to-all-done.1 = f32[4,2,3,256,128]{4,3,1,2,0:T(8,128)S(1)} async-done(((f32[4,2,3,256,128]{4,3,1,2,0:T(8,128)}), f32[4,2,3,256,128]{4,3,1,2,0:T(8,128)S(1)}, u32[]{:S(2)}, u32[]{:S(2)}) %all-to-all-start.1) | async-done | bytes 3145760 | tf_op jit(solution)/shard_map/all_to_all | solution.py:52
  85.1 1.0 reduce_sum.174
  86.1 0.0 copy-start.3
  86.1 1.3 fusion.50
  87.4 0.0 copy-done
  87.4 1.1 convolution_bitcast_fusion
  88.6 0.0 copy-start.5
  88.6 1.6 fusion.105
  90.2 0.2 fusion.27
  90.4 1.3 fusion.28
  91.7 0.0 copy-done.3
  91.7 1.1 fusion.62
  92.9 0.6 fusion.80
  93.5 0.8 pad_maximum_fusion
  94.3 0.0 all-gather.2.cloned.1.call-update
  94.3 0.2 reduce-scatter.2.cloned.1.call-start
  94.5 0.0 copy-done.5
  94.5 0.2 copy.91
  94.7 31.0 %all-gather.2.cloned.1.call-done = bf16[16,3,256,128]{3,2,0,1:T(8,128)(2,1)} async-done(((bf16[2,3,256,128]{3,2,0,1:T(8,128)(2,1)}), bf16[16,3,256,128]{3,2,0,1:T(8,128)(2,1)}) %all-gather.2.cloned.1.call-update) | async-done | bytes 3145744 | tf_op jit(solution)/shard_map/all_gather | solution.py:96
  125.7 8.2 %convert_bitcast_fusion = bf16[768,3,16,128]{0,3,1,2:T(8,128)(2,1)} fusion(bf16[256,768,1,1]{0,1,3,2:T(8,128)(2,1)S(1)} %bitcast.172, bf16[16,3,256,128]{3,2,0,1:T(8,128)(2,1)} %all-gather.2.cloned.1.call-done), kind=kOutput, calls=%fused_computation.8 | convolution fusion | flops 2420637696 | bytes 12976128 | tf_op jit(solution)/shard_map/td,hste->dshe/dot_general | solution.py:104
  133.9 13.2 %copy.95 = bf16[768,3,16,128]{3,2,1,0:T(8,128)(2,1)} copy(bf16[768,3,16,128]{0,3,1,2:T(8,128)(2,1)} %convert_bitcast_fusion) | data formatting | bytes 18874368 | tf_op jit(solution)/shard_map/convert_element_type | solution.py:106
  147.1 0.0 reduce-scatter.2.cloned.1.call-update
  147.2 0.0 copy-start.2
  147.2 0.0 copy-start.6
  147.2 0.0 copy-start.1
  147.2 7.3 %fusion.16 = bf16[256,768]{1,0:T(8,128)(2,1)S(1)} fusion(bf16[16,3,256,128]{3,2,0,1:T(8,128)(2,1)} %all-gather.2.cloned.1.call-done, bf16[3,768,2048]{2,1,0:T(8,128)(2,1)} %param.7), kind=kOutput, calls=%fused_computation.14 | convolution fusion | flops 2416115712 | bytes 12976128 | tf_op jit(solution)/shard_map/hste,sdhe->td/dot_general | solution.py:97
  154.5 1.6 collective-permute-start
  156.1 9.8 %collective-permute-done = bf16[256,768]{1,0:T(8,128)(2,1)S(1)} collective-permute-done((bf16[256,768]{1,0:T(8,128)(2,1)S(1)}, bf16[256,768]{1,0:T(8,128)(2,1)S(1)}, u32[]{:S(2)}, u32[]{:S(2)}) %collective-permute-start) | collective-permute-done | bytes 393248 | tf_op jit(solution)/shard_map/ppermute | solution.py:110
  165.9 0.0 copy-done.2
  165.9 0.0 copy-done.6
  165.9 0.4 fusion.45
  166.3 11.6 %all-reduce.1 = (f32[256]{0:T(256)S(1)}, f32[256]{0:T(256)S(1)}) all-reduce(f32[256]{0:T(256)S(1)} %get-tuple-element.13, f32[256]{0:T(256)S(1)} %get-tuple-element.14), channel_id=1, replica_groups=mesh['dph'=2,'dpz'=8,'mxx'=4,'mxc'=2,'my'=2] {'mxx','mxc'}, use_global_device_ids=true, to_apply=%region_23.0 | all-reduce | flops 512 | bytes 4096 | tf_op jit(solution)/shard_map/psum | solution.py:113
  177.9 45.9 %all-reduce = (f32[768]{0:T(1024)}, f32[2,2,128]{2,1,0:T(2,128)}) all-reduce(f32[768]{0:T(1024)S(1)} %get-tuple-element.12, f32[2,2,128]{2,1,0:T(2,128)S(1)} %pad_maximum_fusion.1), channel_id=1, replica_groups=mesh['dph'=2,'dpz'=8,'mxx'=4,'mxc'=2,'my'=2] {'dph','dpz'}, use_global_device_ids=true, to_apply=%region_25.0 | all-reduce | flops 1280 | bytes 10240 | tf_op jit(solution)/shard_map/psum | solution.py:120
  223.8 1.1 fusion.44
  224.9 29.6 %reduce-scatter.2.cloned.1.call-done = bf16[96,3,16,128]{3,2,1,0:T(8,128)(2,1)} async-done(((bf16[768,3,16,128]{3,2,1,0:T(8,128)(2,1)}), bf16[96,3,16,128]{3,2,1,0:T(8,128)(2,1)}) %reduce-scatter.2.cloned.1.call-update) | async-done | bytes 1179664 | tf_op jit(solution)/shard_map/reduce_scatter | solution.py:107
  254.5 1.1 dynamic-slice_bitcast_fusion
  255.6 3.1 %collective-permute-start.1 = (bf16[48,3,16,128]{3,2,1,0:T(8,128)(2,1)S(1)}, bf16[48,3,16,128]{3,2,1,0:T(8,128)(2,1)S(1)}, u32[]{:S(2)}, u32[]{:S(2)}) collective-permute-start(bf16[48,3,16,128]{3,2,1,0:T(8,128)(2,1)S(1)} %dynamic-slice_bitcast_fusion), channel_id=1, source_target_pairs={{0,128},{128,0},{1,129},{129,1},{2,130},{130,2},{3,131},{131,3},{4... | collective-permute-start | bytes 1769480 | tf_op jit(solution)/shard_map/ppermute | solution.py:126
  258.7 13.5 %collective-permute-done.1 = bf16[48,3,16,128]{3,2,1,0:T(8,128)(2,1)S(1)} collective-permute-done((bf16[48,3,16,128]{3,2,1,0:T(8,128)(2,1)S(1)}, bf16[48,3,16,128]{3,2,1,0:T(8,128)(2,1)S(1)}, u32[]{:S(2)}, u32[]{:S(2)}) %collective-permute-start.1) | collective-permute-done | bytes 589856 | tf_op jit(solution)/shard_map/ppermute | solution.py:126
  272.2 1.2 fusion.26
  273.4 0.1 copy.100
  273.6 1.1 convert_element_type.173
  274.6 0.0 copy-done.1
  (10 shorter events, 0.1 us)
Async XLA Ops:
  7.2 80.2 %copy-start = (bf16[256,256]{1,0:T(8,128)(2,1)S(1)}, bf16[256,256]{1,0:T(8,128)(2,1)}, u32[]{:S(2)}) copy-start(bf16[256,256]{1,0:T(8,128)(2,1)} %param.9) | copy-start | bytes 393220
  22.1 5.4 %copy-start.4 = (bf16[256,768]{1,0:T(8,128)(2,1)}, bf16[256,768]{1,0:T(8,128)(2,1)S(1)}, u32[]{:S(2)}) copy-start(bf16[256,768]{1,0:T(8,128)(2,1)S(1)} %fusion.39) | copy-start | bytes 1179652
  41.8 6.6 %copy-start.7 = (f32[2,2,128]{2,1,0:T(2,128)S(1)}, f32[2,2,128]{2,1,0:T(2,128)}, u32[]{:S(2)}) copy-start(f32[2,2,128]{2,1,0:T(2,128)} %param.8) | copy-start | bytes 6148
  43.6 41.4 %all-to-all-start.1 = ((f32[4,2,3,256,128]{4,3,1,2,0:T(8,128)}), f32[4,2,3,256,128]{4,3,1,2,0:T(8,128)S(1)}, u32[]{:S(2)}, u32[]{:S(2)}) async-start(f32[4,2,3,256,128]{4,3,1,2,0:T(8,128)} %copy.83), calls=%async_computation.1 | async-start | bytes 6291456 | tf_op jit(solution)/shard_map/all_to_all | solution.py:52
  48.4 77.3 %all-gather.2.cloned.1.call-start = ((), (), s32[]{:S(2)}) async-start(), calls=%async_computation.3 | async-start | bytes 3538944 | tf_op jit(solution)/shard_map/all_gather | solution.py:96
  86.1 5.7 %copy-start.3 = (bf16[2,3,256,128]{3,2,0,1:T(8,128)(2,1)S(1)}, bf16[2,3,256,128]{3,2,0,1:T(8,128)(2,1)}, u32[]{:S(2)}) copy-start(bf16[2,3,256,128]{3,2,0,1:T(8,128)(2,1)} %reduce_sum.174) | copy-start | bytes 1179652
  88.6 6.0 %copy-start.5 = (bf16[256,768]{1,0:T(8,128)(2,1)S(1)}, bf16[256,768]{1,0:T(8,128)(2,1)}, u32[]{:S(2)}) copy-start(bf16[256,768]{1,0:T(8,128)(2,1)} %copy-done.4) | copy-start | bytes 1179652
  94.3 160.2 %reduce-scatter.2.cloned.1.call-start = ((), (), s32[]{:S(2)}) async-start(), calls=%async_computation.4 | async-start | bytes 10616832 | tf_op jit(solution)/shard_map/reduce_scatter | solution.py:107
  147.2 18.7 %copy-start.2 = (bf16[256,768]{1,0:T(8,128)(2,1)S(1)}, bf16[256,768]{1,0:T(8,128)(2,1)}, u32[]{:S(2)}) copy-start(bf16[256,768]{1,0:T(8,128)(2,1)} %param.5) | copy-start | bytes 1179652
  147.2 18.7 %copy-start.6 = (f32[768]{0:T(1024)S(1)}, f32[768]{0:T(1024)}, u32[]{:S(2)}) copy-start(f32[768]{0:T(1024)} %param.6) | copy-start | bytes 9220
  147.2 127.4 %copy-start.1 = (bf16[256,256]{1,0:T(8,128)(2,1)S(1)}, bf16[256,256]{1,0:T(8,128)(2,1)}, u32[]{:S(2)}) copy-start(bf16[256,256]{1,0:T(8,128)(2,1)} %param.9) | copy-start | bytes 393220
  154.5 11.3 %collective-permute-start = (bf16[256,768]{1,0:T(8,128)(2,1)S(1)}, bf16[256,768]{1,0:T(8,128)(2,1)S(1)}, u32[]{:S(2)}, u32[]{:S(2)}) collective-permute-start(bf16[256,768]{1,0:T(8,128)(2,1)S(1)} %fusion.16), channel_id=1, source_target_pairs={{0,1},{1,0},{2,3},{3,2},{4,5},{5,4},{6,7},{7,6},{8,9},{9,8},{10,11... | collective-permute-start | bytes 1179656 | tf_op jit(solution)/shard_map/ppermute | solution.py:110
  255.6 16.6 %collective-permute-start.1 = (bf16[48,3,16,128]{3,2,1,0:T(8,128)(2,1)S(1)}, bf16[48,3,16,128]{3,2,1,0:T(8,128)(2,1)S(1)}, u32[]{:S(2)}, u32[]{:S(2)}) collective-permute-start(bf16[48,3,16,128]{3,2,1,0:T(8,128)(2,1)S(1)} %dynamic-slice_bitcast_fusion), channel_id=1, source_target_pairs={{0,128},{128,0},{1,129},{129,1},{2,130},{130,2},{3,131},{131,3},{4... | collective-permute-start | bytes 1769480 | tf_op jit(solution)/shard_map/ppermute | solution.py:126
Sparse Core Ops, SparseCore 0:
  94.4 31.2 all-gather.1
  147.3 107.1 reduce-scatter.1

commit v12 on v11

--- a/solution.py
+++ b/solution.py
@@ -48,7 +48,9 @@
     n_c = lax.axis_size("mxc")
     partial = jnp.einsum("td,sdhe->hste", scaled, weights, preferred_element_type=jnp.float32)
     partial = partial.reshape(n_x, n_c, local_heads, 3, token_rows, head_size).transpose(1, 0, 2, 3, 4, 5)
-    on_chip = jnp.sum(lax.all_to_all(partial, "mxc", split_axis=0, concat_axis=0), axis=0)
+    core_index = lax.axis_index("mxc")
+    from_core = lax.ppermute(partial[1 - core_index], "mxc", [(0, 1), (1, 0)])
+    on_chip = partial[core_index] + from_core
     projected = jnp.sum(lax.all_to_all(on_chip, "mxx", split_axis=0, concat_axis=0), axis=0)
     projected = projected.astype(jnp.bfloat16)
     images = token_rows // PATCH

time: 282 us -> 281 us (level)
  blocking collectives: 79.9 us -> 69.9 us
  waiting for transfers between devices: 121 us -> 126 us
    all_to_all x1 -> x0, blocking collectives: 9.99 us -> none  [body(): lax.all_to_all(partial, 'mxc', split_axis=0, concat_axis=0)]
    ppermute x0 -> x1, waiting for transfers between devices: none -> 5.65 us  [body(): from_core = lax.ppermute(partial[1 - core_index], 'mxc', [(0, 1), (1, 0)])]
    dot_general x1, matrix products: 5.4 us -> 9.01 us  [body(): jnp.einsum('td,sdhe->hste', scaled, weights, preferred_element_type=jnp.f...]
    reduce_sum x1 -> x0, other arithmetic: 3.54 us -> none  [body(): jnp.sum(lax.all_to_all(partial, 'mxc', split_axis=0, concat_axis=0), axis=0)]
    another operation x0 -> x2, local copies, waits for them, and re-layouts: none -> 3.46 us
  transfers between devices with their start and end apart: 5 -> 6, of which waited for: 5 -> 6; matrix products, arithmetic and copies ran while one was open for 3% -> 3% of each run, Pallas kernels for 0% -> 0%
where the time goes in v12:
time: 281 us; the launch traced here: 280 us
  waiting for transfers between devices  126 us (45%)
  blocking collectives  69.9 us (25%)
  matrix products  28.9 us (10%)
  local copies, waits for them, and re-layouts  19.9 us (7%)
  between operations  14.2 us (5%)
  other arithmetic  11.1 us (4%)
  starting transfers between devices  9.85 us (4%)
    psum x1, blocking collectives, body(): lax.psum((head_gain_part, feature_part), ('dph', 'dpz'))  45.9 us
    all_to_all x1, waiting for transfers between devices, body(): lax.all_to_all(on_chip, 'mxx', split_axis=0, concat_axis=0)  36.7 us
    all_gather x1, waiting for transfers between devices, body(): gathered = lax.all_gather(stacked, MX, axis=0, tiled=True)  31 us
    reduce_scatter x1, waiting for transfers between devices, body(): w_half = lax.psum_scatter(w_part, 'dpz', scatter_dimension=0, tiled=True)  29.6 us
    ppermute x1, waiting for transfers between devices, body(): swapped = lax.ppermute(halves[1 - hi_index], 'dph', [(0, 1), (1, 0)])  13.5 us
    convert_element_type x1, local copies, waits for them, and re-layouts, body(): w_part = jnp.einsum('td,hste->dshe', feature_part, gathered, preferred_el...  13.2 us
    psum x1, blocking collectives, body(): lax.psum((jnp.sum(d_hat, axis=1), jnp.sum(d_hat * normed, axis=1)), MX)  11.6 us
    psum x1, blocking collectives, body(): totals = lax.psum(totals, 'mxx')  9.94 us
  transfers between devices with their start and end apart: 6, of which 6 were waited for; matrix products, arithmetic and copies ran while one was open for 3% of the time, Pallas kernels for 0%

profile of v12, /device:TPU:2, one launch (start us, length us, event | category | flops | bytes accessed | tf_op | source)
XLA Modules:
  0.0 280.1 jit_solution(17559266299705982338)
XLA Ops:
  7.2 0.0 copy-start
  7.2 1.3 convert_reduce_fusion
  8.4 2.5 all-reduce.3
  10.9 9.9 %all-reduce.2 = (f32[256]{0:T(256)S(1)}, f32[256]{0:T(256)S(1)}) all-reduce(f32[256]{0:T(256)S(1)} %get-tuple-element.35, f32[256]{0:T(256)S(1)} %get-tuple-element.36), channel_id=1, replica_groups=mesh['dph'=2,'dpz'=8,'mxx'=4,'mxc'=2,'my'=2] {'mxx'}, use_global_device_ids=true, to_apply=%region_5.0 | all-reduce | flops 512 | bytes 4096 | tf_op jit(solution)/shard_map/psum | solution.py:37
  20.9 1.2 fusion.39
  22.1 0.0 copy-start.3
  22.1 0.7 copy-done.3
  22.8 9.0 %fusion.5 = f32[256,3,16,128]{3,0,2,1:T(8,128)} fusion(bf16[256,768]{1,0:T(8,128)(2,1)S(1)} %fusion.39, bf16[3,768,2048]{2,1,0:T(8,128)(2,1)} %param.7), kind=kOutput, calls=%fused_computation.5 | convolution fusion | flops 2415919104 | bytes 16121856 | tf_op jit(solution)/shard_map/td,sdhe->hste/dot_general | solution.py:49
  31.9 3.3 %constant_dynamic-slice_fusion.1 = (f32[4,1,2,3,256,128]{5,4,2,1,0,3:T(8,128)S(1)}, f32[4,1,2,3,256,128]{5,4,2,1,0,3:T(8,128)S(1)}) fusion(f32[4,2,2,3,256,128]{5,4,2,1,0,3:T(8,128)} %bitcast.166, s32[]{:T(128)S(6)} %select_n.12, s32[]{:T(128)S(6)} %select_n.13), kind=kLoop, calls=%fused_computation.115 | loop fusion | bytes 12582920 | tf_op jit(solution)/shard_map/dynamic-slice
  35.1 0.2 copy.125
  35.3 0.1 collective-permute-start
  35.4 5.6 %collective-permute-done = f32[4,2,3,256,128]{4,3,1,2,0:T(8,128)S(1)} collective-permute-done((f32[4,2,3,256,128]{4,3,1,2,0:T(8,128)S(1)}, f32[4,2,3,256,128]{4,3,1,2,0:T(8,128)S(1)}, u32[]{:S(2)}, u32[]{:S(2)}) %collective-permute-start) | collective-permute-done | bytes 3145760 | tf_op jit(solution)/shard_map/ppermute | solution.py:52
  41.1 2.1 bitcast_add_fusion
  43.1 0.0 copy-start.6
  43.1 4.9 %all-to-all-start = ((f32[4,2,3,256,128]{4,3,1,2,0:T(8,128)}), f32[4,2,3,256,128]{4,3,1,2,0:T(8,128)S(1)}, u32[]{:S(2)}, u32[]{:S(2)}) async-start(f32[4,2,3,256,128]{4,3,1,2,0:T(8,128)} %bitcast_add_fusion), calls=%async_computation | async-start | bytes 6291456 | tf_op jit(solution)/shard_map/all_to_all | solution.py:54
  48.0 0.0 all-gather.2.cloned.1.call-start
  48.0 0.0 copy-done.6
  48.0 36.7 %all-to-all-done = f32[4,2,3,256,128]{4,3,1,2,0:T(8,128)S(1)} async-done(((f32[4,2,3,256,128]{4,3,1,2,0:T(8,128)}), f32[4,2,3,256,128]{4,3,1,2,0:T(8,128)S(1)}, u32[]{:S(2)}, u32[]{:S(2)}) %all-to-all-start) | async-done | bytes 3145760 | tf_op jit(solution)/shard_map/all_to_all | solution.py:54
  84.7 1.0 reduce_sum.164
  85.7 0.0 copy-start.2
  85.7 1.3 fusion.50
  87.0 0.0 copy-done
  87.0 1.1 convolution_bitcast_fusion
  88.2 1.6 fusion.105
  89.7 0.2 fusion.27
  90.0 0.0 copy-done.2
  90.0 0.4 fusion.28
  90.4 0.0 copy-start.4
  90.4 1.1 fusion.62
  91.5 0.6 fusion.80
  92.1 0.8 pad_maximum_fusion
  92.9 0.0 all-gather.2.cloned.1.call-update
  93.0 0.2 reduce-scatter.2.cloned.1.call-start
  93.2 0.0 copy-done.4
  93.2 0.2 copy.70
  93.4 31.0 %all-gather.2.cloned.1.call-done = bf16[16,3,256,128]{3,2,0,1:T(8,128)(2,1)} async-done(((bf16[2,3,256,128]{3,2,0,1:T(8,128)(2,1)}), bf16[16,3,256,128]{3,2,0,1:T(8,128)(2,1)}) %all-gather.2.cloned.1.call-update) | async-done | bytes 3145744 | tf_op jit(solution)/shard_map/all_gather | solution.py:98
  124.4 8.2 %convert_bitcast_fusion = bf16[768,3,16,128]{0,3,1,2:T(8,128)(2,1)} fusion(bf16[256,768,1,1]{0,1,3,2:T(8,128)(2,1)S(1)} %bitcast.174, bf16[16,3,256,128]{3,2,0,1:T(8,128)(2,1)} %all-gather.2.cloned.1.call-done), kind=kOutput, calls=%fused_computation.8 | convolution fusion | flops 2420637696 | bytes 12976128 | tf_op jit(solution)/shard_map/td,hste->dshe/dot_general | solution.py:106
  132.6 13.2 %copy.74 = bf16[768,3,16,128]{3,2,1,0:T(8,128)(2,1)} copy(bf16[768,3,16,128]{0,3,1,2:T(8,128)(2,1)} %convert_bitcast_fusion) | data formatting | bytes 18874368 | tf_op jit(solution)/shard_map/convert_element_type | solution.py:108
  145.8 0.0 reduce-scatter.2.cloned.1.call-update
  145.8 0.0 copy-start.1
  145.8 0.0 copy-start.5
  145.9 7.3 %fusion.16 = bf16[256,768]{1,0:T(8,128)(2,1)S(1)} fusion(bf16[16,3,256,128]{3,2,0,1:T(8,128)(2,1)} %all-gather.2.cloned.1.call-done, bf16[3,768,2048]{2,1,0:T(8,128)(2,1)} %param.7), kind=kOutput, calls=%fused_computation.15 | convolution fusion | flops 2416115712 | bytes 12976128 | tf_op jit(solution)/shard_map/hste,sdhe->td/dot_general | solution.py:99
  153.2 1.6 collective-permute-start.1
  154.7 9.8 %collective-permute-done.1 = bf16[256,768]{1,0:T(8,128)(2,1)S(1)} collective-permute-done((bf16[256,768]{1,0:T(8,128)(2,1)S(1)}, bf16[256,768]{1,0:T(8,128)(2,1)S(1)}, u32[]{:S(2)}, u32[]{:S(2)}) %collective-permute-start.1) | collective-permute-done | bytes 393248 | tf_op jit(solution)/shard_map/ppermute | solution.py:112
  164.5 0.0 copy-done.1
  164.5 0.0 copy-done.5
  164.5 0.4 fusion.45
  165.0 11.6 %all-reduce.1 = (f32[256]{0:T(256)S(1)}, f32[256]{0:T(256)S(1)}) all-reduce(f32[256]{0:T(256)S(1)} %get-tuple-element.13, f32[256]{0:T(256)S(1)} %get-tuple-element.14), channel_id=1, replica_groups=mesh['dph'=2,'dpz'=8,'mxx'=4,'mxc'=2,'my'=2] {'mxx','mxc'}, use_global_device_ids=true, to_apply=%region_22.0 | all-reduce | flops 512 | bytes 4096 | tf_op jit(solution)/shard_map/psum | solution.py:115
  176.6 45.9 %all-reduce = (f32[768]{0:T(1024)}, f32[2,2,128]{2,1,0:T(2,128)}) all-reduce(f32[768]{0:T(1024)S(1)} %get-tuple-element.12, f32[2,2,128]{2,1,0:T(2,128)S(1)} %pad_maximum_fusion.1), channel_id=1, replica_groups=mesh['dph'=2,'dpz'=8,'mxx'=4,'mxc'=2,'my'=2] {'dph','dpz'}, use_global_device_ids=true, to_apply=%region_24.0 | all-reduce | flops 1280 | bytes 10240 | tf_op jit(solution)/shard_map/psum | solution.py:122
  222.5 1.1 fusion.44
  223.6 29.6 %reduce-scatter.2.cloned.1.call-done = bf16[96,3,16,128]{3,2,1,0:T(8,128)(2,1)} async-done(((bf16[768,3,16,128]{3,2,1,0:T(8,128)(2,1)}), bf16[96,3,16,128]{3,2,1,0:T(8,128)(2,1)}) %reduce-scatter.2.cloned.1.call-update) | async-done | bytes 1179664 | tf_op jit(solution)/shard_map/reduce_scatter | solution.py:109
  253.2 1.1 dynamic-slice_bitcast_fusion
  254.3 3.1 %collective-permute-start.2 = (bf16[48,3,16,128]{3,2,1,0:T(8,128)(2,1)S(1)}, bf16[48,3,16,128]{3,2,1,0:T(8,128)(2,1)S(1)}, u32[]{:S(2)}, u32[]{:S(2)}) collective-permute-start(bf16[48,3,16,128]{3,2,1,0:T(8,128)(2,1)S(1)} %dynamic-slice_bitcast_fusion), channel_id=1, source_target_pairs={{0,128},{128,0},{1,129},{129,1},{2,130},{130,2},{3,131},{131,3},{4... | collective-permute-start | bytes 1769480 | tf_op jit(solution)/shard_map/ppermute | solution.py:128
  257.4 13.5 %collective-permute-done.2 = bf16[48,3,16,128]{3,2,1,0:T(8,128)(2,1)S(1)} collective-permute-done((bf16[48,3,16,128]{3,2,1,0:T(8,128)(2,1)S(1)}, bf16[48,3,16,128]{3,2,1,0:T(8,128)(2,1)S(1)}, u32[]{:S(2)}, u32[]{:S(2)}) %collective-permute-start.2) | collective-permute-done | bytes 589856 | tf_op jit(solution)/shard_map/ppermute | solution.py:128
  270.9 1.2 fusion.26
  272.1 0.1 copy.79
  272.2 1.1 convert_element_type.173
  (10 shorter events, 0.1 us)
Async XLA Ops:
  7.2 79.9 %copy-start = (bf16[256,256]{1,0:T(8,128)(2,1)S(1)}, bf16[256,256]{1,0:T(8,128)(2,1)}, u32[]{:S(2)}) copy-start(bf16[256,256]{1,0:T(8,128)(2,1)} %param.9) | copy-start | bytes 393220
  22.1 0.7 copy-start.3
  35.3 5.7 %collective-permute-start = (f32[4,2,3,256,128]{4,3,1,2,0:T(8,128)S(1)}, f32[4,2,3,256,128]{4,3,1,2,0:T(8,128)S(1)}, u32[]{:S(2)}, u32[]{:S(2)}) collective-permute-start(f32[4,2,3,256,128]{4,3,1,2,0:T(8,128)S(1)} %bitcast.167), channel_id=1, source_target_pairs={{0,2},{2,0},{1,3},{3,1},{4,6},{6,4},{5,7},{7,5},{8,10},{10,8},{9,1... | collective-permute-start | bytes 9437192 | tf_op jit(solution)/shard_map/ppermute | solution.py:52
  43.1 4.9 %copy-start.6 = (f32[2,2,128]{2,1,0:T(2,128)S(1)}, f32[2,2,128]{2,1,0:T(2,128)}, u32[]{:S(2)}) copy-start(f32[2,2,128]{2,1,0:T(2,128)} %param.8) | copy-start | bytes 6148
  43.1 41.6 %all-to-all-start = ((f32[4,2,3,256,128]{4,3,1,2,0:T(8,128)}), f32[4,2,3,256,128]{4,3,1,2,0:T(8,128)S(1)}, u32[]{:S(2)}, u32[]{:S(2)}) async-start(f32[4,2,3,256,128]{4,3,1,2,0:T(8,128)} %bitcast_add_fusion), calls=%async_computation | async-start | bytes 6291456 | tf_op jit(solution)/shard_map/all_to_all | solution.py:54
  48.0 76.4 %all-gather.2.cloned.1.call-start = ((), (), s32[]{:S(2)}) async-start(), calls=%async_computation.2 | async-start | bytes 3538944 | tf_op jit(solution)/shard_map/all_gather | solution.py:98
  85.7 4.2 %copy-start.2 = (bf16[2,3,256,128]{3,2,0,1:T(8,128)(2,1)S(1)}, bf16[2,3,256,128]{3,2,0,1:T(8,128)(2,1)}, u32[]{:S(2)}) copy-start(bf16[2,3,256,128]{3,2,0,1:T(8,128)(2,1)} %reduce_sum.164) | copy-start | bytes 1179652
  90.4 2.8 copy-start.4
  93.0 160.2 %reduce-scatter.2.cloned.1.call-start = ((), (), s32[]{:S(2)}) async-start(), calls=%async_computation.3 | async-start | bytes 10616832 | tf_op jit(solution)/shard_map/reduce_scatter | solution.py:109
  145.8 18.7 %copy-start.1 = (bf16[256,768]{1,0:T(8,128)(2,1)S(1)}, bf16[256,768]{1,0:T(8,128)(2,1)}, u32[]{:S(2)}) copy-start(bf16[256,768]{1,0:T(8,128)(2,1)} %param.5) | copy-start | bytes 1179652
  145.8 18.7 %copy-start.5 = (f32[768]{0:T(1024)S(1)}, f32[768]{0:T(1024)}, u32[]{:S(2)}) copy-start(f32[768]{0:T(1024)} %param.6) | copy-start | bytes 9220
  153.2 11.3 %collective-permute-start.1 = (bf16[256,768]{1,0:T(8,128)(2,1)S(1)}, bf16[256,768]{1,0:T(8,128)(2,1)S(1)}, u32[]{:S(2)}, u32[]{:S(2)}) collective-permute-start(bf16[256,768]{1,0:T(8,128)(2,1)S(1)} %fusion.16), channel_id=1, source_target_pairs={{0,1},{1,0},{2,3},{3,2},{4,5},{5,4},{6,7},{7,6},{8,9},{9,8},{10,11... | collective-permute-start | bytes 1179656 | tf_op jit(solution)/shard_map/ppermute | solution.py:112
  254.3 16.6 %collective-permute-start.2 = (bf16[48,3,16,128]{3,2,1,0:T(8,128)(2,1)S(1)}, bf16[48,3,16,128]{3,2,1,0:T(8,128)(2,1)S(1)}, u32[]{:S(2)}, u32[]{:S(2)}) collective-permute-start(bf16[48,3,16,128]{3,2,1,0:T(8,128)(2,1)S(1)} %dynamic-slice_bitcast_fusion), channel_id=1, source_target_pairs={{0,128},{128,0},{1,129},{129,1},{2,130},{130,2},{3,131},{131,3},{4... | collective-permute-start | bytes 1769480 | tf_op jit(solution)/shard_map/ppermute | solution.py:128
Sparse Core Ops, SparseCore 0:
  93.1 31.2 all-gather.1
  146.0 107.1 reduce-scatter.1
